TPU v7x, 512 devices: a whole 4x4x16 slice. The times are simulated.
512 devices in a mesh: gx: 4 (over z_hi, core), gy: 8 (over z_lo), gz: 16 (over x, y).
Axes of the slice: x: 4, y: 4, z: 16 (z_hi: 2, z_lo: 8; z = z_hi * 8 + z_lo), core: 2. Of those that a mesh axis runs over, the one named last changes fastest.
Arguments:
- right_side: float32 [32, 128, 2048], P('gx', 'gy', 'gz'), may hold values from -8 to 8
- coefficient: float32 [32, 128, 2048], P('gx', 'gy', 'gz'), may hold values from 0.05 to 2
Outputs:
- correction: float32 [32, 128, 2048], P('gx', 'gy', 'gz')
All inputs are finite; a program needn't handle non-finite values.
Results may differ from a plain program's by a relative error of at most 0.00002.
Values sent between devices are 32-bit elements; how exact they have to be, the bound alone decides.
No kernel may reach another device: no remote copies, remote signals or barrier semaphores. Data moves between devices by JAX's collectives and lax.ppermute only.
A program may use at most 64 MiB of HBM per device.

v0:
```python
import jax
import jax.numpy as jnp
from jax import lax
from jax.sharding import PartitionSpec as P

SWEEPS = 4


RELAX_WEIGHT = 0.8


def sent_together(arrays, axis, dim, along):
    ends, at = ([], 0)
    for a in arrays[:-1]:
        at += a.shape[along]
        ends.append(at)
    both = jnp.concatenate(arrays, axis=along)
    return tuple(jnp.split(lax.all_gather(both, axis, axis=dim, tiled=True), ends, axis=along))


def from_everyone(shard, axis):
    copies = jnp.broadcast_to(shard, (lax.axis_size(axis), *shard.shape))
    return lax.all_to_all(copies, axis, split_axis=0, concat_axis=0, tiled=True)


def in_order(blocks, dim):
    blocks = jnp.moveaxis(blocks, 0, dim)
    shape = blocks.shape
    return blocks.reshape(*shape[:dim], shape[dim] * shape[dim + 1], *shape[dim + 2 :])


def gathered_copies(shard, axis, dim):
    blocks = from_everyone(shard, axis)
    return in_order(blocks, dim)


def padded_2(shard, sides, width):
    for axis, dim in sides:
        peers, length = (lax.axis_size(axis), shard.shape[dim])
        up = [(i, (i + 1) % peers) for i in range(peers - 1)]
        down = [(j, i) for i, j in up]
        last = lax.slice_in_dim(shard, length - width, length, axis=dim)
        leading = lax.slice_in_dim(shard, 0, width, axis=dim)
        before = lax.ppermute(last, axis, up)
        after = lax.ppermute(leading, axis, down)
        shard = jnp.concatenate([before, shard, after], axis=dim)
    return shard


def restrict(values):
    return values.reshape(
        values.shape[0] // 2, 2, values.shape[1] // 2, 2, values.shape[2] // 2, 2
    ).mean(axis=(1, 3, 5))


def prolong(values):
    return jnp.repeat(jnp.repeat(jnp.repeat(values, 2, axis=0), 2, axis=1), 2, axis=2)


def neighbours(padded):
    beside_all = padded[2:, 1:-1, 1:-1] + padded[:-2, 1:-1, 1:-1]
    beside_all = beside_all + padded[1:-1, 2:, 1:-1] + padded[1:-1, :-2, 1:-1]
    return beside_all + padded[1:-1, 1:-1, 2:] + padded[1:-1, 1:-1, :-2]


def plane_term(residual, coefficient):
    return jnp.mean(residual, axis=(0, 1)) / jnp.mean(coefficient + 0.0625, axis=(0, 1))


def sweep_deep(extended, spacing_scale, inside_mask, depth_dims):
    residual = extended[0]
    diagonal = 6.0 * spacing_scale + extended[1]
    iterate = RELAX_WEIGHT * residual / diagonal * inside_mask
    for repeat in range(SWEEPS - 1):
        beside_all = neighbours(jnp.pad(iterate, 1))
        iterate = (
            iterate
            + RELAX_WEIGHT
            * (residual - (diagonal * iterate - spacing_scale * beside_all))
            / diagonal
        ) * inside_mask
    cropped = iterate
    for dimension in depth_dims:
        cropped = lax.slice_in_dim(
            cropped, SWEEPS - 1, cropped.shape[dimension] - (SWEEPS - 1), axis=dimension
        )
    return cropped


def inside_band(first_cell, local_length, whole_length):
    rim_depth = SWEEPS - 1
    position = first_cell + jnp.arange(-rim_depth, local_length + rim_depth, dtype=jnp.int32)
    return jnp.where((position >= 0) & (position < whole_length), 1.0, 0.0).astype(jnp.float32)


def per_device(right_side, coefficient):
    local_x, local_y, local_z = right_side.shape
    count_x = lax.axis_size("gx")
    count_y = lax.axis_size("gy")
    count_z = lax.axis_size("gz")
    spot_x = lax.axis_index("gx")
    spot_y = lax.axis_index("gy")
    spot_z = lax.axis_index("gz")
    residual_one = restrict(right_side)
    coeff_one = restrict(coefficient)
    residual_mid, coeff_mid = sent_together((residual_one, coeff_one), "gx", 0, 1)
    stacked = jnp.stack([restrict(residual_one), restrict(coeff_one)])[None]
    pieces = gathered_copies(stacked, ("gx", "gy"), 0)
    part_x, part_y, part_z = (stacked.shape[2], stacked.shape[3], stacked.shape[4])
    arranged = pieces.reshape(count_x, count_y, 2, part_x, part_y, part_z)
    arranged = arranged.transpose(2, 0, 3, 1, 4, 5).reshape(
        2, count_x * part_x, count_y * part_y, part_z
    )
    residual_two = arranged[0]
    coeff_two = arranged[1]
    rim_depth = SWEEPS - 1
    coarse_ext = padded_2(jnp.stack([residual_two, coeff_two]), (("gz", 3),), rim_depth)
    coarse_z = residual_two.shape[2]
    coarse_mask = inside_band(spot_z * coarse_z, coarse_z, coarse_z * count_z)[None, None, :]
    coarse_part = sweep_deep(coarse_ext, 0.0625, coarse_mask, (2,))
    middle_ext = padded_2(jnp.stack([residual_mid, coeff_mid]), (("gy", 2), ("gz", 3)), rim_depth)
    middle_y = residual_mid.shape[1]
    middle_z = residual_mid.shape[2]
    middle_mask = (
        inside_band(spot_y * middle_y, middle_y, middle_y * count_y)[None, :, None]
        * inside_band(spot_z * middle_z, middle_z, middle_z * count_z)[None, None, :]
    )
    middle_part = sweep_deep(middle_ext, 0.25, middle_mask, (1, 2))
    fine_ext = padded_2(
        jnp.stack([right_side, coefficient]), (("gx", 1), ("gy", 2), ("gz", 3)), rim_depth
    )
    fine_mask = (
        inside_band(spot_x * local_x, local_x, local_x * count_x)[:, None, None]
        * inside_band(spot_y * local_y, local_y, local_y * count_y)[None, :, None]
        * inside_band(spot_z * local_z, local_z, local_z * count_z)[None, None, :]
    )
    fine_part = sweep_deep(fine_ext, 1.0, fine_mask, (0, 1, 2))
    coarse_part = coarse_part + plane_term(residual_two, coeff_two)[None, None, :]
    coarse_own = lax.dynamic_slice_in_dim(
        coarse_part, spot_y * (local_y // 4), local_y // 4, axis=1
    )
    middle_total = middle_part + prolong(coarse_own)
    middle_own = lax.dynamic_slice_in_dim(
        middle_total, spot_x * (local_x // 2), local_x // 2, axis=0
    )
    return fine_part + prolong(middle_own)


def solution(mesh):
    in_specs = (P("gx", "gy", "gz"), P("gx", "gy", "gz"))
    out_specs = P("gx", "gy", "gz")
    return jax.shard_map(
        per_device, mesh=mesh, in_specs=in_specs, out_specs=out_specs, check_vma=False
    )
```

profile of v0, /device:TPU:25, one launch (start us, length us, event | category | flops | bytes accessed | tf_op | source)
XLA Modules:
  0.0 133.9 jit_solution(8664250107185127574)
XLA Ops:
  0.0 6.3 %reshape.187 = f32[4,2,8,2,64,2]{5,4,3,2,1,0:T(8,128)} reshape(f32[8,16,128]{2,1,0:T(8,128)} %param.3) | data formatting | bytes 131072 | tf_op jit(solution)/shard_map/reshape | solution.py:51
  6.3 2.6 %reduce_sum.55 = f32[4,8,64]{2,1,0:T(8,128)S(1)} reduce(f32[4,2,8,2,64,2]{5,4,3,2,1,0:T(8,128)} %reshape.187, f32[]{:T(128)} %constant.34.clone.1), dimensions={1,3,5}, to_apply=%region_1.0 | reduce | flops 14336 | bytes 73732 | tf_op jit(solution)/shard_map/reduce_sum | solution.py:53
  8.9 5.5 %reshape.186 = f32[4,2,8,2,64,2]{5,4,3,2,1,0:T(8,128)} reshape(f32[8,16,128]{2,1,0:T(8,128)S(1)} %copy-done.1) | data formatting | bytes 131072 | tf_op jit(solution)/shard_map/reshape | solution.py:51
  14.4 2.5 %reduce_sum.54 = f32[4,8,64]{2,1,0:T(8,128)S(1)} reduce(f32[4,2,8,2,64,2]{5,4,3,2,1,0:T(8,128)} %reshape.186, f32[]{:T(128)} %constant.34.clone.1), dimensions={1,3,5}, to_apply=%region_0.0 | reduce | flops 14336 | bytes 73732 | tf_op jit(solution)/shard_map/reduce_sum | solution.py:53
  17.0 18.0 %all_gather.3 = f32[16,16,64]{2,1,0:T(8,128)S(1)} all-gather(f32[4,16,64]{2,1,0:T(8,128)S(1)} %pad_maximum_fusion.8), channel_id=1, replica_groups=mesh['gx'=4,'gy'=8,'gz'=16] {'gx'}, dimensions={0}, use_global_device_ids=true | all-gather | bytes 81920 | tf_op jit(solution)/shard_map/all_gather | solution.py:18
  35.0 2.6 %collective-permute-start.6 = (f32[2,16,3,64]{3,2,1,0:T(4,128)S(1)}, f32[2,16,3,64]{3,2,1,0:T(4,128)S(1)}, u32[]{:S(2)}, u32[]{:S(2)}) collective-permute-start(f32[2,16,3,64]{3,2,1,0:T(4,128)S(1)} %get-tuple-element.30), channel_id=1, source_target_pairs={{0,16},{16,32},{32,48},{48,64},{64,80},{80,96},{96,112},{1,17},{17... | collective-permute-start | bytes 73736 | tf_op jit(solution)/shard_map/ppermute | solution.py:44
  41.1 13.9 %all-to-all-start = ((f32[32,1,512]{2,1,0:T(1,128)}), f32[32,1,512]{2,1,0:T(1,128)S(1)}, u32[]{:S(2)}, u32[]{:S(2)}) async-start(f32[32,1,512]{2,1,0:T(1,128)} %reshape.194), calls=%async_computation | async-start | bytes 131072 | tf_op jit(solution)/shard_map/all_to_all | solution.py:23
  55.1 12.3 %collective-permute-start = (f32[2,3,16,128]{3,2,1,0:T(8,128)S(1)}, f32[2,3,16,128]{3,2,1,0:T(8,128)S(1)}, u32[]{:S(2)}, u32[]{:S(2)}) collective-permute-start(f32[2,3,16,128]{3,2,1,0:T(8,128)S(1)} %get-tuple-element.33), channel_id=1, source_target_pairs={{0,128},{128,256},{256,384},{1,129},{129,257},{257,385},{2,130},{1... | collective-permute-start | bytes 147464 | tf_op jit(solution)/shard_map/ppermute | solution.py:44
  67.3 1.9 %collective-permute-start.1 = (f32[2,3,16,128]{3,2,1,0:T(8,128)S(1)}, f32[2,3,16,128]{3,2,1,0:T(8,128)S(1)}, u32[]{:S(2)}, u32[]{:S(2)}) collective-permute-start(f32[2,3,16,128]{3,2,1,0:T(8,128)S(1)} %get-tuple-element.34), channel_id=1, source_target_pairs={{128,0},{256,128},{384,256},{129,1},{257,129},{385,257},{130,2},{2... | collective-permute-start | bytes 147464 | tf_op jit(solution)/shard_map/ppermute | solution.py:45
  69.7 2.8 %collective-permute-start.8 = (f32[2,16,14,3]{3,1,2,0:T(8,128)S(1)}, f32[2,16,14,3]{3,1,2,0:T(8,128)S(1)}, u32[]{:S(2)}, u32[]{:S(2)}) collective-permute-start(f32[2,16,14,3]{3,1,2,0:T(8,128)S(1)} %get-tuple-element.25), channel_id=1, source_target_pairs={{0,1},{1,2},{2,3},{3,4},{4,5},{5,6},{6,7},{7,8},{8,9},{9,10},{10,1... | collective-permute-start | bytes 16136 | tf_op jit(solution)/shard_map/ppermute | solution.py:44
  72.5 2.5 %collective-permute-start.9 = (f32[2,16,14,3]{3,1,2,0:T(8,128)S(1)}, f32[2,16,14,3]{3,1,2,0:T(8,128)S(1)}, u32[]{:S(2)}, u32[]{:S(2)}) collective-permute-start(f32[2,16,14,3]{3,1,2,0:T(8,128)S(1)} %get-tuple-element.26), channel_id=1, source_target_pairs={{1,0},{2,1},{3,2},{4,3},{5,4},{6,5},{7,6},{8,7},{9,8},{10,9},{11,1... | collective-permute-start | bytes 16136 | tf_op jit(solution)/shard_map/ppermute | solution.py:45
  76.5 4.9 %collective-permute-done.9 = f32[2,16,14,3]{3,1,2,0:T(8,128)S(1)} collective-permute-done((f32[2,16,14,3]{3,1,2,0:T(8,128)S(1)}, f32[2,16,14,3]{3,1,2,0:T(8,128)S(1)}, u32[]{:S(2)}, u32[]{:S(2)}) %collective-permute-start.9) | collective-permute-done | bytes 5408 | tf_op jit(solution)/shard_map/ppermute | solution.py:45
  82.0 3.4 %collective-permute-start.2 = (f32[2,14,3,128]{3,0,2,1:T(2,128)S(1)}, f32[2,14,3,128]{3,0,2,1:T(2,128)S(1)}, u32[]{:S(2)}, u32[]{:S(2)}) collective-permute-start(f32[2,14,3,128]{3,0,2,1:T(2,128)S(1)} %copy.62), channel_id=1, source_target_pairs={{0,16},{16,32},{32,48},{48,64},{64,80},{80,96},{96,112},{1,17},{17... | collective-permute-start | bytes 129032 | tf_op jit(solution)/shard_map/ppermute | solution.py:44
  87.1 3.5 %collective-permute-done.3 = f32[2,14,3,128]{3,0,2,1:T(2,128)S(1)} collective-permute-done((f32[2,14,3,128]{3,0,2,1:T(2,128)S(1)}, f32[2,14,3,128]{3,0,2,1:T(2,128)S(1)}, u32[]{:S(2)}, u32[]{:S(2)}) %collective-permute-start.3) | collective-permute-done | bytes 43040 | tf_op jit(solution)/shard_map/ppermute | solution.py:45
  91.1 2.8 %collective-permute-start.4 = (f32[2,14,22,3]{3,0,2,1:T(2,128)S(1)}, f32[2,14,22,3]{3,0,2,1:T(2,128)S(1)}, u32[]{:S(2)}, u32[]{:S(2)}) collective-permute-start(f32[2,14,22,3]{3,0,2,1:T(2,128)S(1)} %get-tuple-element.15), channel_id=1, source_target_pairs={{0,1},{1,2},{2,3},{3,4},{4,5},{5,6},{6,7},{7,8},{8,9},{9,10},{10,1... | collective-permute-start | bytes 22184 | tf_op jit(solution)/shard_map/ppermute | solution.py:44
  93.8 2.7 %collective-permute-start.5 = (f32[2,14,22,3]{3,0,2,1:T(2,128)S(1)}, f32[2,14,22,3]{3,0,2,1:T(2,128)S(1)}, u32[]{:S(2)}, u32[]{:S(2)}) collective-permute-start(f32[2,14,22,3]{3,0,2,1:T(2,128)S(1)} %get-tuple-element.16), channel_id=1, source_target_pairs={{1,0},{2,1},{3,2},{4,3},{5,4},{6,5},{7,6},{8,7},{9,8},{10,9},{11,1... | collective-permute-start | bytes 22184 | tf_op jit(solution)/shard_map/ppermute | solution.py:45
  98.7 4.9 %collective-permute-done.5 = f32[2,14,22,3]{3,0,2,1:T(2,128)S(1)} collective-permute-done((f32[2,14,22,3]{3,0,2,1:T(2,128)S(1)}, f32[2,14,22,3]{3,0,2,1:T(2,128)S(1)}, u32[]{:S(2)}, u32[]{:S(2)}) %collective-permute-start.5) | collective-permute-done | bytes 7424 | tf_op jit(solution)/shard_map/ppermute | solution.py:45
  109.0 2.4 %fusion.80 = (f32[14,22,134]{1,0,2:T(8,128)}, f32[14,22,134]{1,0,2:T(8,128)S(1)}, f32[14,22,134]{1,0,2:T(8,128)}) fusion(f32[1,14,22,134]{2,1,3,0:T(8,128)S(1)} %copy.55, f32[134]{0:T(256)S(1)} %and_select_fusion.3, f32[14,22]{1,0:T(8,128)S(1)} %broadcast_multiply_fusion.4, f32[14,22,134]{1,0,2:T(8,128)S(1)} %multiply_multiply_fusion.1, ...), kind=kLoop, calls=%fused_computation.190 | loop fusion | flops 619080 | bytes 992296 | tf_op jit(solution)/shard_map/mul | solution.py:79
  111.4 1.6 %slice_add_fusion = f32[14,22,134]{1,0,2:T(8,128)} fusion(f32[14,22,134]{1,0,2:T(8,128)S(1)} %get-tuple-element.12), kind=kLoop, calls=%fused_computation.3 | loop fusion | flops 206360 | bytes 330176 | tf_op jit(solution)/shard_map/add | solution.py:63
  116.1 1.9 %collective-permute-start.10 = (f32[2,8,32,3]{3,2,1,0:T(8,128)S(1)}, f32[2,8,32,3]{3,2,1,0:T(8,128)S(1)}, u32[]{:S(2)}, u32[]{:S(2)}) collective-permute-start(f32[2,8,32,3]{3,2,1,0:T(8,128)S(1)} %get-tuple-element.21), channel_id=1, source_target_pairs={{0,1},{1,2},{2,3},{3,4},{4,5},{5,6},{6,7},{7,8},{8,9},{9,10},{10,1... | collective-permute-start | bytes 18440 | tf_op jit(solution)/shard_map/ppermute | solution.py:44
  118.0 3.4 %collective-permute-start.11 = (f32[2,8,32,3]{3,2,1,0:T(8,128)S(1)}, f32[2,8,32,3]{3,2,1,0:T(8,128)S(1)}, u32[]{:S(2)}, u32[]{:S(2)}) collective-permute-start(f32[2,8,32,3]{3,2,1,0:T(8,128)S(1)} %get-tuple-element.22), channel_id=1, source_target_pairs={{1,0},{2,1},{3,2},{4,3},{5,4},{6,5},{7,6},{8,7},{9,8},{10,9},{11,1... | collective-permute-start | bytes 18440 | tf_op jit(solution)/shard_map/ppermute | solution.py:45
  121.4 1.8 %collective-permute-done.10 = f32[2,8,32,3]{3,2,1,0:T(8,128)S(1)} collective-permute-done((f32[2,8,32,3]{3,2,1,0:T(8,128)S(1)}, f32[2,8,32,3]{3,2,1,0:T(8,128)S(1)}, u32[]{:S(2)}, u32[]{:S(2)}) %collective-permute-start.10) | collective-permute-done | bytes 6176 | tf_op jit(solution)/shard_map/ppermute | solution.py:44
  123.2 4.0 %collective-permute-done.11 = f32[2,8,32,3]{3,2,1,0:T(8,128)S(1)} collective-permute-done((f32[2,8,32,3]{3,2,1,0:T(8,128)S(1)}, f32[2,8,32,3]{3,2,1,0:T(8,128)S(1)}, u32[]{:S(2)}, u32[]{:S(2)}) %collective-permute-start.11) | collective-permute-done | bytes 6176 | tf_op jit(solution)/shard_map/ppermute | solution.py:45
  130.0 3.1 %fusion.6 = f32[8,16,128]{1,0,2:T(8,128)S(1)} fusion(f32[14,22,134]{1,0,2:T(8,128)} %get-tuple-element.35, f32[14,22,134]{1,0,2:T(8,128)S(1)} %get-tuple-element.12, f32[14,22,134]{1,0,2:T(8,128)} %add_bitcast_fusion, f32[14,22,134]{1,0,2:T(8,128)S(1)} %bitcast.80, f32[14,22,134]{1,0,2:T(8,128)} %slice_add_fusion, f32[14,22,134]{1,0,2:T(8,128)} %get-tuple-element.11, ...), kind=kLoop, calls=%fused_computation.22 | loop fusion | flops 114688 | bytes 491520 | tf_op jit(solution)/shard_map/add | solution.py:146
  (100 shorter events, 21.9 us)
Async XLA Ops:
  6.3 2.6 %copy-start.1 = (f32[8,16,128]{2,1,0:T(8,128)S(1)}, f32[8,16,128]{2,1,0:T(8,128)}, u32[]{:S(2)}) copy-start(f32[8,16,128]{2,1,0:T(8,128)} %param.2) | copy-start | bytes 196612
  35.0 34.5 %collective-permute-start.6 = (f32[2,16,3,64]{3,2,1,0:T(4,128)S(1)}, f32[2,16,3,64]{3,2,1,0:T(4,128)S(1)}, u32[]{:S(2)}, u32[]{:S(2)}) collective-permute-start(f32[2,16,3,64]{3,2,1,0:T(4,128)S(1)} %get-tuple-element.30), channel_id=1, source_target_pairs={{0,16},{16,32},{32,48},{48,64},{64,80},{80,96},{96,112},{1,17},{17... | collective-permute-start | bytes 73736 | tf_op jit(solution)/shard_map/ppermute | solution.py:44
  37.6 32.0 %collective-permute-start.7 = (f32[2,16,3,64]{3,2,1,0:T(4,128)S(1)}, f32[2,16,3,64]{3,2,1,0:T(4,128)S(1)}, u32[]{:S(2)}, u32[]{:S(2)}) collective-permute-start(f32[2,16,3,64]{3,2,1,0:T(4,128)S(1)} %get-tuple-element.29), channel_id=1, source_target_pairs={{16,0},{32,16},{48,32},{64,48},{80,64},{96,80},{112,96},{17,1},{33... | collective-permute-start | bytes 73736 | tf_op jit(solution)/shard_map/ppermute | solution.py:45
  39.4 15.6 %copy-start = (f32[8,16,128]{2,1,0:T(8,128)S(1)}, f32[8,16,128]{2,1,0:T(8,128)}, u32[]{:S(2)}) copy-start(f32[8,16,128]{2,1,0:T(8,128)} %param.3) | copy-start | bytes 196612
  41.1 73.0 %all-to-all-start = ((f32[32,1,512]{2,1,0:T(1,128)}), f32[32,1,512]{2,1,0:T(1,128)S(1)}, u32[]{:S(2)}, u32[]{:S(2)}) async-start(f32[32,1,512]{2,1,0:T(1,128)} %reshape.194), calls=%async_computation | async-start | bytes 131072 | tf_op jit(solution)/shard_map/all_to_all | solution.py:23
  55.1 26.9 %collective-permute-start = (f32[2,3,16,128]{3,2,1,0:T(8,128)S(1)}, f32[2,3,16,128]{3,2,1,0:T(8,128)S(1)}, u32[]{:S(2)}, u32[]{:S(2)}) collective-permute-start(f32[2,3,16,128]{3,2,1,0:T(8,128)S(1)} %get-tuple-element.33), channel_id=1, source_target_pairs={{0,128},{128,256},{256,384},{1,129},{129,257},{257,385},{2,130},{1... | collective-permute-start | bytes 147464 | tf_op jit(solution)/shard_map/ppermute | solution.py:44
  67.3 14.6 %collective-permute-start.1 = (f32[2,3,16,128]{3,2,1,0:T(8,128)S(1)}, f32[2,3,16,128]{3,2,1,0:T(8,128)S(1)}, u32[]{:S(2)}, u32[]{:S(2)}) collective-permute-start(f32[2,3,16,128]{3,2,1,0:T(8,128)S(1)} %get-tuple-element.34), channel_id=1, source_target_pairs={{128,0},{256,128},{384,256},{129,1},{257,129},{385,257},{130,2},{2... | collective-permute-start | bytes 147464 | tf_op jit(solution)/shard_map/ppermute | solution.py:45
  69.7 6.8 %collective-permute-start.8 = (f32[2,16,14,3]{3,1,2,0:T(8,128)S(1)}, f32[2,16,14,3]{3,1,2,0:T(8,128)S(1)}, u32[]{:S(2)}, u32[]{:S(2)}) collective-permute-start(f32[2,16,14,3]{3,1,2,0:T(8,128)S(1)} %get-tuple-element.25), channel_id=1, source_target_pairs={{0,1},{1,2},{2,3},{3,4},{4,5},{5,6},{6,7},{7,8},{8,9},{9,10},{10,1... | collective-permute-start | bytes 16136 | tf_op jit(solution)/shard_map/ppermute | solution.py:44
  72.5 8.9 %collective-permute-start.9 = (f32[2,16,14,3]{3,1,2,0:T(8,128)S(1)}, f32[2,16,14,3]{3,1,2,0:T(8,128)S(1)}, u32[]{:S(2)}, u32[]{:S(2)}) collective-permute-start(f32[2,16,14,3]{3,1,2,0:T(8,128)S(1)} %get-tuple-element.26), channel_id=1, source_target_pairs={{1,0},{2,1},{3,2},{4,3},{5,4},{6,5},{7,6},{8,7},{9,8},{10,9},{11,1... | collective-permute-start | bytes 16136 | tf_op jit(solution)/shard_map/ppermute | solution.py:45
  82.0 4.9 %collective-permute-start.2 = (f32[2,14,3,128]{3,0,2,1:T(2,128)S(1)}, f32[2,14,3,128]{3,0,2,1:T(2,128)S(1)}, u32[]{:S(2)}, u32[]{:S(2)}) collective-permute-start(f32[2,14,3,128]{3,0,2,1:T(2,128)S(1)} %copy.62), channel_id=1, source_target_pairs={{0,16},{16,32},{32,48},{48,64},{64,80},{80,96},{96,112},{1,17},{17... | collective-permute-start | bytes 129032 | tf_op jit(solution)/shard_map/ppermute | solution.py:44
  85.6 5.1 %collective-permute-start.3 = (f32[2,14,3,128]{3,0,2,1:T(2,128)S(1)}, f32[2,14,3,128]{3,0,2,1:T(2,128)S(1)}, u32[]{:S(2)}, u32[]{:S(2)}) collective-permute-start(f32[2,14,3,128]{3,0,2,1:T(2,128)S(1)} %copy.63), channel_id=1, source_target_pairs={{16,0},{32,16},{48,32},{64,48},{80,64},{96,80},{112,96},{17,1},{33... | collective-permute-start | bytes 129032 | tf_op jit(solution)/shard_map/ppermute | solution.py:45
  91.1 7.7 %collective-permute-start.4 = (f32[2,14,22,3]{3,0,2,1:T(2,128)S(1)}, f32[2,14,22,3]{3,0,2,1:T(2,128)S(1)}, u32[]{:S(2)}, u32[]{:S(2)}) collective-permute-start(f32[2,14,22,3]{3,0,2,1:T(2,128)S(1)} %get-tuple-element.15), channel_id=1, source_target_pairs={{0,1},{1,2},{2,3},{3,4},{4,5},{5,6},{6,7},{7,8},{8,9},{9,10},{10,1... | collective-permute-start | bytes 22184 | tf_op jit(solution)/shard_map/ppermute | solution.py:44
  93.8 9.8 %collective-permute-start.5 = (f32[2,14,22,3]{3,0,2,1:T(2,128)S(1)}, f32[2,14,22,3]{3,0,2,1:T(2,128)S(1)}, u32[]{:S(2)}, u32[]{:S(2)}) collective-permute-start(f32[2,14,22,3]{3,0,2,1:T(2,128)S(1)} %get-tuple-element.16), channel_id=1, source_target_pairs={{1,0},{2,1},{3,2},{4,3},{5,4},{6,5},{7,6},{8,7},{9,8},{10,9},{11,1... | collective-permute-start | bytes 22184 | tf_op jit(solution)/shard_map/ppermute | solution.py:45
  116.1 7.1 %collective-permute-start.10 = (f32[2,8,32,3]{3,2,1,0:T(8,128)S(1)}, f32[2,8,32,3]{3,2,1,0:T(8,128)S(1)}, u32[]{:S(2)}, u32[]{:S(2)}) collective-permute-start(f32[2,8,32,3]{3,2,1,0:T(8,128)S(1)} %get-tuple-element.21), channel_id=1, source_target_pairs={{0,1},{1,2},{2,3},{3,4},{4,5},{5,6},{6,7},{7,8},{8,9},{9,10},{10,1... | collective-permute-start | bytes 18440 | tf_op jit(solution)/shard_map/ppermute | solution.py:44
  118.0 9.2 %collective-permute-start.11 = (f32[2,8,32,3]{3,2,1,0:T(8,128)S(1)}, f32[2,8,32,3]{3,2,1,0:T(8,128)S(1)}, u32[]{:S(2)}, u32[]{:S(2)}) collective-permute-start(f32[2,8,32,3]{3,2,1,0:T(8,128)S(1)} %get-tuple-element.22), channel_id=1, source_target_pairs={{1,0},{2,1},{3,2},{4,3},{5,4},{6,5},{7,6},{8,7},{9,8},{10,9},{11,1... | collective-permute-start | bytes 18440 | tf_op jit(solution)/shard_map/ppermute | solution.py:45
where the time goes:
time: 135 us; the launch traced here: 134 us
  starting transfers between devices  52.7 us (39%)
  local copies, waits for them, and re-layouts  21.9 us (16%)
  waiting for transfers between devices  21.1 us (16%)
  other arithmetic  19.6 us (15%)
  blocking collectives  18 us (13%)
    ppermute x6, starting transfers between devices, padded_2(): before = lax.ppermute(last, axis, up)  25.7 us
    all_gather x1, blocking collectives, sent_together(): lax.all_gather(both, axis, axis=dim, tiled=True)  18 us
    ppermute x6, waiting for transfers between devices, padded_2(): after = lax.ppermute(leading, axis, down)  17.4 us
    all_to_all x1, starting transfers between devices, from_everyone(): return lax.all_to_all(copies, axis, split_axis=0, concat_axis=0, tiled=True)  13.9 us
    ppermute x6, starting transfers between devices, padded_2(): after = lax.ppermute(leading, axis, down)  13.1 us
    reshape x2, local copies, waits for them, and re-layouts, restrict(): values.reshape(values.shape[0] // 2, 2, values.shape[1] // 2, 2, values.s...  11.8 us
    reduce_sum x4, other arithmetic, restrict(): return values.reshape(values.shape[0] // 2, 2, values.shape[1] // 2, 2, v...  5.37 us
    unnamed x15, local copies, waits for them, and re-layouts  3.96 us
  transfers between devices with their start and end apart: 13, of which 7 were waited for; matrix products, arithmetic and copies ran while one was open for 12% of the time, Pallas kernels for 0%

commit v1 on v0

v1 whole, which is shorter than its diff:
```python
import functools
import itertools

import jax
import jax.numpy as jnp
from jax import lax
from jax.experimental import pallas as pl
from jax.experimental.pallas import tpu as pltpu
from jax.sharding import PartitionSpec as P

SWEEPS = 4
RELAX = 0.8
KEEP = 1.0 - RELAX
F32 = jnp.float32
VMEM = pl.BlockSpec(memory_space=pltpu.VMEM)
HIGHEST = lax.Precision.HIGHEST
AXES = ("gx", "gy", "gz")


def even_groups(nx, ny, nz):
    groups = []
    for gx, ya, za in itertools.product(range(nx), range(0, ny, 2), range(0, nz, 2)):
        groups.append([(gx * ny + ya + a) * nz + za + b for a in (0, 1) for b in (0, 1)])
    return groups


def odd_groups(nx, ny, nz):
    groups = []
    for gx in range(nx):
        flat = lambda gy, gz: (gx * ny + gy) * nz + gz % nz
        for ya, za in itertools.product(range(1, ny - 1, 2), range(1, nz, 2)):
            groups.append([flat(ya + a, za + b) for a in (0, 1) for b in (0, 1)])
        for gy, za in itertools.product((0, ny - 1), range(1, nz, 4)):
            groups.append([flat(gy, za + 2 * a + b) for a in (0, 1) for b in (0, 1)])
    return groups


def spots(ny, nz):
    gx, gy, gz = (lax.axis_index(a) for a in AXES)
    one = 2 * (gy & 1) + (gz & 1)
    inner = (gy > 0) & (gy < ny - 1)
    half = jnp.where(inner, (gy + 1) & 1, ((gz + nz - 1) & (nz - 1)) // 2 & 1)
    two = 2 * half + ((gz + 1) & 1)
    return gx, gy, gz, one, two, inner


def lanes(shape=(8, 128)):
    return lax.broadcasted_iota(jnp.int32, shape, len(shape) - 1)


def rows(shape=(8, 128)):
    return lax.broadcasted_iota(jnp.int32, shape, len(shape) - 2)


def turn(x, shift, axis):
    shift = shift % x.shape[axis]
    return pltpu.roll(x, shift, axis) if shift else x


def first_kernel(nx, r_ref, c_ref, x_ref, v_ref, w_ref, v1_ref, w1_ref, v2_ref, w2_ref, s_ref, t_ref, u_ref, d_ref):
    gx = lax.axis_index("gx")
    r, c = r_ref[...], c_ref[...]
    w = RELAX / (6.0 + c)
    v = w * r
    v_ref[...] = v
    w_ref[...] = w
    r4, c4 = r.reshape(4, 2, 16, 128), c.reshape(4, 2, 16, 128)
    t_ref[0:4] = r4[:, 0] + r4[:, 1]
    t_ref[4:8] = c4[:, 0] + c4[:, 1]
    a = t_ref[:, pl.ds(0, 8, stride=2), :] + t_ref[:, pl.ds(1, 8, stride=2), :]
    src, dst = rows((128, 128)), lanes((128, 128))
    half = jnp.where((src >> 1) == (dst & 63), 0.125, 0.0).astype(F32)
    one = jnp.dot(a.reshape(64, 128), half, precision=HIGHEST, preferred_element_type=F32)
    r1, c1 = one[:32].reshape(4, 8, 128), one[32:].reshape(4, 8, 128)
    d1 = RELAX / (1.5 + c1)
    v1, w1 = d1 * r1, d1 * 0.25
    v1_ref[...] = v1
    w1_ref[...] = w1
    a4 = a.reshape(4, 2, 8, 128)
    u_ref[...] = a4[:, 0] + a4[:, 1]
    e = u_ref[:, pl.ds(0, 4, stride=2), :] + u_ref[:, pl.ds(1, 4, stride=2), :]
    d_ref[:, 0:4, :] = e
    d_ref[:, 4:8, :] = e
    quarter = jnp.where((src >> 2) == (dst & 31), 0.015625, 0.0).astype(F32)
    two = jnp.dot(d_ref[...].reshape(32, 128), quarter, precision=HIGHEST, preferred_element_type=F32)
    r2, c2 = two[:16].reshape(2, 8, 128), two[16:].reshape(2, 8, 128)
    d2 = RELAX / (0.375 + c2)
    v2, w2 = d2 * r2, d2 * 0.0625
    v2_ref[...] = v2
    w2_ref[...] = w2
    lane, row = lanes(), rows()
    low = lane < 64
    sums = jnp.where(low, r2[0] + r2[1], c2[0] + c2[1])
    s_ref[...] = 0.5 * jnp.sum(sums, axis=0, keepdims=True)
    quad = (lane & 63) < 32
    both = [jnp.where(quad, v2[i], w2[i]) for i in (0, 1)]
    last = jnp.where(row < 4, both[0], both[1])
    for j in range(nx):
        up = j > gx
        for d in range(3):
            face = jnp.where(up, v[7 - d], v[d])
            x_ref[j, 2 * d] = face[0:8]
            x_ref[j, 2 * d + 1] = face[8:16]
        for d in range(2):
            face = jnp.where(up, w[7 - d], w[d])
            x_ref[j, 6 + 2 * d] = face[0:8]
            x_ref[j, 7 + 2 * d] = face[8:16]
        for d in range(3):
            x_ref[j, 10 + d] = jnp.where(low, jnp.where(up, v1[3 - d], v1[d]), jnp.where(up, w1[3 - d], w1[d]))
        x_ref[j, 13] = last


def extended(nx, gx, v_ref, w_ref, v1_ref, w1_ref, v2_ref, w2_ref, x_ref):
    lane, row = lanes(), rows()
    low = lane < 64
    quad = (lane & 63) < 32
    left, right = jnp.maximum(gx - 1, 0), jnp.minimum(gx + 1, nx - 1)
    far_left, far_right = jnp.maximum(gx - 2, 0), jnp.minimum(gx + 2, nx - 1)
    has_left, has_right = gx > 0, gx < nx - 1
    has_far_left, has_far_right = gx > 1, gx < nx - 2

    def pick(slot, tile, have):
        return jnp.where(have, x_ref[slot, tile], 0.0)

    def pair(slot, tile, have):
        return jnp.concatenate([pick(slot, tile, have), pick(slot, tile + 1, have)], axis=0)

    def fine(slot, d, have):
        return pair(slot, 2 * d, have), (pair(slot, 6 + 2 * d, have) if d < 2 else None)

    def middle(slot, d, have):
        t = pick(slot, 10 + d, have)
        s = turn(t, 64, 1)
        return jnp.where(low, t, s), jnp.where(low, s, t)

    def coarse(slot, layer, have):
        t = pick(slot, 13, have)
        s = turn(t, 4, 0)
        t = jnp.where(row < 4, t, s) if layer == 0 else jnp.where(row < 4, s, t)
        s = turn(t, 32, 1)
        return jnp.where(quad, t, s), jnp.where(quad, s, t)

    level0 = (
        [fine(left, d, has_left) for d in (2, 1, 0)]
        + [(v_ref[i], w_ref[i]) for i in range(8)]
        + [fine(right, d, has_right) for d in (0, 1, 2)]
    )
    level1 = (
        [middle(left, d, has_left) for d in (2, 1, 0)]
        + [(v1_ref[i], w1_ref[i]) for i in range(4)]
        + [middle(right, d, has_right) for d in (0, 1, 2)]
    )
    level2 = (
        [coarse(far_left, 1, has_far_left), coarse(left, 0, has_left), coarse(left, 1, has_left)]
        + [(v2_ref[i], w2_ref[i]) for i in range(2)]
        + [coarse(right, 0, has_right), coarse(right, 1, has_right), coarse(far_right, 0, has_far_right)]
    )
    return level0, level1, level2


def edge_lanes(layers):
    shape = layers[0][0].shape
    lane = lanes(shape)
    packed = jnp.zeros(shape, F32)
    for k, (v, w) in enumerate(layers):
        at = 10 * k
        packed = jnp.where((lane >= at) & (lane < at + 6), turn(v, at + 3, 1), packed)
        packed = jnp.where((lane >= at + 6) & (lane < at + 10), turn(w, at + 8, 1), packed)
    return packed


def second_kernel(nx, ny, nz, v_ref, w_ref, v1_ref, w1_ref, v2_ref, w2_ref, x_ref, one_ref, two_ref):
    gx, gy, gz, one, two, _ = spots(ny, nz)
    level0, level1, level2 = extended(nx, gx, v_ref, w_ref, v1_ref, w1_ref, v2_ref, w2_ref, x_ref)
    lane, row = lanes(), rows()
    low = lane < 64
    quad = (lane & 63) < 32
    up = (gy & 1) == 0
    ends = [edge_lanes(level0[1:13])]
    ends = [ends[0][0:8], ends[0][8:16], edge_lanes(level1[1:9]), edge_lanes(level2[1:7])]
    for i, tile in enumerate(ends):
        for slot in (one ^ 1, one ^ 2, one ^ 3):
            one_ref[slot, 12 + i] = tile
        for slot in (two ^ 1, two ^ 3):
            two_ref[slot, i] = tile
    for k in range(12):
        v, w = level0[k + 1]
        if k < 8:
            a, b = level1[k + 1]
            extra = jnp.where(low, a, b)
        elif k < 11:
            a, b = (jnp.where(quad, *level2[1 + 2 * (k - 8) + i]) for i in (0, 1))
            extra = jnp.where(low, a, b)
        else:
            extra = jnp.zeros((8, 128), F32)
        high = jnp.where(row >= 5, v[8:16], jnp.where(row >= 3, turn(w[8:16], 5, 0), turn(extra, 3, 0)))
        base = jnp.where(row < 3, v[0:8], jnp.where(row < 5, turn(w[0:8], 3, 0), turn(extra, 5, 0)))
        one_ref[one ^ 2, k] = jnp.where(up, high, base)
        two_ref[two ^ 2, k] = jnp.where(up, base, high)


def forward_kernel(ny, nz, got_ref, old_ref, two_ref):
    _, _, _, one, two, _ = spots(ny, nz)
    two_ref[...] = old_ref[...]
    for i in range(4):
        two_ref[two ^ 2, 12 + i] = got_ref[one ^ 1, 12 + i]
        two_ref[two ^ 1, 12 + i] = got_ref[one ^ 2, 12 + i]


def around(v, above, below):
    return (
        above
        + below
        + turn(v, 1, 0)
        + turn(v, -1, 0)
        + turn(v, 1, 1)
        + turn(v, -1, 1)
    )


def relaxed(v_ref, w_ref, a_ref, b_ref, count):
    done = []
    for sweep in range(SWEEPS - 1):
        source = (v_ref, a_ref, b_ref)[sweep]
        target = (a_ref, b_ref, None)[sweep]
        for i in range(sweep + 1, count - sweep - 1):
            v = source[i]
            new = KEEP * v + v_ref[i] + w_ref[i] * around(v, source[i - 1], source[i + 1])
            if target is None:
                done.append(new)
            else:
                target[i] = new
    return done


def last_kernel(
    nx, ny, nz, v_ref, w_ref, v1_ref, w1_ref, v2_ref, w2_ref, x_ref, one_ref, two_ref, plane_ref, out_ref,
    fv, fw, fa, fb, mv, mw, ma, mb, cv, cw, ca, cb, wide_ref, deep_ref,
):
    gx, gy, gz, one, two, has_y = spots(ny, nz)
    has_z = (gz > 0) & (gz < nz - 1)
    up = (gy & 1) == 0
    ahead = (gz & 1) == 0
    level0, level1, level2 = extended(nx, gx, v_ref, w_ref, v1_ref, w1_ref, v2_ref, w2_ref, x_ref)
    lane, row = lanes(), rows()
    part = lane - 10 * (lane // 10)
    first_half = (part < 3) | ((part >= 6) & (part < 8))
    from_one = jnp.where(ahead, jnp.where(first_half, 0, 1), jnp.where(first_half, 1, 0)) == 1

    own, plus, minus = [], [], []
    for i in range(4):
        z_two = jnp.where(has_z, two_ref[two ^ 1, i], 0.0)
        own.append(jnp.where(from_one, one_ref[one ^ 1, 12 + i], z_two))
        z_two = jnp.where(has_z, two_ref[two ^ 1, 12 + i], 0.0)
        t_one = jnp.where(from_one, one_ref[one ^ 3, 12 + i], z_two)
        z_two = jnp.where(has_z, two_ref[two ^ 3, i], 0.0)
        t_two = jnp.where(has_y, jnp.where(from_one, two_ref[two ^ 2, 12 + i], z_two), 0.0)
        plus.append(jnp.where(up, t_one, t_two))
        minus.append(jnp.where(up, t_two, t_one))
    none = jnp.zeros((8, 128), F32)

    def outer(p, m):
        return jnp.where(row < 3, p, jnp.where(row >= 5, m, none))

    z0 = jnp.concatenate([own[0], own[1], outer(plus[0], minus[1])], axis=0)
    z1 = jnp.concatenate([own[2], outer(plus[2], minus[2])], axis=0)
    z2 = jnp.concatenate([jnp.where(row < 4, own[3], plus[3]), jnp.where(row >= 5, minus[3], none)], axis=0)

    lane16 = lanes((16, 128))
    fv[0, 0:16, 0:128] = level0[0][0]
    fv[13, 0:16, 0:128] = level0[13][0]
    for i in (0, 13):
        fv[i, 16:24, 0:128] = none
        fv[i, :, 128:256] = jnp.zeros((24, 128), F32)
    for k in range(12):
        a = one_ref[one ^ 2, k]
        b = jnp.where(has_y, two_ref[two ^ 2, k], 0.0)
        p, m = jnp.where(up, a, b), jnp.where(up, b, a)
        v, w = level0[k + 1]
        fv[k + 1, 0:16, 0:128] = v
        fw[k + 1, 0:16, 0:128] = w
        fv[k + 1, 16:24, 0:128] = outer(p, m)
        fw[k + 1, 16:24, 0:128] = jnp.where(row < 2, turn(p, 5, 0), jnp.where(row >= 6, turn(m, 3, 0), none))
        fv[k + 1, :, 128:256] = turn(z0, -(10 * k + 3), 1)
        fw[k + 1, :, 128:256] = turn(z0, -(10 * k + 8), 1)
        if k < 8:
            extra = outer(turn(p, 3, 0), turn(m, 5, 0))
            v, w = level1[k + 1]
            v = jnp.concatenate([v, extra], axis=0)
            w = jnp.concatenate([w, turn(extra, 64, 1)], axis=0)
            at = 10 * k + 3
            mv[k + 1] = jnp.where(lane16 < 64, v, jnp.where(lane16 < 96, turn(z1, 64 - at, 1), turn(z1, -at, 1)))
            at = 10 * k + 8
            mw[k + 1] = jnp.where(lane16 < 64, w, jnp.where(lane16 < 96, turn(z1, 64 - at, 1), turn(z1, -at, 1)))
        elif k < 11:
            near, far = turn(p, 7, 0), turn(m, 5, 0)
            for i in (0, 1):
                j = 2 * (k - 8) + i
                v, w = level2[j + 1]
                for field, target in ((0, cv), (1, cw)):
                    shift = -(64 * i + 32 * field)
                    top = jnp.where(row < 4, (v, w)[field], turn(near, shift, 1))
                    full = jnp.concatenate([top, jnp.where(row >= 5, turn(far, shift, 1), none)], axis=0)
                    at = 10 * j + (3, 8)[field]
                    ends = jnp.where(lane16 < 64, turn(z2, 32 - at, 1), turn(z2, -at, 1))
                    target[j + 1] = jnp.where(lane16 < 32, full, ends)
    for i in (0, 9):
        mv[i, 0:8] = level1[i][0]
        mv[i, 8:16] = none
    for i in (0, 7):
        cv[i, 0:8] = level2[i][0]
        cv[i, 8:16] = none

    coarse = relaxed(cv, cw, ca, cb, 8)
    s = plane_ref[...]
    plane = jnp.where(lane < 64, s / (turn(jnp.broadcast_to(s, (8, 128)), 64, 1) + 16.0), 0.0)
    src, dst = rows((128, 128)), lanes((128, 128))
    spread4 = jnp.where(src == (dst >> 2), 1.0, 0.0).astype(F32)
    spread2 = jnp.where(src == (dst >> 1), 1.0, 0.0).astype(F32)
    c = jnp.concatenate([layer[0:8] + plane for layer in coarse], axis=0)
    c = jnp.dot(c, spread4, precision=HIGHEST, preferred_element_type=F32).reshape(2, 8, 128)
    middle = relaxed(mv, mw, ma, mb, 10)
    m = jnp.concatenate([layer[0:8] for layer in middle], axis=0)
    m = jnp.dot(m, spread2, precision=HIGHEST, preferred_element_type=F32).reshape(4, 8, 128)
    for i in range(2):
        for j in range(2):
            deep_ref[i, pl.ds(j, 4, stride=2), :] = c[i, 0:4]
    for i in range(4):
        total = m[i] + deep_ref[i // 2]
        for j in range(2):
            wide_ref[i, pl.ds(j, 8, stride=2), :] = total
    fine = relaxed(fv, fw, fa, fb, 14)
    for i in range(8):
        out_ref[i] = fine[i][0:16, 0:128] + wide_ref[i // 2]


def per_device(nx, ny, nz, right_side, coefficient):
    shape = jax.ShapeDtypeStruct
    call = functools.partial(pl.pallas_call)
    kept = [shape((8, 16, 128), F32)] * 2 + [shape((4, 8, 128), F32)] * 2 + [shape((2, 8, 128), F32)] * 2
    x_out, *own, sums = call(
        functools.partial(first_kernel, nx),
        out_shape=[shape((nx, 14, 8, 128), F32)] + kept + [shape((1, 128), F32)],
        in_specs=[VMEM] * 2,
        out_specs=[VMEM] * 8,
        scratch_shapes=[pltpu.VMEM((8, 16, 128), F32), pltpu.VMEM((4, 8, 128), F32), pltpu.VMEM((4, 8, 128), F32)],
        name="first",
    )(right_side, coefficient)
    x_in = lax.all_to_all(x_out, "gx", 0, 0, tiled=True)
    copies = jnp.broadcast_to(sums[None], (nx * ny, 1, 128))
    plane = jnp.sum(lax.all_to_all(copies, ("gx", "gy"), 0, 0, tiled=True), axis=0)
    one_out, two_out = call(
        functools.partial(second_kernel, nx, ny, nz),
        out_shape=[shape((4, 16, 8, 128), F32)] * 2,
        in_specs=[VMEM] * 7,
        out_specs=[VMEM] * 2,
        name="second",
    )(*own, x_in)
    one_in = lax.all_to_all(one_out, AXES, 0, 0, tiled=True, axis_index_groups=even_groups(nx, ny, nz))
    two_out = call(
        functools.partial(forward_kernel, ny, nz),
        out_shape=shape((4, 16, 8, 128), F32),
        in_specs=[VMEM] * 2,
        out_specs=VMEM,
        name="forward",
    )(one_in, two_out)
    two_in = lax.all_to_all(two_out, AXES, 0, 0, tiled=True, axis_index_groups=odd_groups(nx, ny, nz))
    fine, middle, coarse = (pltpu.VMEM(s, F32) for s in ((14, 24, 256), (10, 16, 128), (8, 16, 128)))
    return call(
        functools.partial(last_kernel, nx, ny, nz),
        out_shape=shape((8, 16, 128), F32),
        in_specs=[VMEM] * 10,
        out_specs=VMEM,
        scratch_shapes=[fine] * 4 + [middle] * 4 + [coarse] * 4
        + [pltpu.VMEM((4, 16, 128), F32), pltpu.VMEM((2, 8, 128), F32)],
        name="last",
    )(*own, x_in, one_in, two_in, plane)


def solution(mesh):
    nx, ny, nz = (mesh.shape[a] for a in AXES)
    spec = P(*AXES)
    return jax.shard_map(
        functools.partial(per_device, nx, ny, nz), mesh=mesh, in_specs=(spec, spec), out_specs=spec, check_vma=False
    )
```

time: 135 us -> 85.3 us (0.63)
  the two profiles are of different devices: /device:TPU:25 before, /device:TPU:1 now
where the time goes in v1:
time: 85.3 us; the launch traced here: 84.8 us
  blocking collectives  45.7 us (54%)
  waiting for transfers between devices  14.2 us (17%)
  starting transfers between devices  13.7 us (16%)
  Pallas kernels  8.62 us (10%)
  local copies, waits for them, and re-layouts  1.98 us (2%)
    all_to_all x1, blocking collectives, per_device(): x_in = lax.all_to_all(x_out, 'gx', 0, 0, tiled=True)  30.4 us
    all_to_all x1, blocking collectives, per_device(): lax.all_to_all(one_out, AXES, 0, 0, tiled=True, axis_index_groups=even_gr...  15.2 us
    all_to_all x1, waiting for transfers between devices, per_device(): lax.all_to_all(copies, ('gx', 'gy'), 0, 0, tiled=True)  9.87 us
    all_to_all x1, starting transfers between devices, per_device(): lax.all_to_all(copies, ('gx', 'gy'), 0, 0, tiled=True)  7.66 us
    all_to_all x1, starting transfers between devices, per_device(): lax.all_to_all(two_out, AXES, 0, 0, tiled=True, axis_index_groups=odd_gro...  6.06 us
    all_to_all x1, waiting for transfers between devices, per_device(): lax.all_to_all(two_out, AXES, 0, 0, tiled=True, axis_index_groups=odd_gro...  4.36 us
    pallas_call x1, Pallas kernels, per_device(): call(functools.partial(last_kernel, nx, ny, nz), out_shape=shape((8, 16,...  2.92 us
    pallas_call x1, Pallas kernels, per_device(): call(functools.partial(second_kernel, nx, ny, nz), out_shape=[shape((4, 1...  2.06 us
  transfers between devices with their start and end apart: 2, of which 2 were waited for; matrix products, arithmetic and copies ran while one was open for 1% of the time, Pallas kernels for 2%

profile of v1, /device:TPU:1, one launch (start us, length us, event | category | flops | bytes accessed | tf_op | source)
XLA Modules:
  0.0 84.8 jit_solution(5506341044880757899)
XLA Ops:
  0.0 1.9 %first.1 = (f32[4,14,8,128]{3,2,1,0:T(8,128)}, f32[8,16,128]{2,1,0:T(8,128)}, f32[8,16,128]{2,1,0:T(8,128)}, f32[4,8,128]{2,1,0:T(8,128)}, f32[4,8,128]{2,1,0:T(...) custom-call(f32[8,16,128]{2,1,0:T(8,128)} %r_ref.1, f32[8,16,128]{2,1,0:T(8,128)} %c_ref.1), custom_call_target="tpu_custom_call" | custom-call | tf_op jit(solution)/shard_map/first/pallas_call | solution.py:341
  1.9 30.4 %all_to_all.20.x_ref = f32[4,14,8,128]{3,2,1,0:T(8,128)} all-to-all(f32[4,14,8,128]{3,2,1,0:T(8,128)} %get-tuple-element.21), channel_id=1, replica_groups=mesh['gx'=4,'gy'=8,'gz'=16] {'gx'}, dimensions={0} | all-to-all | bytes 458752 | tf_op jit(solution)/shard_map/all_to_all | solution.py:349
  32.3 2.1 %second.1 = (f32[4,16,8,128]{3,2,1,0:T(8,128)}, f32[4,16,8,128]{3,2,1,0:T(8,128)}) custom-call(f32[8,16,128]{2,1,0:T(8,128)} %get-tuple-element.15.v_ref, f32[8,16,128]{2,1,0:T(8,128)} %get-tuple-element.16.w_ref, f32[4,8,128]{2,1,0:T(8,128)} %get-tuple-element.17.v1_ref, f32[4,8,128]{2,1,0:T(8,128)} %get-tuple-element.18.w1_ref, ...), custom_call_target="tpu_custom_call" | custom-call | tf_op jit(solution)/shard_map/second/pallas_call | solution.py:352
  34.4 15.2 %all_to_all.21.got_ref.one_ref = f32[4,16,8,128]{3,2,1,0:T(8,128)} all-to-all(f32[4,16,8,128]{3,2,1,0:T(8,128)} %get-tuple-element.22), channel_id=1, replica_groups={{0,1,16,17},{2,3,18,19},{4,5,20,21},{6,7,22,23},{8,9,24,25},{10,11,26,2..., dimensions={0} | all-to-all | bytes 524288 | tf_op jit(solution)/shard_map/all_to_all | solution.py:359
  49.6 0.0 copy-start.1
  49.6 0.7 copy-done.1
  50.3 0.6 broadcast_in_dim.9
  50.9 7.7 %all-to-all-start.3 = ((f32[32,1,128]{2,1,0:T(1,128)}), f32[32,1,128]{2,1,0:T(1,128)S(1)}, u32[]{:S(2)}, u32[]{:S(2)}) async-start(f32[32,1,128]{2,1,0:T(1,128)} %broadcast_in_dim.9), calls=%async_computation.3 | async-start | bytes 32768 | tf_op jit(solution)/shard_map/all_to_all | solution.py:351
  58.5 1.8 %forward.1 = f32[4,16,8,128]{3,2,1,0:T(8,128)} custom-call(f32[4,16,8,128]{3,2,1,0:T(8,128)} %all_to_all.21.got_ref.one_ref, f32[4,16,8,128]{3,2,1,0:T(8,128)} %get-tuple-element.23.old_ref), custom_call_target="tpu_custom_call" | custom-call | tf_op jit(solution)/shard_map/forward/pallas_call | solution.py:360
  60.3 9.9 %all-to-all-done.3 = f32[32,1,128]{2,1,0:T(1,128)S(1)} async-done(((f32[32,1,128]{2,1,0:T(1,128)}), f32[32,1,128]{2,1,0:T(1,128)S(1)}, u32[]{:S(2)}, u32[]{:S(2)}) %all-to-all-start.3) | async-done | bytes 16416 | tf_op jit(solution)/shard_map/all_to_all | solution.py:351
  70.2 6.1 %all-to-all-start.2 = ((f32[4,16,8,128]{3,2,1,0:T(8,128)}), f32[4,16,8,128]{3,2,1,0:T(8,128)S(1)}, u32[]{:S(2)}, u32[]{:S(2)}) async-start(f32[4,16,8,128]{3,2,1,0:T(8,128)} %forward.1), calls=%async_computation.2 | async-start | bytes 524288 | tf_op jit(solution)/shard_map/all_to_all | solution.py:367
  76.2 0.6 reduce_sum.11
  76.8 4.4 %all-to-all-done.2.two_ref = f32[4,16,8,128]{3,2,1,0:T(8,128)S(1)} async-done(((f32[4,16,8,128]{3,2,1,0:T(8,128)}), f32[4,16,8,128]{3,2,1,0:T(8,128)S(1)}, u32[]{:S(2)}, u32[]{:S(2)}) %all-to-all-start.2) | async-done | bytes 262176 | tf_op jit(solution)/shard_map/all_to_all | solution.py:367
  81.2 0.0 copy-start
  81.2 0.7 copy-done
  81.9 2.9 %last.1 = f32[8,16,128]{2,1,0:T(8,128)} custom-call(f32[8,16,128]{2,1,0:T(8,128)} %get-tuple-element.15.v_ref, f32[8,16,128]{2,1,0:T(8,128)} %get-tuple-element.16.w_ref, f32[4,8,128]{2,1,0:T(8,128)} %get-tuple-element.17.v1_ref, f32[4,8,128]{2,1,0:T(8,128)} %get-tuple-element.18.w1_ref, f32[2,8,128]{2,1,0:T(8,128)} %get-tuple-element.19.v2_ref, ...), custom_call_target="tpu_custom_call" | custom-call | tf_op jit(solution)/shard_map/last/pallas_call | solution.py:369
Async XLA Ops:
  49.6 0.7 copy-start.1
  50.9 19.3 %all-to-all-start.3 = ((f32[32,1,128]{2,1,0:T(1,128)}), f32[32,1,128]{2,1,0:T(1,128)S(1)}, u32[]{:S(2)}, u32[]{:S(2)}) async-start(f32[32,1,128]{2,1,0:T(1,128)} %broadcast_in_dim.9), calls=%async_computation.3 | async-start | bytes 32768 | tf_op jit(solution)/shard_map/all_to_all | solution.py:351
  70.2 11.0 %all-to-all-start.2 = ((f32[4,16,8,128]{3,2,1,0:T(8,128)}), f32[4,16,8,128]{3,2,1,0:T(8,128)S(1)}, u32[]{:S(2)}, u32[]{:S(2)}) async-start(f32[4,16,8,128]{3,2,1,0:T(8,128)} %forward.1), calls=%async_computation.2 | async-start | bytes 524288 | tf_op jit(solution)/shard_map/all_to_all | solution.py:367
  81.2 0.7 copy-start

commit v2 on v1

--- a/solution.py
+++ b/solution.py
@@ -7,6 +7,7 @@
 from jax.experimental import pallas as pl
 from jax.experimental.pallas import tpu as pltpu
 from jax.sharding import PartitionSpec as P
+
 
 SWEEPS = 4
 RELAX = 0.8
@@ -57,9 +58,19 @@
     return pltpu.roll(x, shift, axis) if shift else x
 
 
-def first_kernel(nx, r_ref, c_ref, x_ref, v_ref, w_ref, v1_ref, w1_ref, v2_ref, w2_ref, s_ref, t_ref, u_ref, d_ref):
+def first_kernel(
+    nx, ny, r_ref, c_ref, a_ref, b_ref, s_ref, v_ref, w_ref, v1_ref, w1_ref, v2_ref, w2_ref, t_ref, u_ref, d_ref,
+    rv_ref, cv_ref, sems,
+):
     gx = lax.axis_index("gx")
-    r, c = r_ref[...], c_ref[...]
+    fetches = [
+        pltpu.make_async_copy(src, dst, sems.at[i]) for i, (src, dst) in enumerate(((r_ref, rv_ref), (c_ref, cv_ref)))
+    ]
+    for fetch in fetches:
+        fetch.start()
+    for fetch in fetches:
+        fetch.wait()
+    r, c = rv_ref[...], cv_ref[...]
     w = RELAX / (6.0 + c)
     v = w * r
     v_ref[...] = v
@@ -91,69 +102,70 @@
     lane, row = lanes(), rows()
     low = lane < 64
     sums = jnp.where(low, r2[0] + r2[1], c2[0] + c2[1])
-    s_ref[...] = 0.5 * jnp.sum(sums, axis=0, keepdims=True)
+    sums = 0.5 * jnp.sum(sums, axis=0, keepdims=True)
     quad = (lane & 63) < 32
     both = [jnp.where(quad, v2[i], w2[i]) for i in (0, 1)]
     last = jnp.where(row < 4, both[0], both[1])
+    ends = [jnp.sum(jnp.where((lane >> 5) == row, v2[i], 0.0), axis=0, keepdims=True) for i in (0, 1)]
     for j in range(nx):
-        up = j > gx
+        far = jnp.where(j > gx, ends[1], ends[0])
+        mail = jnp.concatenate([sums, far], axis=0)
+        s_ref[j * ny : (j + 1) * ny] = jnp.broadcast_to(mail[None], (ny, 2, 128))
+    even = (gx & 1) == 0
+    for x_ref, up in ((a_ref, even), (b_ref, jnp.logical_not(even))):
         for d in range(3):
             face = jnp.where(up, v[7 - d], v[d])
-            x_ref[j, 2 * d] = face[0:8]
-            x_ref[j, 2 * d + 1] = face[8:16]
+            x_ref[2 * d] = face[0:8]
+            x_ref[2 * d + 1] = face[8:16]
         for d in range(2):
             face = jnp.where(up, w[7 - d], w[d])
-            x_ref[j, 6 + 2 * d] = face[0:8]
-            x_ref[j, 7 + 2 * d] = face[8:16]
+            x_ref[6 + 2 * d] = face[0:8]
+            x_ref[7 + 2 * d] = face[8:16]
         for d in range(3):
-            x_ref[j, 10 + d] = jnp.where(low, jnp.where(up, v1[3 - d], v1[d]), jnp.where(up, w1[3 - d], w1[d]))
-        x_ref[j, 13] = last
-
-
-def extended(nx, gx, v_ref, w_ref, v1_ref, w1_ref, v2_ref, w2_ref, x_ref):
+            x_ref[10 + d] = jnp.where(low, jnp.where(up, v1[3 - d], v1[d]), jnp.where(up, w1[3 - d], w1[d]))
+        x_ref[13] = last
+
+
+def extended(gx, v_ref, w_ref, v1_ref, w1_ref, v2_ref, w2_ref, a_ref, b_ref, far=(None, None)):
     lane, row = lanes(), rows()
     low = lane < 64
     quad = (lane & 63) < 32
-    left, right = jnp.maximum(gx - 1, 0), jnp.minimum(gx + 1, nx - 1)
-    far_left, far_right = jnp.maximum(gx - 2, 0), jnp.minimum(gx + 2, nx - 1)
-    has_left, has_right = gx > 0, gx < nx - 1
-    has_far_left, has_far_right = gx > 1, gx < nx - 2
-
-    def pick(slot, tile, have):
-        return jnp.where(have, x_ref[slot, tile], 0.0)
-
-    def pair(slot, tile, have):
-        return jnp.concatenate([pick(slot, tile, have), pick(slot, tile + 1, have)], axis=0)
-
-    def fine(slot, d, have):
-        return pair(slot, 2 * d, have), (pair(slot, 6 + 2 * d, have) if d < 2 else None)
-
-    def middle(slot, d, have):
-        t = pick(slot, 10 + d, have)
+    even = (gx & 1) == 0
+    left = lambda tile: jnp.where(even, b_ref[tile], a_ref[tile])
+    right = lambda tile: jnp.where(even, a_ref[tile], b_ref[tile])
+
+    def pair(side, tile):
+        return jnp.concatenate([side(tile), side(tile + 1)], axis=0)
+
+    def fine(side, d):
+        return pair(side, 2 * d), (pair(side, 6 + 2 * d) if d < 2 else None)
+
+    def middle(side, d):
+        t = side(10 + d)
         s = turn(t, 64, 1)
         return jnp.where(low, t, s), jnp.where(low, s, t)
 
-    def coarse(slot, layer, have):
-        t = pick(slot, 13, have)
+    def coarse(side, layer):
+        t = side(13)
         s = turn(t, 4, 0)
         t = jnp.where(row < 4, t, s) if layer == 0 else jnp.where(row < 4, s, t)
         s = turn(t, 32, 1)
         return jnp.where(quad, t, s), jnp.where(quad, s, t)
 
     level0 = (
-        [fine(left, d, has_left) for d in (2, 1, 0)]
+        [fine(left, d) for d in (2, 1, 0)]
         + [(v_ref[i], w_ref[i]) for i in range(8)]
-        + [fine(right, d, has_right) for d in (0, 1, 2)]
+        + [fine(right, d) for d in (0, 1, 2)]
     )
     level1 = (
-        [middle(left, d, has_left) for d in (2, 1, 0)]
+        [middle(left, d) for d in (2, 1, 0)]
         + [(v1_ref[i], w1_ref[i]) for i in range(4)]
-        + [middle(right, d, has_right) for d in (0, 1, 2)]
+        + [middle(right, d) for d in (0, 1, 2)]
     )
     level2 = (
-        [coarse(far_left, 1, has_far_left), coarse(left, 0, has_left), coarse(left, 1, has_left)]
+        [(far[0], None), coarse(left, 0), coarse(left, 1)]
         + [(v2_ref[i], w2_ref[i]) for i in range(2)]
-        + [coarse(right, 0, has_right), coarse(right, 1, has_right), coarse(far_right, 0, has_far_right)]
+        + [coarse(right, 0), coarse(right, 1), (far[1], None)]
     )
     return level0, level1, level2
 
@@ -169,9 +181,9 @@
     return packed
 
 
-def second_kernel(nx, ny, nz, v_ref, w_ref, v1_ref, w1_ref, v2_ref, w2_ref, x_ref, one_ref, two_ref):
-    gx, gy, gz, one, two, _ = spots(ny, nz)
-    level0, level1, level2 = extended(nx, gx, v_ref, w_ref, v1_ref, w1_ref, v2_ref, w2_ref, x_ref)
+def second_kernel(ny, nz, v_ref, w_ref, v1_ref, w1_ref, v2_ref, w2_ref, a_ref, b_ref, one_ref, two_ref):
+    gx, gy, _, one, two, _ = spots(ny, nz)
+    level0, level1, level2 = extended(gx, v_ref, w_ref, v1_ref, w1_ref, v2_ref, w2_ref, a_ref, b_ref)
     lane, row = lanes(), rows()
     low = lane < 64
     quad = (lane & 63) < 32
@@ -234,15 +246,26 @@
 
 
 def last_kernel(
-    nx, ny, nz, v_ref, w_ref, v1_ref, w1_ref, v2_ref, w2_ref, x_ref, one_ref, two_ref, plane_ref, out_ref,
+    nx, ny, nz, v_ref, w_ref, v1_ref, w1_ref, v2_ref, w2_ref, ax_ref, bx_ref, one_ref, two_ref, s_ref, out_ref,
     fv, fw, fa, fb, mv, mw, ma, mb, cv, cw, ca, cb, wide_ref, deep_ref,
 ):
     gx, gy, gz, one, two, has_y = spots(ny, nz)
     has_z = (gz > 0) & (gz < nz - 1)
     up = (gy & 1) == 0
     ahead = (gz & 1) == 0
-    level0, level1, level2 = extended(nx, gx, v_ref, w_ref, v1_ref, w1_ref, v2_ref, w2_ref, x_ref)
     lane, row = lanes(), rows()
+
+    def far(slot, have):
+        t = jnp.broadcast_to(s_ref[slot * ny + gy, 1:2], (8, 128))
+        spread = jnp.zeros((8, 128), F32)
+        for i in range(4):
+            spread = jnp.where(row == i, turn(t, -32 * i, 1), spread)
+        return jnp.where(have, spread, 0.0)
+
+    outer_layers = far(jnp.maximum(gx - 2, 0), gx > 1), far(jnp.minimum(gx + 2, nx - 1), gx < nx - 2)
+    level0, level1, level2 = extended(
+        gx, v_ref, w_ref, v1_ref, w1_ref, v2_ref, w2_ref, ax_ref, bx_ref, outer_layers
+    )
     part = lane - 10 * (lane // 10)
     first_half = (part < 3) | ((part >= 6) & (part < 8))
     from_one = jnp.where(ahead, jnp.where(first_half, 0, 1), jnp.where(first_half, 1, 0)) == 1
@@ -312,7 +335,7 @@
         cv[i, 8:16] = none
 
     coarse = relaxed(cv, cw, ca, cb, 8)
-    s = plane_ref[...]
+    s = jnp.sum(s_ref[...], axis=0)[0:1]
     plane = jnp.where(lane < 64, s / (turn(jnp.broadcast_to(s, (8, 128)), 64, 1) + 16.0), 0.0)
     src, dst = rows((128, 128)), lanes((128, 128))
     spread4 = jnp.where(src == (dst >> 2), 1.0, 0.0).astype(F32)
@@ -336,32 +359,39 @@
 
 def per_device(nx, ny, nz, right_side, coefficient):
     shape = jax.ShapeDtypeStruct
-    call = functools.partial(pl.pallas_call)
+    call = pl.pallas_call
     kept = [shape((8, 16, 128), F32)] * 2 + [shape((4, 8, 128), F32)] * 2 + [shape((2, 8, 128), F32)] * 2
-    x_out, *own, sums = call(
-        functools.partial(first_kernel, nx),
-        out_shape=[shape((nx, 14, 8, 128), F32)] + kept + [shape((1, 128), F32)],
-        in_specs=[VMEM] * 2,
-        out_specs=[VMEM] * 8,
-        scratch_shapes=[pltpu.VMEM((8, 16, 128), F32), pltpu.VMEM((4, 8, 128), F32), pltpu.VMEM((4, 8, 128), F32)],
+    a_out, b_out, s_out, *own = call(
+        functools.partial(first_kernel, nx, ny),
+        out_shape=[shape((14, 8, 128), F32)] * 2 + [shape((nx * ny, 2, 128), F32)] + kept,
+        in_specs=[pl.BlockSpec(memory_space=pltpu.HBM)] * 2,
+        out_specs=[VMEM] * 9,
+        scratch_shapes=[pltpu.VMEM(s, F32) for s in ((8, 16, 128), (4, 8, 128), (4, 8, 128), (8, 16, 128), (8, 16, 128))]
+        + [pltpu.SemaphoreType.DMA((2,))],
+        compiler_params=pltpu.CompilerParams(vmem_limit_bytes=8 << 20),
         name="first",
     )(right_side, coefficient)
-    x_in = lax.all_to_all(x_out, "gx", 0, 0, tiled=True)
-    copies = jnp.broadcast_to(sums[None], (nx * ny, 1, 128))
-    plane = jnp.sum(lax.all_to_all(copies, ("gx", "gy"), 0, 0, tiled=True), axis=0)
+    near = [(i, i ^ 1) for i in range(nx)]
+    across = [(i, i + 1 if i & 1 else i - 1) for i in range(1, nx - 1)]
+    b_in = lax.ppermute(b_out, "gx", across)
+    s_in = lax.all_to_all(s_out, ("gx", "gy"), 0, 0, tiled=True)
+    a_in = lax.ppermute(a_out, "gx", near)
     one_out, two_out = call(
-        functools.partial(second_kernel, nx, ny, nz),
+        functools.partial(second_kernel, ny, nz),
         out_shape=[shape((4, 16, 8, 128), F32)] * 2,
-        in_specs=[VMEM] * 7,
+        in_specs=[VMEM] * 8,
         out_specs=[VMEM] * 2,
+        compiler_params=pltpu.CompilerParams(vmem_limit_bytes=8 << 20),
         name="second",
-    )(*own, x_in)
+    )(*own, a_in, b_in)
+    one_out, s_in = lax.optimization_barrier((one_out, s_in))
     one_in = lax.all_to_all(one_out, AXES, 0, 0, tiled=True, axis_index_groups=even_groups(nx, ny, nz))
     two_out = call(
         functools.partial(forward_kernel, ny, nz),
         out_shape=shape((4, 16, 8, 128), F32),
         in_specs=[VMEM] * 2,
         out_specs=VMEM,
+        compiler_params=pltpu.CompilerParams(vmem_limit_bytes=8 << 20),
         name="forward",
     )(one_in, two_out)
     two_in = lax.all_to_all(two_out, AXES, 0, 0, tiled=True, axis_index_groups=odd_groups(nx, ny, nz))
@@ -369,17 +399,18 @@
     return call(
         functools.partial(last_kernel, nx, ny, nz),
         out_shape=shape((8, 16, 128), F32),
-        in_specs=[VMEM] * 10,
+        in_specs=[VMEM] * 11,
         out_specs=VMEM,
         scratch_shapes=[fine] * 4 + [middle] * 4 + [coarse] * 4
         + [pltpu.VMEM((4, 16, 128), F32), pltpu.VMEM((2, 8, 128), F32)],
+        compiler_params=pltpu.CompilerParams(vmem_limit_bytes=8 << 20),
         name="last",
-    )(*own, x_in, one_in, two_in, plane)
+    )(*own, a_in, b_in, one_in, two_in, s_in)
 
 
 def solution(mesh):
     nx, ny, nz = (mesh.shape[a] for a in AXES)
     spec = P(*AXES)
-    return jax.shard_map(
-        functools.partial(per_device, nx, ny, nz), mesh=mesh, in_specs=(spec, spec), out_specs=spec, check_vma=False
-    )
+    body = functools.partial(per_device, nx, ny, nz)
+
+    return jax.shard_map(body, mesh=mesh, in_specs=(spec, spec), out_specs=spec, check_vma=False)

time: 85.3 us -> 57.8 us (0.68)
  the two profiles are of different devices: /device:TPU:1 before, /device:TPU:97 now
where the time goes in v2:
time: 57.8 us; the launch traced here: 57.5 us
  starting transfers between devices  26.2 us (45%)
  blocking collectives  21.4 us (37%)
  waiting for transfers between devices  5.19 us (9%)
  Pallas kernels  2.91 us (5%)
  local copies, waits for them, and re-layouts  1.68 us (3%)
    all_to_all x1, starting transfers between devices, per_device(): s_in = lax.all_to_all(s_out, ('gx', 'gy'), 0, 0, tiled=True)  14.7 us
    all_to_all x1, blocking collectives, per_device(): lax.all_to_all(two_out, AXES, 0, 0, tiled=True, axis_index_groups=odd_gro...  14.1 us
    ppermute x1, starting transfers between devices, per_device(): b_in = lax.ppermute(b_out, 'gx', across)  9.17 us
    all_to_all x1, blocking collectives, per_device(): lax.all_to_all(one_out, AXES, 0, 0, tiled=True, axis_index_groups=even_gr...  7.34 us
    ppermute x1, waiting for transfers between devices, per_device(): b_in = lax.ppermute(b_out, 'gx', across)  5.18 us
    ppermute x1, starting transfers between devices, per_device(): a_in = lax.ppermute(a_out, 'gx', near)  2.3 us
    unnamed x4, local copies, waits for them, and re-layouts  1.68 us
    pallas_call x1, Pallas kernels, per_device(): call(functools.partial(last_kernel, nx, ny, nz), out_shape=shape((8, 16,...  1.64 us
  transfers between devices with their start and end apart: 3, of which 1 were waited for; matrix products, arithmetic and copies ran while one was open for 0% of the time, Pallas kernels for 0%

profile of v2, /device:TPU:97, one launch (start us, length us, event | category | flops | bytes accessed | tf_op | source)
XLA Modules:
  0.0 57.5 jit_solution(10592823014906496922)
XLA Ops:
  0.0 0.0 copy-start
  0.0 0.8 %copy-done = f32[8,16,128]{2,1,0:T(8,128)S(1)} copy-done((f32[8,16,128]{2,1,0:T(8,128)S(1)}, f32[8,16,128]{2,1,0:T(8,128)}, u32[]{:S(2)}) %copy-start) | copy-done | bytes 65560
  0.8 0.0 copy-start.1
  0.8 0.8 %copy-done.1 = f32[8,16,128]{2,1,0:T(8,128)S(1)} copy-done((f32[8,16,128]{2,1,0:T(8,128)S(1)}, f32[8,16,128]{2,1,0:T(8,128)}, u32[]{:S(2)}) %copy-start.1) | copy-done | bytes 65560
  1.7 1.1 %first.1 = (f32[14,8,128]{2,1,0:T(8,128)S(1)}, f32[14,8,128]{2,1,0:T(8,128)S(1)}, f32[32,2,128]{2,1,0:T(2,128)}, f32[8,16,128]{2,1,0:T(8,128)S(1)}, f32[8,16,128...) custom-call(f32[8,16,128]{2,1,0:T(8,128)S(1)} %copy-done, ...), custom_call_target="tpu_custom_call" | custom-call | tf_op jit(solution)/shard_map/first/pallas_call | solution.py:364
  2.8 14.7 %all-to-all-start = ((f32[32,2,128]{2,1,0:T(2,128)}), f32[32,2,128]{2,1,0:T(2,128)S(1)}, u32[]{:S(2)}, u32[]{:S(2)}) async-start(f32[32,2,128]{2,1,0:T(2,128)} %get-tuple-element.27), calls=%async_computation | async-start | bytes 65536 | tf_op jit(solution)/shard_map/all_to_all | solution.py:377
  17.5 2.3 %collective-permute-start = (f32[14,8,128]{2,1,0:T(8,128)S(1)}, f32[14,8,128]{2,1,0:T(8,128)S(1)}, u32[]{:S(2)}, u32[]{:S(2)}) collective-permute-start(f32[14,8,128]{2,1,0:T(8,128)S(1)} %get-tuple-element.24), channel_id=1, source_target_pairs={{0,128},{128,0},{256,384},{384,256},{1,129},{129,1},{257,385},{385... | collective-permute-start | bytes 172040 | tf_op jit(solution)/shard_map/ppermute | solution.py:378
  19.8 9.2 %collective-permute-start.1 = (f32[14,8,128]{2,1,0:T(8,128)S(1)}, f32[14,8,128]{2,1,0:T(8,128)S(1)}, u32[]{:S(2)}, u32[]{:S(2)}) collective-permute-start(f32[14,8,128]{2,1,0:T(8,128)S(1)} %get-tuple-element.25), channel_id=1, source_target_pairs={{128,256},{256,128},{129,257},{257,129},{130,258},{258,130},{131,2... | collective-permute-start | bytes 172040 | tf_op jit(solution)/shard_map/ppermute | solution.py:376
  29.0 0.0 collective-permute-done.a_ref.ax_ref
  29.0 5.2 %collective-permute-done.1.b_ref.bx_ref = f32[14,8,128]{2,1,0:T(8,128)S(1)} collective-permute-done((f32[14,8,128]{2,1,0:T(8,128)S(1)}, f32[14,8,128]{2,1,0:T(8,128)S(1)}, u32[]{:S(2)}, u32[]{:S(2)}) %collective-permute-start.1) | collective-permute-done | bytes 57376 | tf_op jit(solution)/shard_map/ppermute | solution.py:376
  34.2 0.2 second.1
  34.4 0.0 all-to-all-done.s_ref
  34.4 7.3 %all_to_all.15.got_ref.one_ref = f32[4,16,8,128]{3,2,1,0:T(8,128)S(1)} all-to-all(f32[4,16,8,128]{3,2,1,0:T(8,128)S(1)} %get-tuple-element.28), channel_id=1, replica_groups={{0,1,16,17},{2,3,18,19},{4,5,20,21},{6,7,22,23},{8,9,24,25},{10,11,26,2..., dimensions={0} | all-to-all | bytes 524288 | tf_op jit(solution)/shard_map/all_to_all | solution.py:388
  41.7 14.1 %all_to_all.16.two_ref = f32[4,16,8,128]{3,2,1,0:T(8,128)S(1)} all-to-all(f32[4,16,8,128]{3,2,1,0:T(8,128)S(1)} %forward.1), channel_id=1, replica_groups={{17,18,33,34},{19,20,35,36},{21,22,37,38},{23,24,39,40},{25,26,41,42},{..., dimensions={0} | all-to-all | bytes 524288 | tf_op jit(solution)/shard_map/all_to_all | solution.py:397
  55.9 1.6 %last.1 = f32[8,16,128]{2,1,0:T(8,128)} custom-call(f32[8,16,128]{2,1,0:T(8,128)S(1)} %get-tuple-element.18.v_ref, f32[8,16,128]{2,1,0:T(8,128)S(1)} %get-tuple-element.19.w_ref, f32[4,8,128]{2,1,0:T(8,128)S(1)} %get-tuple-element.20.v1_ref, f32[4,8,128]{2,1,0:T(8,128)S(1)} %get-tuple-element.21.w1_ref, f32[2,8,128]{2,1,0:T(8,128)S(1)} %get-tuple-element.22.v2_ref, ...), custom_call_target="tpu_custom_call" | custom-call | tf_op jit(solution)/shard_map/last/pallas_call | solution.py:399
  (1 shorter events, 0.0 us)
Async XLA Ops:
  0.0 0.8 %copy-start = (f32[8,16,128]{2,1,0:T(8,128)S(1)}, f32[8,16,128]{2,1,0:T(8,128)}, u32[]{:S(2)}) copy-start(f32[8,16,128]{2,1,0:T(8,128)} %r_ref.1) | copy-start | bytes 196612
  0.8 0.8 %copy-start.1 = (f32[8,16,128]{2,1,0:T(8,128)S(1)}, f32[8,16,128]{2,1,0:T(8,128)}, u32[]{:S(2)}) copy-start(f32[8,16,128]{2,1,0:T(8,128)} %c_ref.1) | copy-start | bytes 196612
  2.8 31.6 %all-to-all-start = ((f32[32,2,128]{2,1,0:T(2,128)}), f32[32,2,128]{2,1,0:T(2,128)S(1)}, u32[]{:S(2)}, u32[]{:S(2)}) async-start(f32[32,2,128]{2,1,0:T(2,128)} %get-tuple-element.27), calls=%async_computation | async-start | bytes 65536 | tf_op jit(solution)/shard_map/all_to_all | solution.py:377
  17.5 11.5 %collective-permute-start = (f32[14,8,128]{2,1,0:T(8,128)S(1)}, f32[14,8,128]{2,1,0:T(8,128)S(1)}, u32[]{:S(2)}, u32[]{:S(2)}) collective-permute-start(f32[14,8,128]{2,1,0:T(8,128)S(1)} %get-tuple-element.24), channel_id=1, source_target_pairs={{0,128},{128,0},{256,384},{384,256},{1,129},{129,1},{257,385},{385... | collective-permute-start | bytes 172040 | tf_op jit(solution)/shard_map/ppermute | solution.py:378
  19.8 14.4 %collective-permute-start.1 = (f32[14,8,128]{2,1,0:T(8,128)S(1)}, f32[14,8,128]{2,1,0:T(8,128)S(1)}, u32[]{:S(2)}, u32[]{:S(2)}) collective-permute-start(f32[14,8,128]{2,1,0:T(8,128)S(1)} %get-tuple-element.25), channel_id=1, source_target_pairs={{128,256},{256,128},{129,257},{257,129},{130,258},{258,130},{131,2... | collective-permute-start | bytes 172040 | tf_op jit(solution)/shard_map/ppermute | solution.py:376

commit v3 on v2

--- a/solution.py
+++ b/solution.py
@@ -1,5 +1,4 @@
 import functools
-import itertools
 
 import jax
 import jax.numpy as jnp
@@ -16,33 +15,6 @@
 VMEM = pl.BlockSpec(memory_space=pltpu.VMEM)
 HIGHEST = lax.Precision.HIGHEST
 AXES = ("gx", "gy", "gz")
-
-
-def even_groups(nx, ny, nz):
-    groups = []
-    for gx, ya, za in itertools.product(range(nx), range(0, ny, 2), range(0, nz, 2)):
-        groups.append([(gx * ny + ya + a) * nz + za + b for a in (0, 1) for b in (0, 1)])
-    return groups
-
-
-def odd_groups(nx, ny, nz):
-    groups = []
-    for gx in range(nx):
-        flat = lambda gy, gz: (gx * ny + gy) * nz + gz % nz
-        for ya, za in itertools.product(range(1, ny - 1, 2), range(1, nz, 2)):
-            groups.append([flat(ya + a, za + b) for a in (0, 1) for b in (0, 1)])
-        for gy, za in itertools.product((0, ny - 1), range(1, nz, 4)):
-            groups.append([flat(gy, za + 2 * a + b) for a in (0, 1) for b in (0, 1)])
-    return groups
-
-
-def spots(ny, nz):
-    gx, gy, gz = (lax.axis_index(a) for a in AXES)
-    one = 2 * (gy & 1) + (gz & 1)
-    inner = (gy > 0) & (gy < ny - 1)
-    half = jnp.where(inner, (gy + 1) & 1, ((gz + nz - 1) & (nz - 1)) // 2 & 1)
-    two = 2 * half + ((gz + 1) & 1)
-    return gx, gy, gz, one, two, inner
 
 
 def lanes(shape=(8, 128)):
@@ -181,20 +153,16 @@
     return packed
 
 
-def second_kernel(ny, nz, v_ref, w_ref, v1_ref, w1_ref, v2_ref, w2_ref, a_ref, b_ref, one_ref, two_ref):
-    gx, gy, _, one, two, _ = spots(ny, nz)
+def second_kernel(v_ref, w_ref, v1_ref, w1_ref, v2_ref, w2_ref, a_ref, b_ref, z_ref, ya_ref, yb_ref):
+    gx, gy = lax.axis_index("gx"), lax.axis_index("gy")
     level0, level1, level2 = extended(gx, v_ref, w_ref, v1_ref, w1_ref, v2_ref, w2_ref, a_ref, b_ref)
     lane, row = lanes(), rows()
     low = lane < 64
     quad = (lane & 63) < 32
     up = (gy & 1) == 0
-    ends = [edge_lanes(level0[1:13])]
-    ends = [ends[0][0:8], ends[0][8:16], edge_lanes(level1[1:9]), edge_lanes(level2[1:7])]
-    for i, tile in enumerate(ends):
-        for slot in (one ^ 1, one ^ 2, one ^ 3):
-            one_ref[slot, 12 + i] = tile
-        for slot in (two ^ 1, two ^ 3):
-            two_ref[slot, i] = tile
+    ends = edge_lanes(level0[1:13])
+    for i, tile in enumerate((ends[0:8], ends[8:16], edge_lanes(level1[1:9]), edge_lanes(level2[1:7]))):
+        z_ref[i] = tile
     for k in range(12):
         v, w = level0[k + 1]
         if k < 8:
@@ -207,16 +175,26 @@
             extra = jnp.zeros((8, 128), F32)
         high = jnp.where(row >= 5, v[8:16], jnp.where(row >= 3, turn(w[8:16], 5, 0), turn(extra, 3, 0)))
         base = jnp.where(row < 3, v[0:8], jnp.where(row < 5, turn(w[0:8], 3, 0), turn(extra, 5, 0)))
-        one_ref[one ^ 2, k] = jnp.where(up, high, base)
-        two_ref[two ^ 2, k] = jnp.where(up, base, high)
-
-
-def forward_kernel(ny, nz, got_ref, old_ref, two_ref):
-    _, _, _, one, two, _ = spots(ny, nz)
-    two_ref[...] = old_ref[...]
+        ya_ref[k] = jnp.where(up, high, base)
+        yb_ref[k] = jnp.where(up, base, high)
+
+
+def both_ends(i, za_ref, zb_ref):
+    lane = lanes()
+    part = lane - 10 * (lane // 10)
+    ahead = (lax.axis_index("gz") & 1) == 0
+    last = (part < 3) | ((part >= 6) & (part < 8))
+    from_a = jnp.where(ahead, jnp.where(last, 0, 1), jnp.where(last, 1, 0)) == 1
+    return jnp.where(from_a, za_ref[i], zb_ref[i])
+
+
+def third_kernel(za_ref, zb_ref, ya_ref, yb_ref, ya_out, yb_out):
+    ya_out[0:12] = ya_ref[...]
+    yb_out[0:12] = yb_ref[...]
     for i in range(4):
-        two_ref[two ^ 2, 12 + i] = got_ref[one ^ 1, 12 + i]
-        two_ref[two ^ 1, 12 + i] = got_ref[one ^ 2, 12 + i]
+        ends = both_ends(i, za_ref, zb_ref)
+        ya_out[12 + i] = ends
+        yb_out[12 + i] = ends
 
 
 def around(v, above, below):
@@ -246,13 +224,11 @@
 
 
 def last_kernel(
-    nx, ny, nz, v_ref, w_ref, v1_ref, w1_ref, v2_ref, w2_ref, ax_ref, bx_ref, one_ref, two_ref, s_ref, out_ref,
+    nx, ny, v_ref, w_ref, v1_ref, w1_ref, v2_ref, w2_ref, ax_ref, bx_ref, za_ref, zb_ref, ya_ref, yb_ref, s_ref, out_ref,
     fv, fw, fa, fb, mv, mw, ma, mb, cv, cw, ca, cb, wide_ref, deep_ref,
 ):
-    gx, gy, gz, one, two, has_y = spots(ny, nz)
-    has_z = (gz > 0) & (gz < nz - 1)
+    gx, gy = lax.axis_index("gx"), lax.axis_index("gy")
     up = (gy & 1) == 0
-    ahead = (gz & 1) == 0
     lane, row = lanes(), rows()
 
     def far(slot, have):
@@ -266,20 +242,13 @@
     level0, level1, level2 = extended(
         gx, v_ref, w_ref, v1_ref, w1_ref, v2_ref, w2_ref, ax_ref, bx_ref, outer_layers
     )
-    part = lane - 10 * (lane // 10)
-    first_half = (part < 3) | ((part >= 6) & (part < 8))
-    from_one = jnp.where(ahead, jnp.where(first_half, 0, 1), jnp.where(first_half, 1, 0)) == 1
-
-    own, plus, minus = [], [], []
-    for i in range(4):
-        z_two = jnp.where(has_z, two_ref[two ^ 1, i], 0.0)
-        own.append(jnp.where(from_one, one_ref[one ^ 1, 12 + i], z_two))
-        z_two = jnp.where(has_z, two_ref[two ^ 1, 12 + i], 0.0)
-        t_one = jnp.where(from_one, one_ref[one ^ 3, 12 + i], z_two)
-        z_two = jnp.where(has_z, two_ref[two ^ 3, i], 0.0)
-        t_two = jnp.where(has_y, jnp.where(from_one, two_ref[two ^ 2, 12 + i], z_two), 0.0)
-        plus.append(jnp.where(up, t_one, t_two))
-        minus.append(jnp.where(up, t_two, t_one))
+
+    def sides(k):
+        a, b = ya_ref[k], yb_ref[k]
+        return jnp.where(up, a, b), jnp.where(up, b, a)
+
+    own = [both_ends(i, za_ref, zb_ref) for i in range(4)]
+    plus, minus = zip(*(sides(12 + i) for i in range(4)))
     none = jnp.zeros((8, 128), F32)
 
     def outer(p, m):
@@ -296,9 +265,7 @@
         fv[i, 16:24, 0:128] = none
         fv[i, :, 128:256] = jnp.zeros((24, 128), F32)
     for k in range(12):
-        a = one_ref[one ^ 2, k]
-        b = jnp.where(has_y, two_ref[two ^ 2, k], 0.0)
-        p, m = jnp.where(up, a, b), jnp.where(up, b, a)
+        p, m = sides(k)
         v, w = level0[k + 1]
         fv[k + 1, 0:16, 0:128] = v
         fw[k + 1, 0:16, 0:128] = w
@@ -371,41 +338,43 @@
         compiler_params=pltpu.CompilerParams(vmem_limit_bytes=8 << 20),
         name="first",
     )(right_side, coefficient)
-    near = [(i, i ^ 1) for i in range(nx)]
-    across = [(i, i + 1 if i & 1 else i - 1) for i in range(1, nx - 1)]
-    b_in = lax.ppermute(b_out, "gx", across)
+    even = lambda n: [(i, i ^ 1) for i in range(n)]
+    odd = lambda n: [(i, i + 1 if i & 1 else i - 1) for i in range(1, n - 1)]
+    b_in = lax.ppermute(b_out, "gx", odd(nx))
     s_in = lax.all_to_all(s_out, ("gx", "gy"), 0, 0, tiled=True)
-    a_in = lax.ppermute(a_out, "gx", near)
-    one_out, two_out = call(
-        functools.partial(second_kernel, ny, nz),
-        out_shape=[shape((4, 16, 8, 128), F32)] * 2,
+    a_in = lax.ppermute(a_out, "gx", even(nx))
+    limit = pltpu.CompilerParams(vmem_limit_bytes=8 << 20)
+    z_out, ya_own, yb_own = call(
+        second_kernel,
+        out_shape=[shape((4, 8, 128), F32)] + [shape((12, 8, 128), F32)] * 2,
         in_specs=[VMEM] * 8,
-        out_specs=[VMEM] * 2,
-        compiler_params=pltpu.CompilerParams(vmem_limit_bytes=8 << 20),
+        out_specs=[VMEM] * 3,
+        compiler_params=limit,
         name="second",
     )(*own, a_in, b_in)
-    one_out, s_in = lax.optimization_barrier((one_out, s_in))
-    one_in = lax.all_to_all(one_out, AXES, 0, 0, tiled=True, axis_index_groups=even_groups(nx, ny, nz))
-    two_out = call(
-        functools.partial(forward_kernel, ny, nz),
-        out_shape=shape((4, 16, 8, 128), F32),
-        in_specs=[VMEM] * 2,
-        out_specs=VMEM,
-        compiler_params=pltpu.CompilerParams(vmem_limit_bytes=8 << 20),
-        name="forward",
-    )(one_in, two_out)
-    two_in = lax.all_to_all(two_out, AXES, 0, 0, tiled=True, axis_index_groups=odd_groups(nx, ny, nz))
+    zb_in = lax.ppermute(z_out, "gz", odd(nz))
+    za_in = lax.ppermute(z_out, "gz", even(nz))
+    ya_out, yb_out = call(
+        third_kernel,
+        out_shape=[shape((16, 8, 128), F32)] * 2,
+        in_specs=[VMEM] * 4,
+        out_specs=[VMEM] * 2,
+        compiler_params=limit,
+        name="third",
+    )(za_in, zb_in, ya_own, yb_own)
+    yb_in = lax.ppermute(yb_out, "gy", odd(ny))
+    ya_in = lax.ppermute(ya_out, "gy", even(ny))
     fine, middle, coarse = (pltpu.VMEM(s, F32) for s in ((14, 24, 256), (10, 16, 128), (8, 16, 128)))
     return call(
-        functools.partial(last_kernel, nx, ny, nz),
+        functools.partial(last_kernel, nx, ny),
         out_shape=shape((8, 16, 128), F32),
-        in_specs=[VMEM] * 11,
+        in_specs=[VMEM] * 13,
         out_specs=VMEM,
         scratch_shapes=[fine] * 4 + [middle] * 4 + [coarse] * 4
         + [pltpu.VMEM((4, 16, 128), F32), pltpu.VMEM((2, 8, 128), F32)],
         compiler_params=pltpu.CompilerParams(vmem_limit_bytes=8 << 20),
         name="last",
-    )(*own, a_in, b_in, one_in, two_in, s_in)
+    )(*own, a_in, b_in, za_in, zb_in, ya_in, yb_in, s_in)
 
 
 def solution(mesh):

time: 57.8 us -> 47.9 us (0.83)
  the two profiles are of different devices: /device:TPU:97 before, /device:TPU:134 now
where the time goes in v3:
time: 47.9 us; the launch traced here: 47.5 us
  starting transfers between devices  33.7 us (70%)
  waiting for transfers between devices  9.14 us (19%)
  Pallas kernels  2.91 us (6%)
  local copies, waits for them, and re-layouts  1.68 us (4%)
    all_to_all x1, starting transfers between devices, per_device(): s_in = lax.all_to_all(s_out, ('gx', 'gy'), 0, 0, tiled=True)  18.7 us
    ppermute x1, starting transfers between devices, per_device(): zb_in = lax.ppermute(z_out, 'gz', odd(nz))  5.19 us
    ppermute x1, waiting for transfers between devices, per_device(): yb_in = lax.ppermute(yb_out, 'gy', odd(ny))  4.59 us
    ppermute x1, starting transfers between devices, per_device(): ya_in = lax.ppermute(ya_out, 'gy', even(ny))  3.37 us
    ppermute x1, waiting for transfers between devices, per_device(): za_in = lax.ppermute(z_out, 'gz', even(nz))  3.09 us
    ppermute x1, starting transfers between devices, per_device(): a_in = lax.ppermute(a_out, 'gx', even(nx))  1.92 us
    ppermute x1, starting transfers between devices, per_device(): za_in = lax.ppermute(z_out, 'gz', even(nz))  1.92 us
    ppermute x1, starting transfers between devices, per_device(): yb_in = lax.ppermute(yb_out, 'gy', odd(ny))  1.92 us
  transfers between devices with their start and end apart: 7, of which 4 were waited for; matrix products, arithmetic and copies ran while one was open for 0% of the time, Pallas kernels for 0%

profile of v3, /device:TPU:134, one launch (start us, length us, event | category | flops | bytes accessed | tf_op | source)
XLA Modules:
  0.0 47.5 jit_solution(13639452660981928853)
XLA Ops:
  0.0 0.0 copy-start
  0.0 0.8 %copy-done = f32[8,16,128]{2,1,0:T(8,128)S(1)} copy-done((f32[8,16,128]{2,1,0:T(8,128)S(1)}, f32[8,16,128]{2,1,0:T(8,128)}, u32[]{:S(2)}) %copy-start) | copy-done | bytes 65560
  0.8 0.0 copy-start.1
  0.8 0.8 %copy-done.1 = f32[8,16,128]{2,1,0:T(8,128)S(1)} copy-done((f32[8,16,128]{2,1,0:T(8,128)S(1)}, f32[8,16,128]{2,1,0:T(8,128)}, u32[]{:S(2)}) %copy-start.1) | copy-done | bytes 65560
  1.7 1.1 %first.1 = (f32[14,8,128]{2,1,0:T(8,128)S(1)}, f32[14,8,128]{2,1,0:T(8,128)S(1)}, f32[32,2,128]{2,1,0:T(2,128)}, f32[8,16,128]{2,1,0:T(8,128)S(1)}, f32[8,16,128...) custom-call(f32[8,16,128]{2,1,0:T(8,128)S(1)} %copy-done, ...), custom_call_target="tpu_custom_call" | custom-call | tf_op jit(solution)/shard_map/first/pallas_call | solution.py:331
  2.8 1.9 %collective-permute-start = (f32[14,8,128]{2,1,0:T(8,128)S(1)}, f32[14,8,128]{2,1,0:T(8,128)S(1)}, u32[]{:S(2)}, u32[]{:S(2)}) collective-permute-start(f32[14,8,128]{2,1,0:T(8,128)S(1)} %get-tuple-element.25), channel_id=1, source_target_pairs={{0,128},{128,0},{256,384},{384,256},{1,129},{129,1},{257,385},{385... | collective-permute-start | bytes 172040 | tf_op jit(solution)/shard_map/ppermute | solution.py:345
  4.7 0.7 %collective-permute-start.1 = (f32[14,8,128]{2,1,0:T(8,128)S(1)}, f32[14,8,128]{2,1,0:T(8,128)S(1)}, u32[]{:S(2)}, u32[]{:S(2)}) collective-permute-start(f32[14,8,128]{2,1,0:T(8,128)S(1)} %get-tuple-element.26), channel_id=1, source_target_pairs={{128,256},{256,128},{129,257},{257,129},{130,258},{258,130},{131,2... | collective-permute-start | bytes 172040 | tf_op jit(solution)/shard_map/ppermute | solution.py:343
  5.4 18.7 %all-to-all-start = ((f32[32,2,128]{2,1,0:T(2,128)}), f32[32,2,128]{2,1,0:T(2,128)S(1)}, u32[]{:S(2)}, u32[]{:S(2)}) async-start(f32[32,2,128]{2,1,0:T(2,128)} %get-tuple-element.32), calls=%async_computation | async-start | bytes 65536 | tf_op jit(solution)/shard_map/all_to_all | solution.py:344
  24.1 0.0 collective-permute-done.a_ref.ax_ref
  24.1 0.0 collective-permute-done.1.b_ref.bx_ref
  24.1 0.2 second.1
  24.3 5.2 %collective-permute-start.3 = (f32[4,8,128]{2,1,0:T(8,128)S(1)}, f32[4,8,128]{2,1,0:T(8,128)S(1)}, u32[]{:S(2)}, u32[]{:S(2)}) collective-permute-start(f32[4,8,128]{2,1,0:T(8,128)S(1)} %get-tuple-element.27), channel_id=1, source_target_pairs={{1,2},{2,1},{3,4},{4,3},{5,6},{6,5},{7,8},{8,7},{9,10},{10,9},{11,... | collective-permute-start | bytes 49160 | tf_op jit(solution)/shard_map/ppermute | solution.py:355
  29.5 1.9 %collective-permute-start.2 = (f32[4,8,128]{2,1,0:T(8,128)S(1)}, f32[4,8,128]{2,1,0:T(8,128)S(1)}, u32[]{:S(2)}, u32[]{:S(2)}) collective-permute-start(f32[4,8,128]{2,1,0:T(8,128)S(1)} %get-tuple-element.27), channel_id=1, source_target_pairs={{0,1},{1,0},{2,3},{3,2},{4,5},{5,4},{6,7},{7,6},{8,9},{9,8},{10,11... | collective-permute-start | bytes 49160 | tf_op jit(solution)/shard_map/ppermute | solution.py:356
  31.4 0.6 %collective-permute-done.3.zb_ref = f32[4,8,128]{2,1,0:T(8,128)S(1)} collective-permute-done((f32[4,8,128]{2,1,0:T(8,128)S(1)}, f32[4,8,128]{2,1,0:T(8,128)S(1)}, u32[]{:S(2)}, u32[]{:S(2)}) %collective-permute-start.3) | collective-permute-done | bytes 16416 | tf_op jit(solution)/shard_map/ppermute | solution.py:355
  32.0 3.1 %collective-permute-done.2.za_ref = f32[4,8,128]{2,1,0:T(8,128)S(1)} collective-permute-done((f32[4,8,128]{2,1,0:T(8,128)S(1)}, f32[4,8,128]{2,1,0:T(8,128)S(1)}, u32[]{:S(2)}, u32[]{:S(2)}) %collective-permute-start.2) | collective-permute-done | bytes 16416 | tf_op jit(solution)/shard_map/ppermute | solution.py:356
  35.1 3.4 %collective-permute-start.4 = (f32[16,8,128]{2,1,0:T(8,128)S(1)}, f32[16,8,128]{2,1,0:T(8,128)S(1)}, u32[]{:S(2)}, u32[]{:S(2)}) collective-permute-start(f32[16,8,128]{2,1,0:T(8,128)S(1)} %get-tuple-element.30), channel_id=1, source_target_pairs={{0,16},{16,0},{32,48},{48,32},{64,80},{80,64},{96,112},{112,96},{1... | collective-permute-start | bytes 196616 | tf_op jit(solution)/shard_map/ppermute | solution.py:366
  38.5 1.9 %collective-permute-start.5 = (f32[16,8,128]{2,1,0:T(8,128)S(1)}, f32[16,8,128]{2,1,0:T(8,128)S(1)}, u32[]{:S(2)}, u32[]{:S(2)}) collective-permute-start(f32[16,8,128]{2,1,0:T(8,128)S(1)} %get-tuple-element.31), channel_id=1, source_target_pairs={{16,32},{32,16},{48,64},{64,48},{80,96},{96,80},{17,33},{33,17},{4... | collective-permute-start | bytes 196616 | tf_op jit(solution)/shard_map/ppermute | solution.py:365
  40.4 0.0 all-to-all-done.s_ref
  40.5 0.8 %collective-permute-done.4.ya_ref = f32[16,8,128]{2,1,0:T(8,128)S(1)} collective-permute-done((f32[16,8,128]{2,1,0:T(8,128)S(1)}, f32[16,8,128]{2,1,0:T(8,128)S(1)}, u32[]{:S(2)}, u32[]{:S(2)}) %collective-permute-start.4) | collective-permute-done | bytes 65568 | tf_op jit(solution)/shard_map/ppermute | solution.py:366
  41.3 4.6 %collective-permute-done.5.yb_ref = f32[16,8,128]{2,1,0:T(8,128)S(1)} collective-permute-done((f32[16,8,128]{2,1,0:T(8,128)S(1)}, f32[16,8,128]{2,1,0:T(8,128)S(1)}, u32[]{:S(2)}, u32[]{:S(2)}) %collective-permute-start.5) | collective-permute-done | bytes 65568 | tf_op jit(solution)/shard_map/ppermute | solution.py:365
  45.9 1.6 %last.1 = f32[8,16,128]{2,1,0:T(8,128)} custom-call(f32[8,16,128]{2,1,0:T(8,128)S(1)} %get-tuple-element.19.v_ref, f32[8,16,128]{2,1,0:T(8,128)S(1)} %get-tuple-element.20.w_ref, f32[4,8,128]{2,1,0:T(8,128)S(1)} %get-tuple-element.21.v1_ref, f32[4,8,128]{2,1,0:T(8,128)S(1)} %get-tuple-element.22.w1_ref, f32[2,8,128]{2,1,0:T(8,128)S(1)} %get-tuple-element.23.v2_ref, ...), custom_call_target="tpu_custom_call" | custom-call | tf_op jit(solution)/shard_map/last/pallas_call | solution.py:368
  (1 shorter events, 0.0 us)
Async XLA Ops:
  0.0 0.8 %copy-start = (f32[8,16,128]{2,1,0:T(8,128)S(1)}, f32[8,16,128]{2,1,0:T(8,128)}, u32[]{:S(2)}) copy-start(f32[8,16,128]{2,1,0:T(8,128)} %r_ref.1) | copy-start | bytes 196612
  0.8 0.8 %copy-start.1 = (f32[8,16,128]{2,1,0:T(8,128)S(1)}, f32[8,16,128]{2,1,0:T(8,128)}, u32[]{:S(2)}) copy-start(f32[8,16,128]{2,1,0:T(8,128)} %c_ref.1) | copy-start | bytes 196612
  2.8 21.3 %collective-permute-start = (f32[14,8,128]{2,1,0:T(8,128)S(1)}, f32[14,8,128]{2,1,0:T(8,128)S(1)}, u32[]{:S(2)}, u32[]{:S(2)}) collective-permute-start(f32[14,8,128]{2,1,0:T(8,128)S(1)} %get-tuple-element.25), channel_id=1, source_target_pairs={{0,128},{128,0},{256,384},{384,256},{1,129},{129,1},{257,385},{385... | collective-permute-start | bytes 172040 | tf_op jit(solution)/shard_map/ppermute | solution.py:345
  4.7 19.4 %collective-permute-start.1 = (f32[14,8,128]{2,1,0:T(8,128)S(1)}, f32[14,8,128]{2,1,0:T(8,128)S(1)}, u32[]{:S(2)}, u32[]{:S(2)}) collective-permute-start(f32[14,8,128]{2,1,0:T(8,128)S(1)} %get-tuple-element.26), channel_id=1, source_target_pairs={{128,256},{256,128},{129,257},{257,129},{130,258},{258,130},{131,2... | collective-permute-start | bytes 172040 | tf_op jit(solution)/shard_map/ppermute | solution.py:343
  5.4 35.1 %all-to-all-start = ((f32[32,2,128]{2,1,0:T(2,128)}), f32[32,2,128]{2,1,0:T(2,128)S(1)}, u32[]{:S(2)}, u32[]{:S(2)}) async-start(f32[32,2,128]{2,1,0:T(2,128)} %get-tuple-element.32), calls=%async_computation | async-start | bytes 65536 | tf_op jit(solution)/shard_map/all_to_all | solution.py:344
  24.3 7.7 %collective-permute-start.3 = (f32[4,8,128]{2,1,0:T(8,128)S(1)}, f32[4,8,128]{2,1,0:T(8,128)S(1)}, u32[]{:S(2)}, u32[]{:S(2)}) collective-permute-start(f32[4,8,128]{2,1,0:T(8,128)S(1)} %get-tuple-element.27), channel_id=1, source_target_pairs={{1,2},{2,1},{3,4},{4,3},{5,6},{6,5},{7,8},{8,7},{9,10},{10,9},{11,... | collective-permute-start | bytes 49160 | tf_op jit(solution)/shard_map/ppermute | solution.py:355
  29.5 5.6 %collective-permute-start.2 = (f32[4,8,128]{2,1,0:T(8,128)S(1)}, f32[4,8,128]{2,1,0:T(8,128)S(1)}, u32[]{:S(2)}, u32[]{:S(2)}) collective-permute-start(f32[4,8,128]{2,1,0:T(8,128)S(1)} %get-tuple-element.27), channel_id=1, source_target_pairs={{0,1},{1,0},{2,3},{3,2},{4,5},{5,4},{6,7},{7,6},{8,9},{9,8},{10,11... | collective-permute-start | bytes 49160 | tf_op jit(solution)/shard_map/ppermute | solution.py:356
  35.1 6.2 %collective-permute-start.4 = (f32[16,8,128]{2,1,0:T(8,128)S(1)}, f32[16,8,128]{2,1,0:T(8,128)S(1)}, u32[]{:S(2)}, u32[]{:S(2)}) collective-permute-start(f32[16,8,128]{2,1,0:T(8,128)S(1)} %get-tuple-element.30), channel_id=1, source_target_pairs={{0,16},{16,0},{32,48},{48,32},{64,80},{80,64},{96,112},{112,96},{1... | collective-permute-start | bytes 196616 | tf_op jit(solution)/shard_map/ppermute | solution.py:366
  38.5 7.4 %collective-permute-start.5 = (f32[16,8,128]{2,1,0:T(8,128)S(1)}, f32[16,8,128]{2,1,0:T(8,128)S(1)}, u32[]{:S(2)}, u32[]{:S(2)}) collective-permute-start(f32[16,8,128]{2,1,0:T(8,128)S(1)} %get-tuple-element.31), channel_id=1, source_target_pairs={{16,32},{32,16},{48,64},{64,48},{80,96},{96,80},{17,33},{33,17},{4... | collective-permute-start | bytes 196616 | tf_op jit(solution)/shard_map/ppermute | solution.py:365

commit v4 on v3

--- a/solution.py
+++ b/solution.py
@@ -31,18 +31,10 @@
 
 
 def first_kernel(
-    nx, ny, r_ref, c_ref, a_ref, b_ref, s_ref, v_ref, w_ref, v1_ref, w1_ref, v2_ref, w2_ref, t_ref, u_ref, d_ref,
-    rv_ref, cv_ref, sems,
+    nx, ny, in_ref, a_ref, b_ref, s_ref, v_ref, w_ref, v1_ref, w1_ref, v2_ref, w2_ref, t_ref, u_ref, d_ref,
 ):
     gx = lax.axis_index("gx")
-    fetches = [
-        pltpu.make_async_copy(src, dst, sems.at[i]) for i, (src, dst) in enumerate(((r_ref, rv_ref), (c_ref, cv_ref)))
-    ]
-    for fetch in fetches:
-        fetch.start()
-    for fetch in fetches:
-        fetch.wait()
-    r, c = rv_ref[...], cv_ref[...]
+    r, c = in_ref[0], in_ref[1]
     w = RELAX / (6.0 + c)
     v = w * r
     v_ref[...] = v
@@ -98,13 +90,14 @@
         x_ref[13] = last
 
 
-def extended(gx, v_ref, w_ref, v1_ref, w1_ref, v2_ref, w2_ref, a_ref, b_ref, far=(None, None)):
+def extended(gx, v_ref, w_ref, v1_ref, w1_ref, v2_ref, w2_ref, al_ref, ah_ref, b_ref, far=(None, None)):
     lane, row = lanes(), rows()
     low = lane < 64
     quad = (lane & 63) < 32
     even = (gx & 1) == 0
-    left = lambda tile: jnp.where(even, b_ref[tile], a_ref[tile])
-    right = lambda tile: jnp.where(even, a_ref[tile], b_ref[tile])
+    near = lambda tile: al_ref[tile] + ah_ref[tile]
+    left = lambda tile: jnp.where(even, b_ref[tile], near(tile))
+    right = lambda tile: jnp.where(even, near(tile), b_ref[tile])
 
     def pair(side, tile):
         return jnp.concatenate([side(tile), side(tile + 1)], axis=0)
@@ -153,9 +146,9 @@
     return packed
 
 
-def second_kernel(v_ref, w_ref, v1_ref, w1_ref, v2_ref, w2_ref, a_ref, b_ref, z_ref, ya_ref, yb_ref):
+def second_kernel(v_ref, w_ref, v1_ref, w1_ref, v2_ref, w2_ref, al_ref, ah_ref, b_ref, z_ref, ya_ref, yb_ref):
     gx, gy = lax.axis_index("gx"), lax.axis_index("gy")
-    level0, level1, level2 = extended(gx, v_ref, w_ref, v1_ref, w1_ref, v2_ref, w2_ref, a_ref, b_ref)
+    level0, level1, level2 = extended(gx, v_ref, w_ref, v1_ref, w1_ref, v2_ref, w2_ref, al_ref, ah_ref, b_ref)
     lane, row = lanes(), rows()
     low = lane < 64
     quad = (lane & 63) < 32
@@ -224,7 +217,7 @@
 
 
 def last_kernel(
-    nx, ny, v_ref, w_ref, v1_ref, w1_ref, v2_ref, w2_ref, ax_ref, bx_ref, za_ref, zb_ref, ya_ref, yb_ref, s_ref, out_ref,
+    nx, ny, v_ref, w_ref, v1_ref, w1_ref, v2_ref, w2_ref, al_ref, ah_ref, b_ref, za_ref, zb_ref, ya_ref, yb_ref, s_ref, out_ref,
     fv, fw, fa, fb, mv, mw, ma, mb, cv, cw, ca, cb, wide_ref, deep_ref,
 ):
     gx, gy = lax.axis_index("gx"), lax.axis_index("gy")
@@ -240,7 +233,7 @@
 
     outer_layers = far(jnp.maximum(gx - 2, 0), gx > 1), far(jnp.minimum(gx + 2, nx - 1), gx < nx - 2)
     level0, level1, level2 = extended(
-        gx, v_ref, w_ref, v1_ref, w1_ref, v2_ref, w2_ref, ax_ref, bx_ref, outer_layers
+        gx, v_ref, w_ref, v1_ref, w1_ref, v2_ref, w2_ref, al_ref, ah_ref, b_ref, outer_layers
     )
 
     def sides(k):
@@ -331,27 +324,27 @@
     a_out, b_out, s_out, *own = call(
         functools.partial(first_kernel, nx, ny),
         out_shape=[shape((14, 8, 128), F32)] * 2 + [shape((nx * ny, 2, 128), F32)] + kept,
-        in_specs=[pl.BlockSpec(memory_space=pltpu.HBM)] * 2,
+        in_specs=[VMEM],
         out_specs=[VMEM] * 9,
-        scratch_shapes=[pltpu.VMEM(s, F32) for s in ((8, 16, 128), (4, 8, 128), (4, 8, 128), (8, 16, 128), (8, 16, 128))]
-        + [pltpu.SemaphoreType.DMA((2,))],
+        scratch_shapes=[pltpu.VMEM(s, F32) for s in ((8, 16, 128), (4, 8, 128), (4, 8, 128))],
         compiler_params=pltpu.CompilerParams(vmem_limit_bytes=8 << 20),
         name="first",
-    )(right_side, coefficient)
+    )(jnp.stack([right_side, coefficient]))
     even = lambda n: [(i, i ^ 1) for i in range(n)]
     odd = lambda n: [(i, i + 1 if i & 1 else i - 1) for i in range(1, n - 1)]
+    al_in = lax.ppermute(a_out, "gx", even(nx)[: nx // 2])
     b_in = lax.ppermute(b_out, "gx", odd(nx))
     s_in = lax.all_to_all(s_out, ("gx", "gy"), 0, 0, tiled=True)
-    a_in = lax.ppermute(a_out, "gx", even(nx))
+    ah_in = lax.ppermute(a_out, "gx", even(nx)[nx // 2 :])
     limit = pltpu.CompilerParams(vmem_limit_bytes=8 << 20)
     z_out, ya_own, yb_own = call(
         second_kernel,
         out_shape=[shape((4, 8, 128), F32)] + [shape((12, 8, 128), F32)] * 2,
-        in_specs=[VMEM] * 8,
+        in_specs=[VMEM] * 9,
         out_specs=[VMEM] * 3,
         compiler_params=limit,
         name="second",
-    )(*own, a_in, b_in)
+    )(*own, al_in, ah_in, b_in)
     zb_in = lax.ppermute(z_out, "gz", odd(nz))
     za_in = lax.ppermute(z_out, "gz", even(nz))
     ya_out, yb_out = call(
@@ -368,13 +361,13 @@
     return call(
         functools.partial(last_kernel, nx, ny),
         out_shape=shape((8, 16, 128), F32),
-        in_specs=[VMEM] * 13,
+        in_specs=[VMEM] * 14,
         out_specs=VMEM,
         scratch_shapes=[fine] * 4 + [middle] * 4 + [coarse] * 4
         + [pltpu.VMEM((4, 16, 128), F32), pltpu.VMEM((2, 8, 128), F32)],
         compiler_params=pltpu.CompilerParams(vmem_limit_bytes=8 << 20),
         name="last",
-    )(*own, a_in, b_in, za_in, zb_in, ya_in, yb_in, s_in)
+    )(*own, al_in, ah_in, b_in, za_in, zb_in, ya_in, yb_in, s_in)
 
 
 def solution(mesh):

time: 47.9 us -> 48 us (level)
  local copies, waits for them, and re-layouts: 1.68 us -> 0 us
  starting transfers between devices: 33.7 us -> 34.7 us
  other arithmetic: 0 us -> 0.88 us
    ppermute x1 -> x2, starting transfers between devices: 1.92 us -> 12.9 us  [the longest x1 12.3 us: per_device(): al_in = lax.ppermute(a_out, 'gx', even(nx)[:nx // 2])]
    all_to_all x1, starting transfers between devices: 18.7 us -> 8.74 us  [per_device(): s_in = lax.all_to_all(s_out, ('gx', 'gy'), 0, 0, tiled=True)]
    unnamed x4 -> x0, local copies, waits for them, and re-layouts: 1.68 us -> none
    another operation x0 -> x1, other arithmetic: none -> 0.88 us  [per_device(): jnp.stack([right_side, coefficient])]
  transfers between devices with their start and end apart: 7 -> 8, of which waited for: 4 -> 4; matrix products, arithmetic and copies ran while one was open for 0% -> 0% of each run, Pallas kernels for 0% -> 0%
where the time goes in v4:
time: 48 us; the launch traced here: 47.6 us
  starting transfers between devices  34.7 us (72%)
  waiting for transfers between devices  9.14 us (19%)
  Pallas kernels  2.75 us (6%)
  other arithmetic  0.88 us (2%)
    ppermute x1, starting transfers between devices, per_device(): al_in = lax.ppermute(a_out, 'gx', even(nx)[:nx // 2])  12.3 us
    all_to_all x1, starting transfers between devices, per_device(): s_in = lax.all_to_all(s_out, ('gx', 'gy'), 0, 0, tiled=True)  8.74 us
    ppermute x1, starting transfers between devices, per_device(): zb_in = lax.ppermute(z_out, 'gz', odd(nz))  5.19 us
    ppermute x1, waiting for transfers between devices, per_device(): yb_in = lax.ppermute(yb_out, 'gy', odd(ny))  4.59 us
    ppermute x1, starting transfers between devices, per_device(): ya_in = lax.ppermute(ya_out, 'gy', even(ny))  3.37 us
    ppermute x1, waiting for transfers between devices, per_device(): za_in = lax.ppermute(z_out, 'gz', even(nz))  3.09 us
    ppermute x1, starting transfers between devices, per_device(): za_in = lax.ppermute(z_out, 'gz', even(nz))  1.92 us
    ppermute x1, starting transfers between devices, per_device(): yb_in = lax.ppermute(yb_out, 'gy', odd(ny))  1.92 us
  transfers between devices with their start and end apart: 8, of which 4 were waited for; matrix products, arithmetic and copies ran while one was open for 0% of the time, Pallas kernels for 0%

profile of v4, /device:TPU:134, one launch (start us, length us, event | category | flops | bytes accessed | tf_op | source)
XLA Modules:
  0.0 47.6 jit_solution(2727240523790416778)
XLA Ops:
  0.0 0.9 %pad_maximum_fusion.in_ref = f32[2,8,16,128]{3,2,1,0:T(8,128)S(1)} fusion(f32[1,8,16,128]{3,2,1,0:T(8,128)} %bitcast.2, f32[1,8,16,128]{3,2,1,0:T(8,128)} %bitcast.3), kind=kLoop, calls=%fused_computation | loop fusion | flops 32768 | bytes 262144 | tf_op jit(solution)/shard_map/stack | solution.py:332
  0.9 0.9 %first.1 = (f32[14,8,128]{2,1,0:T(8,128)S(1)}, f32[14,8,128]{2,1,0:T(8,128)S(1)}, f32[32,2,128]{2,1,0:T(2,128)}, f32[8,16,128]{2,1,0:T(8,128)S(1)}, f32[8,16,128...) custom-call(f32[2,8,16,128]{3,2,1,0:T(8,128)S(1)} %pad_maximum_fusio, ...), custom_call_target="tpu_custom_call" | custom-call | tf_op jit(solution)/shard_map/first/pallas_call | solution.py:324
  1.8 0.7 %collective-permute-start.2 = (f32[14,8,128]{2,1,0:T(8,128)S(1)}, f32[14,8,128]{2,1,0:T(8,128)S(1)}, u32[]{:S(2)}, u32[]{:S(2)}) collective-permute-start(f32[14,8,128]{2,1,0:T(8,128)S(1)} %get-tuple-element.26), channel_id=1, source_target_pairs={{128,256},{256,128},{129,257},{257,129},{130,258},{258,130},{131,2... | collective-permute-start | bytes 172040 | tf_op jit(solution)/shard_map/ppermute | solution.py:336
  2.5 0.7 %collective-permute-start.1 = (f32[14,8,128]{2,1,0:T(8,128)S(1)}, f32[14,8,128]{2,1,0:T(8,128)S(1)}, u32[]{:S(2)}, u32[]{:S(2)}) collective-permute-start(f32[14,8,128]{2,1,0:T(8,128)S(1)} %get-tuple-element.25), channel_id=1, source_target_pairs={{256,384},{384,256},{257,385},{385,257},{258,386},{386,258},{259,3... | collective-permute-start | bytes 172040 | tf_op jit(solution)/shard_map/ppermute | solution.py:338
  3.1 12.3 %collective-permute-start = (f32[14,8,128]{2,1,0:T(8,128)S(1)}, f32[14,8,128]{2,1,0:T(8,128)S(1)}, u32[]{:S(2)}, u32[]{:S(2)}) collective-permute-start(f32[14,8,128]{2,1,0:T(8,128)S(1)} %get-tuple-element.25), channel_id=1, source_target_pairs={{0,128},{128,0},{1,129},{129,1},{2,130},{130,2},{3,131},{131,3},{4... | collective-permute-start | bytes 172040 | tf_op jit(solution)/shard_map/ppermute | solution.py:335
  15.4 8.7 %all-to-all-start = ((f32[32,2,128]{2,1,0:T(2,128)}), f32[32,2,128]{2,1,0:T(2,128)S(1)}, u32[]{:S(2)}, u32[]{:S(2)}) async-start(f32[32,2,128]{2,1,0:T(2,128)} %get-tuple-element.32), calls=%async_computation | async-start | bytes 65536 | tf_op jit(solution)/shard_map/all_to_all | solution.py:337
  24.2 0.0 collective-permute-done.2.b_ref
  24.2 0.0 collective-permute-done.1.ah_ref
  24.2 0.0 collective-permute-done.al_ref
  24.2 0.2 second.1
  24.4 5.2 %collective-permute-start.4 = (f32[4,8,128]{2,1,0:T(8,128)S(1)}, f32[4,8,128]{2,1,0:T(8,128)S(1)}, u32[]{:S(2)}, u32[]{:S(2)}) collective-permute-start(f32[4,8,128]{2,1,0:T(8,128)S(1)} %get-tuple-element.27), channel_id=1, source_target_pairs={{1,2},{2,1},{3,4},{4,3},{5,6},{6,5},{7,8},{8,7},{9,10},{10,9},{11,... | collective-permute-start | bytes 49160 | tf_op jit(solution)/shard_map/ppermute | solution.py:348
  29.6 1.9 %collective-permute-start.3 = (f32[4,8,128]{2,1,0:T(8,128)S(1)}, f32[4,8,128]{2,1,0:T(8,128)S(1)}, u32[]{:S(2)}, u32[]{:S(2)}) collective-permute-start(f32[4,8,128]{2,1,0:T(8,128)S(1)} %get-tuple-element.27), channel_id=1, source_target_pairs={{0,1},{1,0},{2,3},{3,2},{4,5},{5,4},{6,7},{7,6},{8,9},{9,8},{10,11... | collective-permute-start | bytes 49160 | tf_op jit(solution)/shard_map/ppermute | solution.py:349
  31.5 0.6 %collective-permute-done.4.zb_ref = f32[4,8,128]{2,1,0:T(8,128)S(1)} collective-permute-done((f32[4,8,128]{2,1,0:T(8,128)S(1)}, f32[4,8,128]{2,1,0:T(8,128)S(1)}, u32[]{:S(2)}, u32[]{:S(2)}) %collective-permute-start.4) | collective-permute-done | bytes 16416 | tf_op jit(solution)/shard_map/ppermute | solution.py:348
  32.1 3.1 %collective-permute-done.3.za_ref = f32[4,8,128]{2,1,0:T(8,128)S(1)} collective-permute-done((f32[4,8,128]{2,1,0:T(8,128)S(1)}, f32[4,8,128]{2,1,0:T(8,128)S(1)}, u32[]{:S(2)}, u32[]{:S(2)}) %collective-permute-start.3) | collective-permute-done | bytes 16416 | tf_op jit(solution)/shard_map/ppermute | solution.py:349
  35.2 3.4 %collective-permute-start.5 = (f32[16,8,128]{2,1,0:T(8,128)S(1)}, f32[16,8,128]{2,1,0:T(8,128)S(1)}, u32[]{:S(2)}, u32[]{:S(2)}) collective-permute-start(f32[16,8,128]{2,1,0:T(8,128)S(1)} %get-tuple-element.30), channel_id=1, source_target_pairs={{0,16},{16,0},{32,48},{48,32},{64,80},{80,64},{96,112},{112,96},{1... | collective-permute-start | bytes 196616 | tf_op jit(solution)/shard_map/ppermute | solution.py:359
  38.6 1.9 %collective-permute-start.6 = (f32[16,8,128]{2,1,0:T(8,128)S(1)}, f32[16,8,128]{2,1,0:T(8,128)S(1)}, u32[]{:S(2)}, u32[]{:S(2)}) collective-permute-start(f32[16,8,128]{2,1,0:T(8,128)S(1)} %get-tuple-element.31), channel_id=1, source_target_pairs={{16,32},{32,16},{48,64},{64,48},{80,96},{96,80},{17,33},{33,17},{4... | collective-permute-start | bytes 196616 | tf_op jit(solution)/shard_map/ppermute | solution.py:358
  40.5 0.0 all-to-all-done.s_ref
  40.5 0.8 %collective-permute-done.5.ya_ref = f32[16,8,128]{2,1,0:T(8,128)S(1)} collective-permute-done((f32[16,8,128]{2,1,0:T(8,128)S(1)}, f32[16,8,128]{2,1,0:T(8,128)S(1)}, u32[]{:S(2)}, u32[]{:S(2)}) %collective-permute-start.5) | collective-permute-done | bytes 65568 | tf_op jit(solution)/shard_map/ppermute | solution.py:359
  41.4 4.6 %collective-permute-done.6.yb_ref = f32[16,8,128]{2,1,0:T(8,128)S(1)} collective-permute-done((f32[16,8,128]{2,1,0:T(8,128)S(1)}, f32[16,8,128]{2,1,0:T(8,128)S(1)}, u32[]{:S(2)}, u32[]{:S(2)}) %collective-permute-start.6) | collective-permute-done | bytes 65568 | tf_op jit(solution)/shard_map/ppermute | solution.py:358
  46.0 1.6 %last.1 = f32[8,16,128]{2,1,0:T(8,128)} custom-call(f32[8,16,128]{2,1,0:T(8,128)S(1)} %get-tuple-element.19.v_ref, f32[8,16,128]{2,1,0:T(8,128)S(1)} %get-tuple-element.20.w_ref, f32[4,8,128]{2,1,0:T(8,128)S(1)} %get-tuple-element.21.v1_ref, f32[4,8,128]{2,1,0:T(8,128)S(1)} %get-tuple-element.22.w1_ref, f32[2,8,128]{2,1,0:T(8,128)S(1)} %get-tuple-element.23.v2_ref, ...), custom_call_target="tpu_custom_call" | custom-call | tf_op jit(solution)/shard_map/last/pallas_call | solution.py:361
  (1 shorter events, 0.0 us)
Async XLA Ops:
  1.8 22.4 %collective-permute-start.2 = (f32[14,8,128]{2,1,0:T(8,128)S(1)}, f32[14,8,128]{2,1,0:T(8,128)S(1)}, u32[]{:S(2)}, u32[]{:S(2)}) collective-permute-start(f32[14,8,128]{2,1,0:T(8,128)S(1)} %get-tuple-element.26), channel_id=1, source_target_pairs={{128,256},{256,128},{129,257},{257,129},{130,258},{258,130},{131,2... | collective-permute-start | bytes 172040 | tf_op jit(solution)/shard_map/ppermute | solution.py:336
  2.5 21.7 %collective-permute-start.1 = (f32[14,8,128]{2,1,0:T(8,128)S(1)}, f32[14,8,128]{2,1,0:T(8,128)S(1)}, u32[]{:S(2)}, u32[]{:S(2)}) collective-permute-start(f32[14,8,128]{2,1,0:T(8,128)S(1)} %get-tuple-element.25), channel_id=1, source_target_pairs={{256,384},{384,256},{257,385},{385,257},{258,386},{386,258},{259,3... | collective-permute-start | bytes 172040 | tf_op jit(solution)/shard_map/ppermute | solution.py:338
  3.1 21.1 %collective-permute-start = (f32[14,8,128]{2,1,0:T(8,128)S(1)}, f32[14,8,128]{2,1,0:T(8,128)S(1)}, u32[]{:S(2)}, u32[]{:S(2)}) collective-permute-start(f32[14,8,128]{2,1,0:T(8,128)S(1)} %get-tuple-element.25), channel_id=1, source_target_pairs={{0,128},{128,0},{1,129},{129,1},{2,130},{130,2},{3,131},{131,3},{4... | collective-permute-start | bytes 172040 | tf_op jit(solution)/shard_map/ppermute | solution.py:335
  15.4 25.1 %all-to-all-start = ((f32[32,2,128]{2,1,0:T(2,128)}), f32[32,2,128]{2,1,0:T(2,128)S(1)}, u32[]{:S(2)}, u32[]{:S(2)}) async-start(f32[32,2,128]{2,1,0:T(2,128)} %get-tuple-element.32), calls=%async_computation | async-start | bytes 65536 | tf_op jit(solution)/shard_map/all_to_all | solution.py:337
  24.4 7.7 %collective-permute-start.4 = (f32[4,8,128]{2,1,0:T(8,128)S(1)}, f32[4,8,128]{2,1,0:T(8,128)S(1)}, u32[]{:S(2)}, u32[]{:S(2)}) collective-permute-start(f32[4,8,128]{2,1,0:T(8,128)S(1)} %get-tuple-element.27), channel_id=1, source_target_pairs={{1,2},{2,1},{3,4},{4,3},{5,6},{6,5},{7,8},{8,7},{9,10},{10,9},{11,... | collective-permute-start | bytes 49160 | tf_op jit(solution)/shard_map/ppermute | solution.py:348
  29.6 5.6 %collective-permute-start.3 = (f32[4,8,128]{2,1,0:T(8,128)S(1)}, f32[4,8,128]{2,1,0:T(8,128)S(1)}, u32[]{:S(2)}, u32[]{:S(2)}) collective-permute-start(f32[4,8,128]{2,1,0:T(8,128)S(1)} %get-tuple-element.27), channel_id=1, source_target_pairs={{0,1},{1,0},{2,3},{3,2},{4,5},{5,4},{6,7},{7,6},{8,9},{9,8},{10,11... | collective-permute-start | bytes 49160 | tf_op jit(solution)/shard_map/ppermute | solution.py:349
  35.2 6.2 %collective-permute-start.5 = (f32[16,8,128]{2,1,0:T(8,128)S(1)}, f32[16,8,128]{2,1,0:T(8,128)S(1)}, u32[]{:S(2)}, u32[]{:S(2)}) collective-permute-start(f32[16,8,128]{2,1,0:T(8,128)S(1)} %get-tuple-element.30), channel_id=1, source_target_pairs={{0,16},{16,0},{32,48},{48,32},{64,80},{80,64},{96,112},{112,96},{1... | collective-permute-start | bytes 196616 | tf_op jit(solution)/shard_map/ppermute | solution.py:359
  38.6 7.4 %collective-permute-start.6 = (f32[16,8,128]{2,1,0:T(8,128)S(1)}, f32[16,8,128]{2,1,0:T(8,128)S(1)}, u32[]{:S(2)}, u32[]{:S(2)}) collective-permute-start(f32[16,8,128]{2,1,0:T(8,128)S(1)} %get-tuple-element.31), channel_id=1, source_target_pairs={{16,32},{32,16},{48,64},{64,48},{80,96},{96,80},{17,33},{33,17},{4... | collective-permute-start | bytes 196616 | tf_op jit(solution)/shard_map/ppermute | solution.py:358

commit v5 on v4

--- a/solution.py
+++ b/solution.py
@@ -15,6 +15,11 @@
 VMEM = pl.BlockSpec(memory_space=pltpu.VMEM)
 HIGHEST = lax.Precision.HIGHEST
 AXES = ("gx", "gy", "gz")
+FIRST_CHIP = 2
+
+
+def along_z(chips):
+    return [(i + FIRST_CHIP) % chips for i in range(chips)]
 
 
 def lanes(shape=(8, 128)):
@@ -71,10 +76,12 @@
     both = [jnp.where(quad, v2[i], w2[i]) for i in (0, 1)]
     last = jnp.where(row < 4, both[0], both[1])
     ends = [jnp.sum(jnp.where((lane >> 5) == row, v2[i], 0.0), axis=0, keepdims=True) for i in (0, 1)]
+    mails = []
     for j in range(nx):
-        far = jnp.where(j > gx, ends[1], ends[0])
-        mail = jnp.concatenate([sums, far], axis=0)
-        s_ref[j * ny : (j + 1) * ny] = jnp.broadcast_to(mail[None], (ny, 2, 128))
+        mails.append(jnp.concatenate([sums, jnp.where(j > gx, ends[1], ends[0])], axis=0))
+    for i, z in enumerate(along_z(nx * ny // 2)):
+        for core in (1, 0):
+            s_ref[2 * i + 1 - core] = mails[2 * (z // ny) + core]
     even = (gx & 1) == 0
     for x_ref, up in ((a_ref, even), (b_ref, jnp.logical_not(even))):
         for d in range(3):
@@ -225,7 +232,9 @@
     lane, row = lanes(), rows()
 
     def far(slot, have):
-        t = jnp.broadcast_to(s_ref[slot * ny + gy, 1:2], (8, 128))
+        chips = nx * ny // 2
+        place = lax.rem((slot >> 1) * ny + gy + chips - FIRST_CHIP, chips)
+        t = jnp.broadcast_to(s_ref[2 * place + 1 - (slot & 1), 1:2], (8, 128))
         spread = jnp.zeros((8, 128), F32)
         for i in range(4):
             spread = jnp.where(row == i, turn(t, -32 * i, 1), spread)
@@ -334,7 +343,8 @@
     odd = lambda n: [(i, i + 1 if i & 1 else i - 1) for i in range(1, n - 1)]
     al_in = lax.ppermute(a_out, "gx", even(nx)[: nx // 2])
     b_in = lax.ppermute(b_out, "gx", odd(nx))
-    s_in = lax.all_to_all(s_out, ("gx", "gy"), 0, 0, tiled=True)
+    ring = [(2 * (z // ny) + core) * ny + z % ny for z in along_z(nx * ny // 2) for core in (1, 0)]
+    s_in = lax.all_to_all(s_out, ("gx", "gy"), 0, 0, tiled=True, axis_index_groups=[ring])
     ah_in = lax.ppermute(a_out, "gx", even(nx)[nx // 2 :])
     limit = pltpu.CompilerParams(vmem_limit_bytes=8 << 20)
     z_out, ya_own, yb_own = call(

time: 48 us -> 47 us (0.979)
  the two profiles are of different devices: /device:TPU:134 before, /device:TPU:38 now
where the time goes in v5:
time: 47 us; the launch traced here: 46.7 us
  starting transfers between devices  35.5 us (76%)
  waiting for transfers between devices  7.46 us (16%)
  Pallas kernels  2.75 us (6%)
  other arithmetic  0.88 us (2%)
    ppermute x1, starting transfers between devices, per_device(): al_in = lax.ppermute(a_out, 'gx', even(nx)[:nx // 2])  16.2 us
    ppermute x1, starting transfers between devices, per_device(): zb_in = lax.ppermute(z_out, 'gz', odd(nz))  5.19 us
    all_to_all x1, starting transfers between devices, per_device(): lax.all_to_all(s_out, ('gx', 'gy'), 0, 0, tiled=True, axis_index_groups=[...  5.11 us
    ppermute x1, waiting for transfers between devices, per_device(): yb_in = lax.ppermute(yb_out, 'gy', odd(ny))  3.36 us
    ppermute x1, starting transfers between devices, per_device(): ya_in = lax.ppermute(ya_out, 'gy', even(ny))  3.36 us
    ppermute x1, waiting for transfers between devices, per_device(): za_in = lax.ppermute(z_out, 'gz', even(nz))  3.09 us
    ppermute x1, starting transfers between devices, per_device(): yb_in = lax.ppermute(yb_out, 'gy', odd(ny))  2.39 us
    ppermute x1, starting transfers between devices, per_device(): za_in = lax.ppermute(z_out, 'gz', even(nz))  1.92 us
  transfers between devices with their start and end apart: 8, of which 4 were waited for; matrix products, arithmetic and copies ran while one was open for 0% of the time, Pallas kernels for 0%

profile of v5, /device:TPU:38, one launch (start us, length us, event | category | flops | bytes accessed | tf_op | source)
XLA Modules:
  0.0 46.7 jit_solution(18042774412543959973)
XLA Ops:
  0.0 0.9 %pad_maximum_fusion.in_ref = f32[2,8,16,128]{3,2,1,0:T(8,128)S(1)} fusion(f32[1,8,16,128]{3,2,1,0:T(8,128)} %bitcast.2, f32[1,8,16,128]{3,2,1,0:T(8,128)} %bitcast.3), kind=kLoop, calls=%fused_computation | loop fusion | flops 32768 | bytes 262144 | tf_op jit(solution)/shard_map/stack | solution.py:341
  0.9 0.9 %first.1 = (f32[14,8,128]{2,1,0:T(8,128)S(1)}, f32[14,8,128]{2,1,0:T(8,128)S(1)}, f32[32,2,128]{2,1,0:T(2,128)}, f32[8,16,128]{2,1,0:T(8,128)S(1)}, f32[8,16,128...) custom-call(f32[2,8,16,128]{3,2,1,0:T(8,128)S(1)} %pad_maximum_fusio, ...), custom_call_target="tpu_custom_call" | custom-call | tf_op jit(solution)/shard_map/first/pallas_call | solution.py:333
  1.8 0.7 %collective-permute-start.2 = (f32[14,8,128]{2,1,0:T(8,128)S(1)}, f32[14,8,128]{2,1,0:T(8,128)S(1)}, u32[]{:S(2)}, u32[]{:S(2)}) collective-permute-start(f32[14,8,128]{2,1,0:T(8,128)S(1)} %get-tuple-element.26), channel_id=1, source_target_pairs={{128,256},{256,128},{129,257},{257,129},{130,258},{258,130},{131,2... | collective-permute-start | bytes 172040 | tf_op jit(solution)/shard_map/ppermute | solution.py:345
  2.5 0.7 %collective-permute-start.1 = (f32[14,8,128]{2,1,0:T(8,128)S(1)}, f32[14,8,128]{2,1,0:T(8,128)S(1)}, u32[]{:S(2)}, u32[]{:S(2)}) collective-permute-start(f32[14,8,128]{2,1,0:T(8,128)S(1)} %get-tuple-element.25), channel_id=1, source_target_pairs={{256,384},{384,256},{257,385},{385,257},{258,386},{386,258},{259,3... | collective-permute-start | bytes 172040 | tf_op jit(solution)/shard_map/ppermute | solution.py:348
  3.1 16.2 %collective-permute-start = (f32[14,8,128]{2,1,0:T(8,128)S(1)}, f32[14,8,128]{2,1,0:T(8,128)S(1)}, u32[]{:S(2)}, u32[]{:S(2)}) collective-permute-start(f32[14,8,128]{2,1,0:T(8,128)S(1)} %get-tuple-element.25), channel_id=1, source_target_pairs={{0,128},{128,0},{1,129},{129,1},{2,130},{130,2},{3,131},{131,3},{4... | collective-permute-start | bytes 172040 | tf_op jit(solution)/shard_map/ppermute | solution.py:344
  19.3 5.1 %all-to-all-start = ((f32[32,2,128]{2,1,0:T(2,128)}), f32[32,2,128]{2,1,0:T(2,128)S(1)}, u32[]{:S(2)}, u32[]{:S(2)}) async-start(f32[32,2,128]{2,1,0:T(2,128)} %get-tuple-element.32), calls=%async_computation | async-start | bytes 65536 | tf_op jit(solution)/shard_map/all_to_all | solution.py:347
  24.4 0.0 collective-permute-done.2.b_ref
  24.5 0.0 collective-permute-done.1.ah_ref
  24.5 0.0 collective-permute-done.al_ref
  24.5 0.2 second.1
  24.7 5.2 %collective-permute-start.4 = (f32[4,8,128]{2,1,0:T(8,128)S(1)}, f32[4,8,128]{2,1,0:T(8,128)S(1)}, u32[]{:S(2)}, u32[]{:S(2)}) collective-permute-start(f32[4,8,128]{2,1,0:T(8,128)S(1)} %get-tuple-element.27), channel_id=1, source_target_pairs={{1,2},{2,1},{3,4},{4,3},{5,6},{6,5},{7,8},{8,7},{9,10},{10,9},{11,... | collective-permute-start | bytes 49160 | tf_op jit(solution)/shard_map/ppermute | solution.py:358
  29.9 1.9 %collective-permute-start.3 = (f32[4,8,128]{2,1,0:T(8,128)S(1)}, f32[4,8,128]{2,1,0:T(8,128)S(1)}, u32[]{:S(2)}, u32[]{:S(2)}) collective-permute-start(f32[4,8,128]{2,1,0:T(8,128)S(1)} %get-tuple-element.27), channel_id=1, source_target_pairs={{0,1},{1,0},{2,3},{3,2},{4,5},{5,4},{6,7},{7,6},{8,9},{9,8},{10,11... | collective-permute-start | bytes 49160 | tf_op jit(solution)/shard_map/ppermute | solution.py:359
  31.8 0.6 %collective-permute-done.4.zb_ref = f32[4,8,128]{2,1,0:T(8,128)S(1)} collective-permute-done((f32[4,8,128]{2,1,0:T(8,128)S(1)}, f32[4,8,128]{2,1,0:T(8,128)S(1)}, u32[]{:S(2)}, u32[]{:S(2)}) %collective-permute-start.4) | collective-permute-done | bytes 16416 | tf_op jit(solution)/shard_map/ppermute | solution.py:358
  32.4 3.1 %collective-permute-done.3.za_ref = f32[4,8,128]{2,1,0:T(8,128)S(1)} collective-permute-done((f32[4,8,128]{2,1,0:T(8,128)S(1)}, f32[4,8,128]{2,1,0:T(8,128)S(1)}, u32[]{:S(2)}, u32[]{:S(2)}) %collective-permute-start.3) | collective-permute-done | bytes 16416 | tf_op jit(solution)/shard_map/ppermute | solution.py:359
  35.5 3.4 %collective-permute-start.5 = (f32[16,8,128]{2,1,0:T(8,128)S(1)}, f32[16,8,128]{2,1,0:T(8,128)S(1)}, u32[]{:S(2)}, u32[]{:S(2)}) collective-permute-start(f32[16,8,128]{2,1,0:T(8,128)S(1)} %get-tuple-element.30), channel_id=1, source_target_pairs={{0,16},{16,0},{32,48},{48,32},{64,80},{80,64},{96,112},{112,96},{1... | collective-permute-start | bytes 196616 | tf_op jit(solution)/shard_map/ppermute | solution.py:369
  38.9 2.4 %collective-permute-start.6 = (f32[16,8,128]{2,1,0:T(8,128)S(1)}, f32[16,8,128]{2,1,0:T(8,128)S(1)}, u32[]{:S(2)}, u32[]{:S(2)}) collective-permute-start(f32[16,8,128]{2,1,0:T(8,128)S(1)} %get-tuple-element.31), channel_id=1, source_target_pairs={{16,32},{32,16},{48,64},{64,48},{80,96},{96,80},{17,33},{33,17},{4... | collective-permute-start | bytes 196616 | tf_op jit(solution)/shard_map/ppermute | solution.py:368
  41.3 0.0 all-to-all-done.s_ref
  41.3 0.4 collective-permute-done.5.ya_ref
  41.7 3.4 %collective-permute-done.6.yb_ref = f32[16,8,128]{2,1,0:T(8,128)S(1)} collective-permute-done((f32[16,8,128]{2,1,0:T(8,128)S(1)}, f32[16,8,128]{2,1,0:T(8,128)S(1)}, u32[]{:S(2)}, u32[]{:S(2)}) %collective-permute-start.6) | collective-permute-done | bytes 65568 | tf_op jit(solution)/shard_map/ppermute | solution.py:368
  45.0 1.6 %last.1 = f32[8,16,128]{2,1,0:T(8,128)} custom-call(f32[8,16,128]{2,1,0:T(8,128)S(1)} %get-tuple-element.19.v_ref, f32[8,16,128]{2,1,0:T(8,128)S(1)} %get-tuple-element.20.w_ref, f32[4,8,128]{2,1,0:T(8,128)S(1)} %get-tuple-element.21.v1_ref, f32[4,8,128]{2,1,0:T(8,128)S(1)} %get-tuple-element.22.w1_ref, f32[2,8,128]{2,1,0:T(8,128)S(1)} %get-tuple-element.23.v2_ref, ...), custom_call_target="tpu_custom_call" | custom-call | tf_op jit(solution)/shard_map/last/pallas_call | solution.py:371
  (1 shorter events, 0.0 us)
Async XLA Ops:
  1.8 22.6 %collective-permute-start.2 = (f32[14,8,128]{2,1,0:T(8,128)S(1)}, f32[14,8,128]{2,1,0:T(8,128)S(1)}, u32[]{:S(2)}, u32[]{:S(2)}) collective-permute-start(f32[14,8,128]{2,1,0:T(8,128)S(1)} %get-tuple-element.26), channel_id=1, source_target_pairs={{128,256},{256,128},{129,257},{257,129},{130,258},{258,130},{131,2... | collective-permute-start | bytes 172040 | tf_op jit(solution)/shard_map/ppermute | solution.py:345
  2.5 22.0 %collective-permute-start.1 = (f32[14,8,128]{2,1,0:T(8,128)S(1)}, f32[14,8,128]{2,1,0:T(8,128)S(1)}, u32[]{:S(2)}, u32[]{:S(2)}) collective-permute-start(f32[14,8,128]{2,1,0:T(8,128)S(1)} %get-tuple-element.25), channel_id=1, source_target_pairs={{256,384},{384,256},{257,385},{385,257},{258,386},{386,258},{259,3... | collective-permute-start | bytes 172040 | tf_op jit(solution)/shard_map/ppermute | solution.py:348
  3.1 21.3 %collective-permute-start = (f32[14,8,128]{2,1,0:T(8,128)S(1)}, f32[14,8,128]{2,1,0:T(8,128)S(1)}, u32[]{:S(2)}, u32[]{:S(2)}) collective-permute-start(f32[14,8,128]{2,1,0:T(8,128)S(1)} %get-tuple-element.25), channel_id=1, source_target_pairs={{0,128},{128,0},{1,129},{129,1},{2,130},{130,2},{3,131},{131,3},{4... | collective-permute-start | bytes 172040 | tf_op jit(solution)/shard_map/ppermute | solution.py:344
  19.3 22.0 %all-to-all-start = ((f32[32,2,128]{2,1,0:T(2,128)}), f32[32,2,128]{2,1,0:T(2,128)S(1)}, u32[]{:S(2)}, u32[]{:S(2)}) async-start(f32[32,2,128]{2,1,0:T(2,128)} %get-tuple-element.32), calls=%async_computation | async-start | bytes 65536 | tf_op jit(solution)/shard_map/all_to_all | solution.py:347
  24.7 7.7 %collective-permute-start.4 = (f32[4,8,128]{2,1,0:T(8,128)S(1)}, f32[4,8,128]{2,1,0:T(8,128)S(1)}, u32[]{:S(2)}, u32[]{:S(2)}) collective-permute-start(f32[4,8,128]{2,1,0:T(8,128)S(1)} %get-tuple-element.27), channel_id=1, source_target_pairs={{1,2},{2,1},{3,4},{4,3},{5,6},{6,5},{7,8},{8,7},{9,10},{10,9},{11,... | collective-permute-start | bytes 49160 | tf_op jit(solution)/shard_map/ppermute | solution.py:358
  29.9 5.6 %collective-permute-start.3 = (f32[4,8,128]{2,1,0:T(8,128)S(1)}, f32[4,8,128]{2,1,0:T(8,128)S(1)}, u32[]{:S(2)}, u32[]{:S(2)}) collective-permute-start(f32[4,8,128]{2,1,0:T(8,128)S(1)} %get-tuple-element.27), channel_id=1, source_target_pairs={{0,1},{1,0},{2,3},{3,2},{4,5},{5,4},{6,7},{7,6},{8,9},{9,8},{10,11... | collective-permute-start | bytes 49160 | tf_op jit(solution)/shard_map/ppermute | solution.py:359
  35.5 6.2 %collective-permute-start.5 = (f32[16,8,128]{2,1,0:T(8,128)S(1)}, f32[16,8,128]{2,1,0:T(8,128)S(1)}, u32[]{:S(2)}, u32[]{:S(2)}) collective-permute-start(f32[16,8,128]{2,1,0:T(8,128)S(1)} %get-tuple-element.30), channel_id=1, source_target_pairs={{0,16},{16,0},{32,48},{48,32},{64,80},{80,64},{96,112},{112,96},{1... | collective-permute-start | bytes 196616 | tf_op jit(solution)/shard_map/ppermute | solution.py:369
  38.9 6.2 %collective-permute-start.6 = (f32[16,8,128]{2,1,0:T(8,128)S(1)}, f32[16,8,128]{2,1,0:T(8,128)S(1)}, u32[]{:S(2)}, u32[]{:S(2)}) collective-permute-start(f32[16,8,128]{2,1,0:T(8,128)S(1)} %get-tuple-element.31), channel_id=1, source_target_pairs={{16,32},{32,16},{48,64},{64,48},{80,96},{96,80},{17,33},{33,17},{4... | collective-permute-start | bytes 196616 | tf_op jit(solution)/shard_map/ppermute | solution.py:368

commit v6 on v5

--- a/solution.py
+++ b/solution.py
@@ -208,14 +208,14 @@
     )
 
 
-def relaxed(v_ref, w_ref, a_ref, b_ref, count):
+def relaxed(start, weight, a_ref, b_ref, count):
     done = []
     for sweep in range(SWEEPS - 1):
-        source = (v_ref, a_ref, b_ref)[sweep]
+        source = (start, lambda i: a_ref[i], lambda i: b_ref[i])[sweep]
         target = (a_ref, b_ref, None)[sweep]
         for i in range(sweep + 1, count - sweep - 1):
-            v = source[i]
-            new = KEEP * v + v_ref[i] + w_ref[i] * around(v, source[i - 1], source[i + 1])
+            v = source(i)
+            new = KEEP * v + start(i) + weight(i) * around(v, source(i - 1), source(i + 1))
             if target is None:
                 done.append(new)
             else:
@@ -223,8 +223,35 @@
     return done
 
 
+def fourth_kernel(
+    v_ref, w_ref, v1_ref, w1_ref, v2_ref, w2_ref, al_ref, ah_ref, b_ref, za_ref, zb_ref, fv, fw, mv, mw
+):
+    level0, level1, _ = extended(
+        lax.axis_index("gx"), v_ref, w_ref, v1_ref, w1_ref, v2_ref, w2_ref, al_ref, ah_ref, b_ref
+    )
+    own = [both_ends(i, za_ref, zb_ref) for i in range(3)]
+    z0, lane = jnp.concatenate(own[0:2], axis=0), lanes()
+    for i in range(14):
+        v, w = level0[i]
+        fv[i, :, 0:128] = v
+        if 1 <= i < 13:
+            fw[i, :, 0:128] = w
+            fv[i, :, 128:256] = turn(z0, -(10 * i - 7), 1)
+            fw[i, :, 128:256] = turn(z0, -(10 * i - 2), 1)
+        else:
+            fv[i, :, 128:256] = jnp.zeros((16, 128), F32)
+    for i in range(10):
+        if 1 <= i < 9:
+            for field, target, at in ((0, mv, 10 * i - 7), (1, mw, 10 * i - 2)):
+                ends = jnp.where(lane < 96, turn(own[2], 64 - at, 1), turn(own[2], -at, 1))
+                target[i] = jnp.where(lane < 64, level1[i][field], ends)
+        else:
+            mv[i] = level1[i][0]
+
+
 def last_kernel(
-    nx, ny, v_ref, w_ref, v1_ref, w1_ref, v2_ref, w2_ref, al_ref, ah_ref, b_ref, za_ref, zb_ref, ya_ref, yb_ref, s_ref, out_ref,
+    nx, ny, v_ref, w_ref, v1_ref, w1_ref, v2_ref, w2_ref, al_ref, ah_ref, b_ref, za_ref, zb_ref,
+    fv_ref, fw_ref, mv_ref, mw_ref, ya_ref, yb_ref, s_ref, out_ref,
     fv, fw, fa, fb, mv, mw, ma, mb, cv, cw, ca, cb, wide_ref, deep_ref,
 ):
     gx, gy = lax.axis_index("gx"), lax.axis_index("gy")
@@ -241,7 +268,7 @@
         return jnp.where(have, spread, 0.0)
 
     outer_layers = far(jnp.maximum(gx - 2, 0), gx > 1), far(jnp.minimum(gx + 2, nx - 1), gx < nx - 2)
-    level0, level1, level2 = extended(
+    _, _, level2 = extended(
         gx, v_ref, w_ref, v1_ref, w1_ref, v2_ref, w2_ref, al_ref, ah_ref, b_ref, outer_layers
     )
 
@@ -249,41 +276,33 @@
         a, b = ya_ref[k], yb_ref[k]
         return jnp.where(up, a, b), jnp.where(up, b, a)
 
-    own = [both_ends(i, za_ref, zb_ref) for i in range(4)]
+    own = both_ends(3, za_ref, zb_ref)
     plus, minus = zip(*(sides(12 + i) for i in range(4)))
     none = jnp.zeros((8, 128), F32)
 
     def outer(p, m):
         return jnp.where(row < 3, p, jnp.where(row >= 5, m, none))
 
-    z0 = jnp.concatenate([own[0], own[1], outer(plus[0], minus[1])], axis=0)
-    z1 = jnp.concatenate([own[2], outer(plus[2], minus[2])], axis=0)
-    z2 = jnp.concatenate([jnp.where(row < 4, own[3], plus[3]), jnp.where(row >= 5, minus[3], none)], axis=0)
+    z0 = outer(plus[0], minus[1])
+    z1 = outer(plus[2], minus[2])
+    z2 = jnp.concatenate([jnp.where(row < 4, own, plus[3]), jnp.where(row >= 5, minus[3], none)], axis=0)
 
     lane16 = lanes((16, 128))
-    fv[0, 0:16, 0:128] = level0[0][0]
-    fv[13, 0:16, 0:128] = level0[13][0]
     for i in (0, 13):
-        fv[i, 16:24, 0:128] = none
-        fv[i, :, 128:256] = jnp.zeros((24, 128), F32)
+        fv[i] = jnp.zeros((8, 256), F32)
+    for i in (0, 9):
+        mv[i] = none
     for k in range(12):
         p, m = sides(k)
-        v, w = level0[k + 1]
-        fv[k + 1, 0:16, 0:128] = v
-        fw[k + 1, 0:16, 0:128] = w
-        fv[k + 1, 16:24, 0:128] = outer(p, m)
-        fw[k + 1, 16:24, 0:128] = jnp.where(row < 2, turn(p, 5, 0), jnp.where(row >= 6, turn(m, 3, 0), none))
+        fv[k + 1, :, 0:128] = outer(p, m)
+        fw[k + 1, :, 0:128] = jnp.where(row < 2, turn(p, 5, 0), jnp.where(row >= 6, turn(m, 3, 0), none))
         fv[k + 1, :, 128:256] = turn(z0, -(10 * k + 3), 1)
         fw[k + 1, :, 128:256] = turn(z0, -(10 * k + 8), 1)
         if k < 8:
             extra = outer(turn(p, 3, 0), turn(m, 5, 0))
-            v, w = level1[k + 1]
-            v = jnp.concatenate([v, extra], axis=0)
-            w = jnp.concatenate([w, turn(extra, 64, 1)], axis=0)
-            at = 10 * k + 3
-            mv[k + 1] = jnp.where(lane16 < 64, v, jnp.where(lane16 < 96, turn(z1, 64 - at, 1), turn(z1, -at, 1)))
-            at = 10 * k + 8
-            mw[k + 1] = jnp.where(lane16 < 64, w, jnp.where(lane16 < 96, turn(z1, 64 - at, 1), turn(z1, -at, 1)))
+            for field, target, at in ((extra, mv, 10 * k + 3), (turn(extra, 64, 1), mw, 10 * k + 8)):
+                ends = jnp.where(lane < 96, turn(z1, 64 - at, 1), turn(z1, -at, 1))
+                target[k + 1] = jnp.where(lane < 64, field, ends)
         elif k < 11:
             near, far = turn(p, 7, 0), turn(m, 5, 0)
             for i in (0, 1):
@@ -296,14 +315,12 @@
                     at = 10 * j + (3, 8)[field]
                     ends = jnp.where(lane16 < 64, turn(z2, 32 - at, 1), turn(z2, -at, 1))
                     target[j + 1] = jnp.where(lane16 < 32, full, ends)
-    for i in (0, 9):
-        mv[i, 0:8] = level1[i][0]
-        mv[i, 8:16] = none
     for i in (0, 7):
         cv[i, 0:8] = level2[i][0]
         cv[i, 8:16] = none
 
-    coarse = relaxed(cv, cw, ca, cb, 8)
+    joined = lambda near_ref, far_ref: lambda i: jnp.concatenate([near_ref[i], far_ref[i]], axis=0)
+    coarse = relaxed(lambda i: cv[i], lambda i: cw[i], ca, cb, 8)
     s = jnp.sum(s_ref[...], axis=0)[0:1]
     plane = jnp.where(lane < 64, s / (turn(jnp.broadcast_to(s, (8, 128)), 64, 1) + 16.0), 0.0)
     src, dst = rows((128, 128)), lanes((128, 128))
@@ -311,7 +328,7 @@
     spread2 = jnp.where(src == (dst >> 1), 1.0, 0.0).astype(F32)
     c = jnp.concatenate([layer[0:8] + plane for layer in coarse], axis=0)
     c = jnp.dot(c, spread4, precision=HIGHEST, preferred_element_type=F32).reshape(2, 8, 128)
-    middle = relaxed(mv, mw, ma, mb, 10)
+    middle = relaxed(joined(mv_ref, mv), joined(mw_ref, mw), ma, mb, 10)
     m = jnp.concatenate([layer[0:8] for layer in middle], axis=0)
     m = jnp.dot(m, spread2, precision=HIGHEST, preferred_element_type=F32).reshape(4, 8, 128)
     for i in range(2):
@@ -321,7 +338,7 @@
         total = m[i] + deep_ref[i // 2]
         for j in range(2):
             wide_ref[i, pl.ds(j, 8, stride=2), :] = total
-    fine = relaxed(fv, fw, fa, fb, 14)
+    fine = relaxed(joined(fv_ref, fv), joined(fw_ref, fw), fa, fb, 14)
     for i in range(8):
         out_ref[i] = fine[i][0:16, 0:128] + wide_ref[i // 2]
 
@@ -367,17 +384,27 @@
     )(za_in, zb_in, ya_own, yb_own)
     yb_in = lax.ppermute(yb_out, "gy", odd(ny))
     ya_in = lax.ppermute(ya_out, "gy", even(ny))
-    fine, middle, coarse = (pltpu.VMEM(s, F32) for s in ((14, 24, 256), (10, 16, 128), (8, 16, 128)))
+    rows_own = call(
+        fourth_kernel,
+        out_shape=[shape((14, 16, 256), F32)] * 2 + [shape((10, 8, 128), F32)] * 2,
+        in_specs=[VMEM] * 11,
+        out_specs=[VMEM] * 4,
+        compiler_params=limit,
+        name="fourth",
+    )(*own, al_in, ah_in, b_in, za_in, zb_in)
+    edge, fine, thin, middle, coarse = (
+        pltpu.VMEM(s, F32) for s in ((14, 8, 256), (14, 24, 256), (10, 8, 128), (10, 16, 128), (8, 16, 128))
+    )
     return call(
         functools.partial(last_kernel, nx, ny),
         out_shape=shape((8, 16, 128), F32),
-        in_specs=[VMEM] * 14,
+        in_specs=[VMEM] * 18,
         out_specs=VMEM,
-        scratch_shapes=[fine] * 4 + [middle] * 4 + [coarse] * 4
+        scratch_shapes=[edge] * 2 + [fine] * 2 + [thin] * 2 + [middle] * 2 + [coarse] * 4
         + [pltpu.VMEM((4, 16, 128), F32), pltpu.VMEM((2, 8, 128), F32)],
-        compiler_params=pltpu.CompilerParams(vmem_limit_bytes=8 << 20),
+        compiler_params=limit,
         name="last",
-    )(*own, al_in, ah_in, b_in, za_in, zb_in, ya_in, yb_in, s_in)
+    )(*own, al_in, ah_in, b_in, za_in, zb_in, *rows_own, ya_in, yb_in, s_in)
 
 
 def solution(mesh):

time: 47 us -> 46.9 us (level)
  transfers between devices with their start and end apart: 8 -> 8, of which waited for: 4 -> 4; matrix products, arithmetic and copies ran while one was open for 0% -> 0% of each run, Pallas kernels for 0% -> 1%
where the time goes in v6:
time: 46.9 us; the launch traced here: 46.6 us
  starting transfers between devices  35.5 us (76%)
  waiting for transfers between devices  7.28 us (16%)
  Pallas kernels  2.81 us (6%)
  other arithmetic  0.88 us (2%)
    ppermute x1, starting transfers between devices, per_device(): al_in = lax.ppermute(a_out, 'gx', even(nx)[:nx // 2])  16.2 us
    ppermute x1, starting transfers between devices, per_device(): zb_in = lax.ppermute(z_out, 'gz', odd(nz))  5.19 us
    all_to_all x1, starting transfers between devices, per_device(): lax.all_to_all(s_out, ('gx', 'gy'), 0, 0, tiled=True, axis_index_groups=[...  5.11 us
    ppermute x1, waiting for transfers between devices, per_device(): yb_in = lax.ppermute(yb_out, 'gy', odd(ny))  3.36 us
    ppermute x1, starting transfers between devices, per_device(): ya_in = lax.ppermute(ya_out, 'gy', even(ny))  3.36 us
    ppermute x1, waiting for transfers between devices, per_device(): za_in = lax.ppermute(z_out, 'gz', even(nz))  3.09 us
    ppermute x1, starting transfers between devices, per_device(): yb_in = lax.ppermute(yb_out, 'gy', odd(ny))  2.39 us
    ppermute x1, starting transfers between devices, per_device(): za_in = lax.ppermute(z_out, 'gz', even(nz))  1.92 us
  transfers between devices with their start and end apart: 8, of which 4 were waited for; matrix products, arithmetic and copies ran while one was open for 0% of the time, Pallas kernels for 1%

profile of v6, /device:TPU:38, one launch (start us, length us, event | category | flops | bytes accessed | tf_op | source)
XLA Modules:
  0.0 46.6 jit_solution(5338959841323092990)
XLA Ops:
  0.0 0.9 %pad_maximum_fusion.in_ref = f32[2,8,16,128]{3,2,1,0:T(8,128)S(1)} fusion(f32[1,8,16,128]{3,2,1,0:T(8,128)} %bitcast.2, f32[1,8,16,128]{3,2,1,0:T(8,128)} %bitcast.3), kind=kLoop, calls=%fused_computation | loop fusion | flops 32768 | bytes 262144 | tf_op jit(solution)/shard_map/stack | solution.py:358
  0.9 0.9 %first.1 = (f32[14,8,128]{2,1,0:T(8,128)S(1)}, f32[14,8,128]{2,1,0:T(8,128)S(1)}, f32[32,2,128]{2,1,0:T(2,128)}, f32[8,16,128]{2,1,0:T(8,128)S(1)}, f32[8,16,128...) custom-call(f32[2,8,16,128]{3,2,1,0:T(8,128)S(1)} %pad_maximum_fusio, ...), custom_call_target="tpu_custom_call" | custom-call | tf_op jit(solution)/shard_map/first/pallas_call | solution.py:350
  1.8 0.7 %collective-permute-start.2 = (f32[14,8,128]{2,1,0:T(8,128)S(1)}, f32[14,8,128]{2,1,0:T(8,128)S(1)}, u32[]{:S(2)}, u32[]{:S(2)}) collective-permute-start(f32[14,8,128]{2,1,0:T(8,128)S(1)} %get-tuple-element.30), channel_id=1, source_target_pairs={{128,256},{256,128},{129,257},{257,129},{130,258},{258,130},{131,2... | collective-permute-start | bytes 172040 | tf_op jit(solution)/shard_map/ppermute | solution.py:362
  2.5 0.7 %collective-permute-start.1 = (f32[14,8,128]{2,1,0:T(8,128)S(1)}, f32[14,8,128]{2,1,0:T(8,128)S(1)}, u32[]{:S(2)}, u32[]{:S(2)}) collective-permute-start(f32[14,8,128]{2,1,0:T(8,128)S(1)} %get-tuple-element.29), channel_id=1, source_target_pairs={{256,384},{384,256},{257,385},{385,257},{258,386},{386,258},{259,3... | collective-permute-start | bytes 172040 | tf_op jit(solution)/shard_map/ppermute | solution.py:365
  3.1 16.2 %collective-permute-start = (f32[14,8,128]{2,1,0:T(8,128)S(1)}, f32[14,8,128]{2,1,0:T(8,128)S(1)}, u32[]{:S(2)}, u32[]{:S(2)}) collective-permute-start(f32[14,8,128]{2,1,0:T(8,128)S(1)} %get-tuple-element.29), channel_id=1, source_target_pairs={{0,128},{128,0},{1,129},{129,1},{2,130},{130,2},{3,131},{131,3},{4... | collective-permute-start | bytes 172040 | tf_op jit(solution)/shard_map/ppermute | solution.py:361
  19.3 5.1 %all-to-all-start = ((f32[32,2,128]{2,1,0:T(2,128)}), f32[32,2,128]{2,1,0:T(2,128)S(1)}, u32[]{:S(2)}, u32[]{:S(2)}) async-start(f32[32,2,128]{2,1,0:T(2,128)} %get-tuple-element.40), calls=%async_computation | async-start | bytes 65536 | tf_op jit(solution)/shard_map/all_to_all | solution.py:364
  24.4 0.0 collective-permute-done.2.b_ref
  24.5 0.0 collective-permute-done.1.ah_ref
  24.5 0.0 collective-permute-done.al_ref
  24.5 0.2 second.1
  24.7 5.2 %collective-permute-start.4 = (f32[4,8,128]{2,1,0:T(8,128)S(1)}, f32[4,8,128]{2,1,0:T(8,128)S(1)}, u32[]{:S(2)}, u32[]{:S(2)}) collective-permute-start(f32[4,8,128]{2,1,0:T(8,128)S(1)} %get-tuple-element.31), channel_id=1, source_target_pairs={{1,2},{2,1},{3,4},{4,3},{5,6},{6,5},{7,8},{8,7},{9,10},{10,9},{11,... | collective-permute-start | bytes 49160 | tf_op jit(solution)/shard_map/ppermute | solution.py:375
  29.9 1.9 %collective-permute-start.3 = (f32[4,8,128]{2,1,0:T(8,128)S(1)}, f32[4,8,128]{2,1,0:T(8,128)S(1)}, u32[]{:S(2)}, u32[]{:S(2)}) collective-permute-start(f32[4,8,128]{2,1,0:T(8,128)S(1)} %get-tuple-element.31), channel_id=1, source_target_pairs={{0,1},{1,0},{2,3},{3,2},{4,5},{5,4},{6,7},{7,6},{8,9},{9,8},{10,11... | collective-permute-start | bytes 49160 | tf_op jit(solution)/shard_map/ppermute | solution.py:376
  31.8 0.6 %collective-permute-done.4.zb_ref = f32[4,8,128]{2,1,0:T(8,128)S(1)} collective-permute-done((f32[4,8,128]{2,1,0:T(8,128)S(1)}, f32[4,8,128]{2,1,0:T(8,128)S(1)}, u32[]{:S(2)}, u32[]{:S(2)}) %collective-permute-start.4) | collective-permute-done | bytes 16416 | tf_op jit(solution)/shard_map/ppermute | solution.py:375
  32.4 3.1 %collective-permute-done.3.za_ref = f32[4,8,128]{2,1,0:T(8,128)S(1)} collective-permute-done((f32[4,8,128]{2,1,0:T(8,128)S(1)}, f32[4,8,128]{2,1,0:T(8,128)S(1)}, u32[]{:S(2)}, u32[]{:S(2)}) %collective-permute-start.3) | collective-permute-done | bytes 16416 | tf_op jit(solution)/shard_map/ppermute | solution.py:376
  35.5 3.4 %collective-permute-start.5 = (f32[16,8,128]{2,1,0:T(8,128)S(1)}, f32[16,8,128]{2,1,0:T(8,128)S(1)}, u32[]{:S(2)}, u32[]{:S(2)}) collective-permute-start(f32[16,8,128]{2,1,0:T(8,128)S(1)} %get-tuple-element.38), channel_id=1, source_target_pairs={{0,16},{16,0},{32,48},{48,32},{64,80},{80,64},{96,112},{112,96},{1... | collective-permute-start | bytes 196616 | tf_op jit(solution)/shard_map/ppermute | solution.py:386
  38.9 2.4 %collective-permute-start.6 = (f32[16,8,128]{2,1,0:T(8,128)S(1)}, f32[16,8,128]{2,1,0:T(8,128)S(1)}, u32[]{:S(2)}, u32[]{:S(2)}) collective-permute-start(f32[16,8,128]{2,1,0:T(8,128)S(1)} %get-tuple-element.39), channel_id=1, source_target_pairs={{16,32},{32,16},{48,64},{64,48},{80,96},{96,80},{17,33},{33,17},{4... | collective-permute-start | bytes 196616 | tf_op jit(solution)/shard_map/ppermute | solution.py:385
  41.3 0.2 fourth.1
  41.5 0.0 all-to-all-done.s_ref
  41.5 0.2 collective-permute-done.5.ya_ref
  41.7 3.4 %collective-permute-done.6.yb_ref = f32[16,8,128]{2,1,0:T(8,128)S(1)} collective-permute-done((f32[16,8,128]{2,1,0:T(8,128)S(1)}, f32[16,8,128]{2,1,0:T(8,128)S(1)}, u32[]{:S(2)}, u32[]{:S(2)}) %collective-permute-start.6) | collective-permute-done | bytes 65568 | tf_op jit(solution)/shard_map/ppermute | solution.py:385
  45.0 1.5 %last.1 = f32[8,16,128]{2,1,0:T(8,128)} custom-call(f32[8,16,128]{2,1,0:T(8,128)S(1)} %get-tuple-element.23.v_ref, f32[8,16,128]{2,1,0:T(8,128)S(1)} %get-tuple-element.24.w_ref, f32[4,8,128]{2,1,0:T(8,128)S(1)} %get-tuple-element.25.v1_ref, f32[4,8,128]{2,1,0:T(8,128)S(1)} %get-tuple-element.26.w1_ref, f32[2,8,128]{2,1,0:T(8,128)S(1)} %get-tuple-element.27.v2_ref, ...), custom_call_target="tpu_custom_call" | custom-call | tf_op jit(solution)/shard_map/last/pallas_call | solution.py:398
  (1 shorter events, 0.0 us)
Async XLA Ops:
  1.8 22.6 %collective-permute-start.2 = (f32[14,8,128]{2,1,0:T(8,128)S(1)}, f32[14,8,128]{2,1,0:T(8,128)S(1)}, u32[]{:S(2)}, u32[]{:S(2)}) collective-permute-start(f32[14,8,128]{2,1,0:T(8,128)S(1)} %get-tuple-element.30), channel_id=1, source_target_pairs={{128,256},{256,128},{129,257},{257,129},{130,258},{258,130},{131,2... | collective-permute-start | bytes 172040 | tf_op jit(solution)/shard_map/ppermute | solution.py:362
  2.5 22.0 %collective-permute-start.1 = (f32[14,8,128]{2,1,0:T(8,128)S(1)}, f32[14,8,128]{2,1,0:T(8,128)S(1)}, u32[]{:S(2)}, u32[]{:S(2)}) collective-permute-start(f32[14,8,128]{2,1,0:T(8,128)S(1)} %get-tuple-element.29), channel_id=1, source_target_pairs={{256,384},{384,256},{257,385},{385,257},{258,386},{386,258},{259,3... | collective-permute-start | bytes 172040 | tf_op jit(solution)/shard_map/ppermute | solution.py:365
  3.1 21.3 %collective-permute-start = (f32[14,8,128]{2,1,0:T(8,128)S(1)}, f32[14,8,128]{2,1,0:T(8,128)S(1)}, u32[]{:S(2)}, u32[]{:S(2)}) collective-permute-start(f32[14,8,128]{2,1,0:T(8,128)S(1)} %get-tuple-element.29), channel_id=1, source_target_pairs={{0,128},{128,0},{1,129},{129,1},{2,130},{130,2},{3,131},{131,3},{4... | collective-permute-start | bytes 172040 | tf_op jit(solution)/shard_map/ppermute | solution.py:361
  19.3 22.1 %all-to-all-start = ((f32[32,2,128]{2,1,0:T(2,128)}), f32[32,2,128]{2,1,0:T(2,128)S(1)}, u32[]{:S(2)}, u32[]{:S(2)}) async-start(f32[32,2,128]{2,1,0:T(2,128)} %get-tuple-element.40), calls=%async_computation | async-start | bytes 65536 | tf_op jit(solution)/shard_map/all_to_all | solution.py:364
  24.7 7.7 %collective-permute-start.4 = (f32[4,8,128]{2,1,0:T(8,128)S(1)}, f32[4,8,128]{2,1,0:T(8,128)S(1)}, u32[]{:S(2)}, u32[]{:S(2)}) collective-permute-start(f32[4,8,128]{2,1,0:T(8,128)S(1)} %get-tuple-element.31), channel_id=1, source_target_pairs={{1,2},{2,1},{3,4},{4,3},{5,6},{6,5},{7,8},{8,7},{9,10},{10,9},{11,... | collective-permute-start | bytes 49160 | tf_op jit(solution)/shard_map/ppermute | solution.py:375
  29.9 5.6 %collective-permute-start.3 = (f32[4,8,128]{2,1,0:T(8,128)S(1)}, f32[4,8,128]{2,1,0:T(8,128)S(1)}, u32[]{:S(2)}, u32[]{:S(2)}) collective-permute-start(f32[4,8,128]{2,1,0:T(8,128)S(1)} %get-tuple-element.31), channel_id=1, source_target_pairs={{0,1},{1,0},{2,3},{3,2},{4,5},{5,4},{6,7},{7,6},{8,9},{9,8},{10,11... | collective-permute-start | bytes 49160 | tf_op jit(solution)/shard_map/ppermute | solution.py:376
  35.5 6.2 %collective-permute-start.5 = (f32[16,8,128]{2,1,0:T(8,128)S(1)}, f32[16,8,128]{2,1,0:T(8,128)S(1)}, u32[]{:S(2)}, u32[]{:S(2)}) collective-permute-start(f32[16,8,128]{2,1,0:T(8,128)S(1)} %get-tuple-element.38), channel_id=1, source_target_pairs={{0,16},{16,0},{32,48},{48,32},{64,80},{80,64},{96,112},{112,96},{1... | collective-permute-start | bytes 196616 | tf_op jit(solution)/shard_map/ppermute | solution.py:386
  38.9 6.2 %collective-permute-start.6 = (f32[16,8,128]{2,1,0:T(8,128)S(1)}, f32[16,8,128]{2,1,0:T(8,128)S(1)}, u32[]{:S(2)}, u32[]{:S(2)}) collective-permute-start(f32[16,8,128]{2,1,0:T(8,128)S(1)} %get-tuple-element.39), channel_id=1, source_target_pairs={{16,32},{32,16},{48,64},{64,48},{80,96},{96,80},{17,33},{33,17},{4... | collective-permute-start | bytes 196616 | tf_op jit(solution)/shard_map/ppermute | solution.py:385

commit v7 on v6

--- a/solution.py
+++ b/solution.py
@@ -153,16 +153,22 @@
     return packed
 
 
-def second_kernel(v_ref, w_ref, v1_ref, w1_ref, v2_ref, w2_ref, al_ref, ah_ref, b_ref, z_ref, ya_ref, yb_ref):
+def second_kernel(v_ref, w_ref, v1_ref, w1_ref, v2_ref, w2_ref, al_ref, ah_ref, b_ref, z_ref):
+    level0, level1, level2 = extended(
+        lax.axis_index("gx"), v_ref, w_ref, v1_ref, w1_ref, v2_ref, w2_ref, al_ref, ah_ref, b_ref
+    )
+    ends = edge_lanes(level0[1:13])
+    for i, tile in enumerate((ends[0:8], ends[8:16], edge_lanes(level1[1:9]), edge_lanes(level2[1:7]))):
+        z_ref[i] = tile
+
+
+def faces_kernel(v_ref, w_ref, v1_ref, w1_ref, v2_ref, w2_ref, al_ref, ah_ref, b_ref, ya_ref, yb_ref):
     gx, gy = lax.axis_index("gx"), lax.axis_index("gy")
     level0, level1, level2 = extended(gx, v_ref, w_ref, v1_ref, w1_ref, v2_ref, w2_ref, al_ref, ah_ref, b_ref)
     lane, row = lanes(), rows()
     low = lane < 64
     quad = (lane & 63) < 32
     up = (gy & 1) == 0
-    ends = edge_lanes(level0[1:13])
-    for i, tile in enumerate((ends[0:8], ends[8:16], edge_lanes(level1[1:9]), edge_lanes(level2[1:7]))):
-        z_ref[i] = tile
     for k in range(12):
         v, w = level0[k + 1]
         if k < 8:
@@ -364,13 +370,21 @@
     s_in = lax.all_to_all(s_out, ("gx", "gy"), 0, 0, tiled=True, axis_index_groups=[ring])
     ah_in = lax.ppermute(a_out, "gx", even(nx)[nx // 2 :])
     limit = pltpu.CompilerParams(vmem_limit_bytes=8 << 20)
-    z_out, ya_own, yb_own = call(
+    z_out = call(
         second_kernel,
-        out_shape=[shape((4, 8, 128), F32)] + [shape((12, 8, 128), F32)] * 2,
+        out_shape=shape((4, 8, 128), F32),
         in_specs=[VMEM] * 9,
-        out_specs=[VMEM] * 3,
+        out_specs=VMEM,
         compiler_params=limit,
         name="second",
+    )(*own, al_in, ah_in, b_in)
+    ya_own, yb_own = call(
+        faces_kernel,
+        out_shape=[shape((12, 8, 128), F32)] * 2,
+        in_specs=[VMEM] * 9,
+        out_specs=[VMEM] * 2,
+        compiler_params=limit,
+        name="faces",
     )(*own, al_in, ah_in, b_in)
     zb_in = lax.ppermute(z_out, "gz", odd(nz))
     za_in = lax.ppermute(z_out, "gz", even(nz))

time: 46.9 us -> 46.9 us (level)
  no operation moved by 1% of the time
where the time goes in v7:
time: 46.9 us; the launch traced here: 46.5 us
  starting transfers between devices  35.5 us (76%)
  waiting for transfers between devices  7.23 us (15%)
  Pallas kernels  2.84 us (6%)
  other arithmetic  0.88 us (2%)
    ppermute x1, starting transfers between devices, per_device(): al_in = lax.ppermute(a_out, 'gx', even(nx)[:nx // 2])  16.2 us
    ppermute x1, starting transfers between devices, per_device(): zb_in = lax.ppermute(z_out, 'gz', odd(nz))  5.19 us
    all_to_all x1, starting transfers between devices, per_device(): lax.all_to_all(s_out, ('gx', 'gy'), 0, 0, tiled=True, axis_index_groups=[...  5.11 us
    ppermute x1, waiting for transfers between devices, per_device(): yb_in = lax.ppermute(yb_out, 'gy', odd(ny))  3.36 us
    ppermute x1, starting transfers between devices, per_device(): ya_in = lax.ppermute(ya_out, 'gy', even(ny))  3.36 us
    ppermute x1, waiting for transfers between devices, per_device(): za_in = lax.ppermute(z_out, 'gz', even(nz))  3.09 us
    ppermute x1, starting transfers between devices, per_device(): yb_in = lax.ppermute(yb_out, 'gy', odd(ny))  2.39 us
    ppermute x1, starting transfers between devices, per_device(): za_in = lax.ppermute(z_out, 'gz', even(nz))  1.92 us
  transfers between devices with their start and end apart: 8, of which 4 were waited for; matrix products, arithmetic and copies ran while one was open for 0% of the time, Pallas kernels for 1%

profile of v7, /device:TPU:38, one launch (start us, length us, event | category | flops | bytes accessed | tf_op | source)
XLA Modules:
  0.0 46.5 jit_solution(3064117311211140986)
XLA Ops:
  0.0 0.9 %pad_maximum_fusion.in_ref = f32[2,8,16,128]{3,2,1,0:T(8,128)S(1)} fusion(f32[1,8,16,128]{3,2,1,0:T(8,128)} %bitcast.2, f32[1,8,16,128]{3,2,1,0:T(8,128)} %bitcast.3), kind=kLoop, calls=%fused_computation | loop fusion | flops 32768 | bytes 262144 | tf_op jit(solution)/shard_map/stack | solution.py:364
  0.9 0.9 %first.1 = (f32[14,8,128]{2,1,0:T(8,128)S(1)}, f32[14,8,128]{2,1,0:T(8,128)S(1)}, f32[32,2,128]{2,1,0:T(2,128)}, f32[8,16,128]{2,1,0:T(8,128)S(1)}, f32[8,16,128...) custom-call(f32[2,8,16,128]{3,2,1,0:T(8,128)S(1)} %pad_maximum_fusio, ...), custom_call_target="tpu_custom_call" | custom-call | tf_op jit(solution)/shard_map/first/pallas_call | solution.py:356
  1.8 0.7 %collective-permute-start.2 = (f32[14,8,128]{2,1,0:T(8,128)S(1)}, f32[14,8,128]{2,1,0:T(8,128)S(1)}, u32[]{:S(2)}, u32[]{:S(2)}) collective-permute-start(f32[14,8,128]{2,1,0:T(8,128)S(1)} %get-tuple-element.29), channel_id=1, source_target_pairs={{128,256},{256,128},{129,257},{257,129},{130,258},{258,130},{131,2... | collective-permute-start | bytes 172040 | tf_op jit(solution)/shard_map/ppermute | solution.py:368
  2.5 0.7 %collective-permute-start.1 = (f32[14,8,128]{2,1,0:T(8,128)S(1)}, f32[14,8,128]{2,1,0:T(8,128)S(1)}, u32[]{:S(2)}, u32[]{:S(2)}) collective-permute-start(f32[14,8,128]{2,1,0:T(8,128)S(1)} %get-tuple-element.28), channel_id=1, source_target_pairs={{256,384},{384,256},{257,385},{385,257},{258,386},{386,258},{259,3... | collective-permute-start | bytes 172040 | tf_op jit(solution)/shard_map/ppermute | solution.py:371
  3.1 16.2 %collective-permute-start = (f32[14,8,128]{2,1,0:T(8,128)S(1)}, f32[14,8,128]{2,1,0:T(8,128)S(1)}, u32[]{:S(2)}, u32[]{:S(2)}) collective-permute-start(f32[14,8,128]{2,1,0:T(8,128)S(1)} %get-tuple-element.28), channel_id=1, source_target_pairs={{0,128},{128,0},{1,129},{129,1},{2,130},{130,2},{3,131},{131,3},{4... | collective-permute-start | bytes 172040 | tf_op jit(solution)/shard_map/ppermute | solution.py:367
  19.3 5.1 %all-to-all-start = ((f32[32,2,128]{2,1,0:T(2,128)}), f32[32,2,128]{2,1,0:T(2,128)S(1)}, u32[]{:S(2)}, u32[]{:S(2)}) async-start(f32[32,2,128]{2,1,0:T(2,128)} %get-tuple-element.38), calls=%async_computation | async-start | bytes 65536 | tf_op jit(solution)/shard_map/all_to_all | solution.py:370
  24.4 0.0 collective-permute-done.2.b_ref
  24.5 0.0 collective-permute-done.1.ah_ref
  24.5 0.0 collective-permute-done.al_ref
  24.5 0.2 second.1
  24.7 5.2 %collective-permute-start.4 = (f32[4,8,128]{2,1,0:T(8,128)S(1)}, f32[4,8,128]{2,1,0:T(8,128)S(1)}, u32[]{:S(2)}, u32[]{:S(2)}) collective-permute-start(f32[4,8,128]{2,1,0:T(8,128)S(1)} %second.1), channel_id=1, source_target_pairs={{1,2},{2,1},{3,4},{4,3},{5,6},{6,5},{7,8},{8,7},{9,10},{10,9},{11,... | collective-permute-start | bytes 49160 | tf_op jit(solution)/shard_map/ppermute | solution.py:389
  29.9 1.9 %collective-permute-start.3 = (f32[4,8,128]{2,1,0:T(8,128)S(1)}, f32[4,8,128]{2,1,0:T(8,128)S(1)}, u32[]{:S(2)}, u32[]{:S(2)}) collective-permute-start(f32[4,8,128]{2,1,0:T(8,128)S(1)} %second.1), channel_id=1, source_target_pairs={{0,1},{1,0},{2,3},{3,2},{4,5},{5,4},{6,7},{7,6},{8,9},{9,8},{10,11... | collective-permute-start | bytes 49160 | tf_op jit(solution)/shard_map/ppermute | solution.py:390
  31.8 0.6 %collective-permute-done.4.zb_ref = f32[4,8,128]{2,1,0:T(8,128)S(1)} collective-permute-done((f32[4,8,128]{2,1,0:T(8,128)S(1)}, f32[4,8,128]{2,1,0:T(8,128)S(1)}, u32[]{:S(2)}, u32[]{:S(2)}) %collective-permute-start.4) | collective-permute-done | bytes 16416 | tf_op jit(solution)/shard_map/ppermute | solution.py:389
  32.4 3.1 %collective-permute-done.3.za_ref = f32[4,8,128]{2,1,0:T(8,128)S(1)} collective-permute-done((f32[4,8,128]{2,1,0:T(8,128)S(1)}, f32[4,8,128]{2,1,0:T(8,128)S(1)}, u32[]{:S(2)}, u32[]{:S(2)}) %collective-permute-start.3) | collective-permute-done | bytes 16416 | tf_op jit(solution)/shard_map/ppermute | solution.py:390
  35.5 3.4 %collective-permute-start.5 = (f32[16,8,128]{2,1,0:T(8,128)S(1)}, f32[16,8,128]{2,1,0:T(8,128)S(1)}, u32[]{:S(2)}, u32[]{:S(2)}) collective-permute-start(f32[16,8,128]{2,1,0:T(8,128)S(1)} %get-tuple-element.36), channel_id=1, source_target_pairs={{0,16},{16,0},{32,48},{48,32},{64,80},{80,64},{96,112},{112,96},{1... | collective-permute-start | bytes 196616 | tf_op jit(solution)/shard_map/ppermute | solution.py:400
  38.9 2.4 %collective-permute-start.6 = (f32[16,8,128]{2,1,0:T(8,128)S(1)}, f32[16,8,128]{2,1,0:T(8,128)S(1)}, u32[]{:S(2)}, u32[]{:S(2)}) collective-permute-start(f32[16,8,128]{2,1,0:T(8,128)S(1)} %get-tuple-element.37), channel_id=1, source_target_pairs={{16,32},{32,16},{48,64},{64,48},{80,96},{96,80},{17,33},{33,17},{4... | collective-permute-start | bytes 196616 | tf_op jit(solution)/shard_map/ppermute | solution.py:399
  41.3 0.2 fourth.1
  41.5 0.0 all-to-all-done.s_ref
  41.5 0.2 collective-permute-done.5.ya_ref
  41.7 3.4 %collective-permute-done.6.yb_ref = f32[16,8,128]{2,1,0:T(8,128)S(1)} collective-permute-done((f32[16,8,128]{2,1,0:T(8,128)S(1)}, f32[16,8,128]{2,1,0:T(8,128)S(1)}, u32[]{:S(2)}, u32[]{:S(2)}) %collective-permute-start.6) | collective-permute-done | bytes 65568 | tf_op jit(solution)/shard_map/ppermute | solution.py:399
  45.0 1.5 %last.1 = f32[8,16,128]{2,1,0:T(8,128)} custom-call(f32[8,16,128]{2,1,0:T(8,128)S(1)} %get-tuple-element.22.v_ref, f32[8,16,128]{2,1,0:T(8,128)S(1)} %get-tuple-element.23.w_ref, f32[4,8,128]{2,1,0:T(8,128)S(1)} %get-tuple-element.24.v1_ref, f32[4,8,128]{2,1,0:T(8,128)S(1)} %get-tuple-element.25.w1_ref, f32[2,8,128]{2,1,0:T(8,128)S(1)} %get-tuple-element.26.v2_ref, ...), custom_call_target="tpu_custom_call" | custom-call | tf_op jit(solution)/shard_map/last/pallas_call | solution.py:412
  (2 shorter events, 0.1 us)
Async XLA Ops:
  1.8 22.6 %collective-permute-start.2 = (f32[14,8,128]{2,1,0:T(8,128)S(1)}, f32[14,8,128]{2,1,0:T(8,128)S(1)}, u32[]{:S(2)}, u32[]{:S(2)}) collective-permute-start(f32[14,8,128]{2,1,0:T(8,128)S(1)} %get-tuple-element.29), channel_id=1, source_target_pairs={{128,256},{256,128},{129,257},{257,129},{130,258},{258,130},{131,2... | collective-permute-start | bytes 172040 | tf_op jit(solution)/shard_map/ppermute | solution.py:368
  2.5 22.0 %collective-permute-start.1 = (f32[14,8,128]{2,1,0:T(8,128)S(1)}, f32[14,8,128]{2,1,0:T(8,128)S(1)}, u32[]{:S(2)}, u32[]{:S(2)}) collective-permute-start(f32[14,8,128]{2,1,0:T(8,128)S(1)} %get-tuple-element.28), channel_id=1, source_target_pairs={{256,384},{384,256},{257,385},{385,257},{258,386},{386,258},{259,3... | collective-permute-start | bytes 172040 | tf_op jit(solution)/shard_map/ppermute | solution.py:371
  3.1 21.3 %collective-permute-start = (f32[14,8,128]{2,1,0:T(8,128)S(1)}, f32[14,8,128]{2,1,0:T(8,128)S(1)}, u32[]{:S(2)}, u32[]{:S(2)}) collective-permute-start(f32[14,8,128]{2,1,0:T(8,128)S(1)} %get-tuple-element.28), channel_id=1, source_target_pairs={{0,128},{128,0},{1,129},{129,1},{2,130},{130,2},{3,131},{131,3},{4... | collective-permute-start | bytes 172040 | tf_op jit(solution)/shard_map/ppermute | solution.py:367
  19.3 22.1 %all-to-all-start = ((f32[32,2,128]{2,1,0:T(2,128)}), f32[32,2,128]{2,1,0:T(2,128)S(1)}, u32[]{:S(2)}, u32[]{:S(2)}) async-start(f32[32,2,128]{2,1,0:T(2,128)} %get-tuple-element.38), calls=%async_computation | async-start | bytes 65536 | tf_op jit(solution)/shard_map/all_to_all | solution.py:370
  24.7 7.7 %collective-permute-start.4 = (f32[4,8,128]{2,1,0:T(8,128)S(1)}, f32[4,8,128]{2,1,0:T(8,128)S(1)}, u32[]{:S(2)}, u32[]{:S(2)}) collective-permute-start(f32[4,8,128]{2,1,0:T(8,128)S(1)} %second.1), channel_id=1, source_target_pairs={{1,2},{2,1},{3,4},{4,3},{5,6},{6,5},{7,8},{8,7},{9,10},{10,9},{11,... | collective-permute-start | bytes 49160 | tf_op jit(solution)/shard_map/ppermute | solution.py:389
  29.9 5.6 %collective-permute-start.3 = (f32[4,8,128]{2,1,0:T(8,128)S(1)}, f32[4,8,128]{2,1,0:T(8,128)S(1)}, u32[]{:S(2)}, u32[]{:S(2)}) collective-permute-start(f32[4,8,128]{2,1,0:T(8,128)S(1)} %second.1), channel_id=1, source_target_pairs={{0,1},{1,0},{2,3},{3,2},{4,5},{5,4},{6,7},{7,6},{8,9},{9,8},{10,11... | collective-permute-start | bytes 49160 | tf_op jit(solution)/shard_map/ppermute | solution.py:390
  35.5 6.2 %collective-permute-start.5 = (f32[16,8,128]{2,1,0:T(8,128)S(1)}, f32[16,8,128]{2,1,0:T(8,128)S(1)}, u32[]{:S(2)}, u32[]{:S(2)}) collective-permute-start(f32[16,8,128]{2,1,0:T(8,128)S(1)} %get-tuple-element.36), channel_id=1, source_target_pairs={{0,16},{16,0},{32,48},{48,32},{64,80},{80,64},{96,112},{112,96},{1... | collective-permute-start | bytes 196616 | tf_op jit(solution)/shard_map/ppermute | solution.py:400
  38.9 6.2 %collective-permute-start.6 = (f32[16,8,128]{2,1,0:T(8,128)S(1)}, f32[16,8,128]{2,1,0:T(8,128)S(1)}, u32[]{:S(2)}, u32[]{:S(2)}) collective-permute-start(f32[16,8,128]{2,1,0:T(8,128)S(1)} %get-tuple-element.37), channel_id=1, source_target_pairs={{16,32},{32,16},{48,64},{64,48},{80,96},{96,80},{17,33},{33,17},{4... | collective-permute-start | bytes 196616 | tf_op jit(solution)/shard_map/ppermute | solution.py:399

commit v8 on v6

--- a/solution.py
+++ b/solution.py
@@ -224,11 +224,31 @@
 
 
 def fourth_kernel(
-    v_ref, w_ref, v1_ref, w1_ref, v2_ref, w2_ref, al_ref, ah_ref, b_ref, za_ref, zb_ref, fv, fw, mv, mw
+    nx, ny, v_ref, w_ref, v1_ref, w1_ref, v2_ref, w2_ref, al_ref, ah_ref, b_ref, za_ref, zb_ref, s_ref,
+    fv, fw, mv, mw, cv, cw, plane_ref,
 ):
-    level0, level1, _ = extended(
-        lax.axis_index("gx"), v_ref, w_ref, v1_ref, w1_ref, v2_ref, w2_ref, al_ref, ah_ref, b_ref
-    )
+    gx, gy = lax.axis_index("gx"), lax.axis_index("gy")
+    row = rows()
+
+    def far(slot, have):
+        chips = nx * ny // 2
+        place = lax.rem((slot >> 1) * ny + gy + chips - FIRST_CHIP, chips)
+        t = jnp.broadcast_to(s_ref[2 * place + 1 - (slot & 1), 1:2], (8, 128))
+        spread = jnp.zeros((8, 128), F32)
+        for i in range(4):
+            spread = jnp.where(row == i, turn(t, -32 * i, 1), spread)
+        return jnp.where(have, spread, 0.0)
+
+    outer_layers = far(jnp.maximum(gx - 2, 0), gx > 1), far(jnp.minimum(gx + 2, nx - 1), gx < nx - 2)
+    level0, level1, level2 = extended(
+        gx, v_ref, w_ref, v1_ref, w1_ref, v2_ref, w2_ref, al_ref, ah_ref, b_ref, outer_layers
+    )
+    for i in range(8):
+        cv[i] = level2[i][0]
+        if 1 <= i < 7:
+            cw[i] = level2[i][1]
+    s = jnp.sum(s_ref[...], axis=0)[0:1]
+    plane_ref[...] = jnp.where(lanes() < 64, s / (turn(jnp.broadcast_to(s, (8, 128)), 64, 1) + 16.0), 0.0)
     own = [both_ends(i, za_ref, zb_ref) for i in range(3)]
     z0, lane = jnp.concatenate(own[0:2], axis=0), lanes()
     for i in range(14):
@@ -250,27 +270,11 @@
 
 
 def last_kernel(
-    nx, ny, v_ref, w_ref, v1_ref, w1_ref, v2_ref, w2_ref, al_ref, ah_ref, b_ref, za_ref, zb_ref,
-    fv_ref, fw_ref, mv_ref, mw_ref, ya_ref, yb_ref, s_ref, out_ref,
+    za_ref, zb_ref, fv_ref, fw_ref, mv_ref, mw_ref, cv_ref, cw_ref, plane_ref, ya_ref, yb_ref, out_ref,
     fv, fw, fa, fb, mv, mw, ma, mb, cv, cw, ca, cb, wide_ref, deep_ref,
 ):
-    gx, gy = lax.axis_index("gx"), lax.axis_index("gy")
-    up = (gy & 1) == 0
+    up = (lax.axis_index("gy") & 1) == 0
     lane, row = lanes(), rows()
-
-    def far(slot, have):
-        chips = nx * ny // 2
-        place = lax.rem((slot >> 1) * ny + gy + chips - FIRST_CHIP, chips)
-        t = jnp.broadcast_to(s_ref[2 * place + 1 - (slot & 1), 1:2], (8, 128))
-        spread = jnp.zeros((8, 128), F32)
-        for i in range(4):
-            spread = jnp.where(row == i, turn(t, -32 * i, 1), spread)
-        return jnp.where(have, spread, 0.0)
-
-    outer_layers = far(jnp.maximum(gx - 2, 0), gx > 1), far(jnp.minimum(gx + 2, nx - 1), gx < nx - 2)
-    _, _, level2 = extended(
-        gx, v_ref, w_ref, v1_ref, w1_ref, v2_ref, w2_ref, al_ref, ah_ref, b_ref, outer_layers
-    )
 
     def sides(k):
         a, b = ya_ref[k], yb_ref[k]
@@ -307,7 +311,7 @@
             near, far = turn(p, 7, 0), turn(m, 5, 0)
             for i in (0, 1):
                 j = 2 * (k - 8) + i
-                v, w = level2[j + 1]
+                v, w = cv_ref[j + 1], cw_ref[j + 1]
                 for field, target in ((0, cv), (1, cw)):
                     shift = -(64 * i + 32 * field)
                     top = jnp.where(row < 4, (v, w)[field], turn(near, shift, 1))
@@ -316,17 +320,15 @@
                     ends = jnp.where(lane16 < 64, turn(z2, 32 - at, 1), turn(z2, -at, 1))
                     target[j + 1] = jnp.where(lane16 < 32, full, ends)
     for i in (0, 7):
-        cv[i, 0:8] = level2[i][0]
+        cv[i, 0:8] = cv_ref[i]
         cv[i, 8:16] = none
 
     joined = lambda near_ref, far_ref: lambda i: jnp.concatenate([near_ref[i], far_ref[i]], axis=0)
     coarse = relaxed(lambda i: cv[i], lambda i: cw[i], ca, cb, 8)
-    s = jnp.sum(s_ref[...], axis=0)[0:1]
-    plane = jnp.where(lane < 64, s / (turn(jnp.broadcast_to(s, (8, 128)), 64, 1) + 16.0), 0.0)
     src, dst = rows((128, 128)), lanes((128, 128))
     spread4 = jnp.where(src == (dst >> 2), 1.0, 0.0).astype(F32)
     spread2 = jnp.where(src == (dst >> 1), 1.0, 0.0).astype(F32)
-    c = jnp.concatenate([layer[0:8] + plane for layer in coarse], axis=0)
+    c = jnp.concatenate([layer[0:8] + plane_ref[...] for layer in coarse], axis=0)
     c = jnp.dot(c, spread4, precision=HIGHEST, preferred_element_type=F32).reshape(2, 8, 128)
     middle = relaxed(joined(mv_ref, mv), joined(mw_ref, mw), ma, mb, 10)
     m = jnp.concatenate([layer[0:8] for layer in middle], axis=0)
@@ -385,26 +387,27 @@
     yb_in = lax.ppermute(yb_out, "gy", odd(ny))
     ya_in = lax.ppermute(ya_out, "gy", even(ny))
     rows_own = call(
-        fourth_kernel,
-        out_shape=[shape((14, 16, 256), F32)] * 2 + [shape((10, 8, 128), F32)] * 2,
-        in_specs=[VMEM] * 11,
-        out_specs=[VMEM] * 4,
+        functools.partial(fourth_kernel, nx, ny),
+        out_shape=[shape((14, 16, 256), F32)] * 2 + [shape((10, 8, 128), F32)] * 2
+        + [shape((8, 8, 128), F32)] * 2 + [shape((8, 128), F32)],
+        in_specs=[VMEM] * 12,
+        out_specs=[VMEM] * 7,
         compiler_params=limit,
         name="fourth",
-    )(*own, al_in, ah_in, b_in, za_in, zb_in)
+    )(*own, al_in, ah_in, b_in, za_in, zb_in, s_in)
     edge, fine, thin, middle, coarse = (
         pltpu.VMEM(s, F32) for s in ((14, 8, 256), (14, 24, 256), (10, 8, 128), (10, 16, 128), (8, 16, 128))
     )
     return call(
-        functools.partial(last_kernel, nx, ny),
+        last_kernel,
         out_shape=shape((8, 16, 128), F32),
-        in_specs=[VMEM] * 18,
+        in_specs=[VMEM] * 11,
         out_specs=VMEM,
         scratch_shapes=[edge] * 2 + [fine] * 2 + [thin] * 2 + [middle] * 2 + [coarse] * 4
         + [pltpu.VMEM((4, 16, 128), F32), pltpu.VMEM((2, 8, 128), F32)],
         compiler_params=limit,
         name="last",
-    )(*own, al_in, ah_in, b_in, za_in, zb_in, *rows_own, ya_in, yb_in, s_in)
+    )(za_in, zb_in, *rows_own, ya_in, yb_in)
 
 
 def solution(mesh):

time: 46.9 us -> 46.9 us (level)
    ppermute x1, starting transfers between devices: 16.2 us -> 1.91 us  [per_device(): al_in = lax.ppermute(a_out, 'gx', even(nx)[:nx // 2])]
    all_to_all x1, starting transfers between devices: 5.11 us -> 19 us  [per_device(): lax.all_to_all(s_out, ('gx', 'gy'), 0, 0, tiled=True, axis_index_groups=[...]
    ppermute x1, waiting for transfers between devices: 3.09 us -> 0.01 us  [per_device(): za_in = lax.ppermute(z_out, 'gz', even(nz))]
    ppermute x1, waiting for transfers between devices: 0.62 us -> 3.37 us  [per_device(): zb_in = lax.ppermute(z_out, 'gz', odd(nz))]
    ppermute x1, starting transfers between devices: 1.92 us -> 3.48 us  [per_device(): za_in = lax.ppermute(z_out, 'gz', even(nz))]
    ppermute x1, starting transfers between devices: 5.19 us -> 4.35 us  [per_device(): zb_in = lax.ppermute(z_out, 'gz', odd(nz))]
  transfers between devices with their start and end apart: 8 -> 8, of which waited for: 4 -> 3; matrix products, arithmetic and copies ran while one was open for 0% -> 0% of each run, Pallas kernels for 1% -> 1%
where the time goes in v8:
time: 46.9 us; the launch traced here: 46.6 us
  starting transfers between devices  35.8 us (76%)
  waiting for transfers between devices  6.93 us (15%)
  Pallas kernels  2.8 us (6%)
  other arithmetic  0.88 us (2%)
    all_to_all x1, starting transfers between devices, per_device(): lax.all_to_all(s_out, ('gx', 'gy'), 0, 0, tiled=True, axis_index_groups=[...  19 us
    ppermute x1, starting transfers between devices, per_device(): zb_in = lax.ppermute(z_out, 'gz', odd(nz))  4.35 us
    ppermute x1, starting transfers between devices, per_device(): za_in = lax.ppermute(z_out, 'gz', even(nz))  3.48 us
    ppermute x1, waiting for transfers between devices, per_device(): zb_in = lax.ppermute(z_out, 'gz', odd(nz))  3.37 us
    ppermute x1, waiting for transfers between devices, per_device(): yb_in = lax.ppermute(yb_out, 'gy', odd(ny))  3.36 us
    ppermute x1, starting transfers between devices, per_device(): ya_in = lax.ppermute(ya_out, 'gy', even(ny))  3.36 us
    ppermute x1, starting transfers between devices, per_device(): yb_in = lax.ppermute(yb_out, 'gy', odd(ny))  2.39 us
    ppermute x1, starting transfers between devices, per_device(): al_in = lax.ppermute(a_out, 'gx', even(nx)[:nx // 2])  1.91 us
  transfers between devices with their start and end apart: 8, of which 3 were waited for; matrix products, arithmetic and copies ran while one was open for 0% of the time, Pallas kernels for 1%

profile of v8, /device:TPU:38, one launch (start us, length us, event | category | flops | bytes accessed | tf_op | source)
XLA Modules:
  0.0 46.6 jit_solution(14422067348785681939)
XLA Ops:
  0.0 0.9 %pad_maximum_fusion.in_ref = f32[2,8,16,128]{3,2,1,0:T(8,128)S(1)} fusion(f32[1,8,16,128]{3,2,1,0:T(8,128)} %bitcast.2, f32[1,8,16,128]{3,2,1,0:T(8,128)} %bitcast.3), kind=kLoop, calls=%fused_computation | loop fusion | flops 32768 | bytes 262144 | tf_op jit(solution)/shard_map/stack | solution.py:360
  0.9 0.9 %first.1 = (f32[14,8,128]{2,1,0:T(8,128)S(1)}, f32[14,8,128]{2,1,0:T(8,128)S(1)}, f32[32,2,128]{2,1,0:T(2,128)}, f32[8,16,128]{2,1,0:T(8,128)S(1)}, f32[8,16,128...) custom-call(f32[2,8,16,128]{3,2,1,0:T(8,128)S(1)} %pad_maximum_fusio, ...), custom_call_target="tpu_custom_call" | custom-call | tf_op jit(solution)/shard_map/first/pallas_call | solution.py:352
  1.8 1.9 %collective-permute-start = (f32[14,8,128]{2,1,0:T(8,128)S(1)}, f32[14,8,128]{2,1,0:T(8,128)S(1)}, u32[]{:S(2)}, u32[]{:S(2)}) collective-permute-start(f32[14,8,128]{2,1,0:T(8,128)S(1)} %get-tuple-element.32), channel_id=1, source_target_pairs={{0,128},{128,0},{1,129},{129,1},{2,130},{130,2},{3,131},{131,3},{4... | collective-permute-start | bytes 172040 | tf_op jit(solution)/shard_map/ppermute | solution.py:363
  3.7 0.7 %collective-permute-start.1 = (f32[14,8,128]{2,1,0:T(8,128)S(1)}, f32[14,8,128]{2,1,0:T(8,128)S(1)}, u32[]{:S(2)}, u32[]{:S(2)}) collective-permute-start(f32[14,8,128]{2,1,0:T(8,128)S(1)} %get-tuple-element.32), channel_id=1, source_target_pairs={{256,384},{384,256},{257,385},{385,257},{258,386},{386,258},{259,3... | collective-permute-start | bytes 172040 | tf_op jit(solution)/shard_map/ppermute | solution.py:367
  4.4 0.7 %collective-permute-start.2 = (f32[14,8,128]{2,1,0:T(8,128)S(1)}, f32[14,8,128]{2,1,0:T(8,128)S(1)}, u32[]{:S(2)}, u32[]{:S(2)}) collective-permute-start(f32[14,8,128]{2,1,0:T(8,128)S(1)} %get-tuple-element.33), channel_id=1, source_target_pairs={{128,256},{256,128},{129,257},{257,129},{130,258},{258,130},{131,2... | collective-permute-start | bytes 172040 | tf_op jit(solution)/shard_map/ppermute | solution.py:364
  5.1 19.0 %all-to-all-start = ((f32[32,2,128]{2,1,0:T(2,128)}), f32[32,2,128]{2,1,0:T(2,128)S(1)}, u32[]{:S(2)}, u32[]{:S(2)}) async-start(f32[32,2,128]{2,1,0:T(2,128)} %get-tuple-element.35), calls=%async_computation | async-start | bytes 65536 | tf_op jit(solution)/shard_map/all_to_all | solution.py:366
  24.1 0.0 collective-permute-done.al_ref
  24.1 0.0 collective-permute-done.1.ah_ref
  24.1 0.0 collective-permute-done.2.b_ref
  24.1 0.2 second.1
  24.3 3.5 %collective-permute-start.3 = (f32[4,8,128]{2,1,0:T(8,128)S(1)}, f32[4,8,128]{2,1,0:T(8,128)S(1)}, u32[]{:S(2)}, u32[]{:S(2)}) collective-permute-start(f32[4,8,128]{2,1,0:T(8,128)S(1)} %get-tuple-element.34), channel_id=1, source_target_pairs={{0,1},{1,0},{2,3},{3,2},{4,5},{5,4},{6,7},{7,6},{8,9},{9,8},{10,11... | collective-permute-start | bytes 49160 | tf_op jit(solution)/shard_map/ppermute | solution.py:378
  27.8 4.4 %collective-permute-start.4 = (f32[4,8,128]{2,1,0:T(8,128)S(1)}, f32[4,8,128]{2,1,0:T(8,128)S(1)}, u32[]{:S(2)}, u32[]{:S(2)}) collective-permute-start(f32[4,8,128]{2,1,0:T(8,128)S(1)} %get-tuple-element.34), channel_id=1, source_target_pairs={{1,2},{2,1},{3,4},{4,3},{5,6},{6,5},{7,8},{8,7},{9,10},{10,9},{11,... | collective-permute-start | bytes 49160 | tf_op jit(solution)/shard_map/ppermute | solution.py:377
  32.1 0.0 collective-permute-done.3.za_ref
  32.1 3.4 %collective-permute-done.4.zb_ref = f32[4,8,128]{2,1,0:T(8,128)S(1)} collective-permute-done((f32[4,8,128]{2,1,0:T(8,128)S(1)}, f32[4,8,128]{2,1,0:T(8,128)S(1)}, u32[]{:S(2)}, u32[]{:S(2)}) %collective-permute-start.4) | collective-permute-done | bytes 16416 | tf_op jit(solution)/shard_map/ppermute | solution.py:377
  35.5 3.4 %collective-permute-start.5 = (f32[16,8,128]{2,1,0:T(8,128)S(1)}, f32[16,8,128]{2,1,0:T(8,128)S(1)}, u32[]{:S(2)}, u32[]{:S(2)}) collective-permute-start(f32[16,8,128]{2,1,0:T(8,128)S(1)} %get-tuple-element.45), channel_id=1, source_target_pairs={{0,16},{16,0},{32,48},{48,32},{64,80},{80,64},{96,112},{112,96},{1... | collective-permute-start | bytes 196616 | tf_op jit(solution)/shard_map/ppermute | solution.py:388
  38.9 2.4 %collective-permute-start.6 = (f32[16,8,128]{2,1,0:T(8,128)S(1)}, f32[16,8,128]{2,1,0:T(8,128)S(1)}, u32[]{:S(2)}, u32[]{:S(2)}) collective-permute-start(f32[16,8,128]{2,1,0:T(8,128)S(1)} %get-tuple-element.46), channel_id=1, source_target_pairs={{16,32},{32,16},{48,64},{64,48},{80,96},{96,80},{17,33},{33,17},{4... | collective-permute-start | bytes 196616 | tf_op jit(solution)/shard_map/ppermute | solution.py:387
  41.3 0.0 all-to-all-done.s_ref
  41.3 0.2 fourth.1
  41.5 0.2 collective-permute-done.5.ya_ref
  41.7 3.4 %collective-permute-done.6.yb_ref = f32[16,8,128]{2,1,0:T(8,128)S(1)} collective-permute-done((f32[16,8,128]{2,1,0:T(8,128)S(1)}, f32[16,8,128]{2,1,0:T(8,128)S(1)}, u32[]{:S(2)}, u32[]{:S(2)}) %collective-permute-start.6) | collective-permute-done | bytes 65568 | tf_op jit(solution)/shard_map/ppermute | solution.py:387
  45.1 1.5 %last.1 = f32[8,16,128]{2,1,0:T(8,128)} custom-call(f32[4,8,128]{2,1,0:T(8,128)S(1)} %collective-permute-done.3.za_ref, f32[4,8,128]{2,1,0:T(8,128)S(1)} %collective-permute-done.4.zb_ref, f32[14,16,256]{2,1,0:T(8,128)S(1)} %get-tuple-element.36.fv_ref, f32[14,16,256]{2,1,0:T(8,128)S(1)} %get-tuple-element.37.fw_ref, ...), custom_call_target="tpu_custom_call" | custom-call | tf_op jit(solution)/shard_map/last/pallas_call | solution.py:401
  (1 shorter events, 0.0 us)
Async XLA Ops:
  1.8 22.3 %collective-permute-start = (f32[14,8,128]{2,1,0:T(8,128)S(1)}, f32[14,8,128]{2,1,0:T(8,128)S(1)}, u32[]{:S(2)}, u32[]{:S(2)}) collective-permute-start(f32[14,8,128]{2,1,0:T(8,128)S(1)} %get-tuple-element.32), channel_id=1, source_target_pairs={{0,128},{128,0},{1,129},{129,1},{2,130},{130,2},{3,131},{131,3},{4... | collective-permute-start | bytes 172040 | tf_op jit(solution)/shard_map/ppermute | solution.py:363
  3.7 20.4 %collective-permute-start.1 = (f32[14,8,128]{2,1,0:T(8,128)S(1)}, f32[14,8,128]{2,1,0:T(8,128)S(1)}, u32[]{:S(2)}, u32[]{:S(2)}) collective-permute-start(f32[14,8,128]{2,1,0:T(8,128)S(1)} %get-tuple-element.32), channel_id=1, source_target_pairs={{256,384},{384,256},{257,385},{385,257},{258,386},{386,258},{259,3... | collective-permute-start | bytes 172040 | tf_op jit(solution)/shard_map/ppermute | solution.py:367
  4.4 19.7 %collective-permute-start.2 = (f32[14,8,128]{2,1,0:T(8,128)S(1)}, f32[14,8,128]{2,1,0:T(8,128)S(1)}, u32[]{:S(2)}, u32[]{:S(2)}) collective-permute-start(f32[14,8,128]{2,1,0:T(8,128)S(1)} %get-tuple-element.33), channel_id=1, source_target_pairs={{128,256},{256,128},{129,257},{257,129},{130,258},{258,130},{131,2... | collective-permute-start | bytes 172040 | tf_op jit(solution)/shard_map/ppermute | solution.py:364
  5.1 36.2 %all-to-all-start = ((f32[32,2,128]{2,1,0:T(2,128)}), f32[32,2,128]{2,1,0:T(2,128)S(1)}, u32[]{:S(2)}, u32[]{:S(2)}) async-start(f32[32,2,128]{2,1,0:T(2,128)} %get-tuple-element.35), calls=%async_computation | async-start | bytes 65536 | tf_op jit(solution)/shard_map/all_to_all | solution.py:366
  24.3 7.9 %collective-permute-start.3 = (f32[4,8,128]{2,1,0:T(8,128)S(1)}, f32[4,8,128]{2,1,0:T(8,128)S(1)}, u32[]{:S(2)}, u32[]{:S(2)}) collective-permute-start(f32[4,8,128]{2,1,0:T(8,128)S(1)} %get-tuple-element.34), channel_id=1, source_target_pairs={{0,1},{1,0},{2,3},{3,2},{4,5},{5,4},{6,7},{7,6},{8,9},{9,8},{10,11... | collective-permute-start | bytes 49160 | tf_op jit(solution)/shard_map/ppermute | solution.py:378
  27.8 7.7 %collective-permute-start.4 = (f32[4,8,128]{2,1,0:T(8,128)S(1)}, f32[4,8,128]{2,1,0:T(8,128)S(1)}, u32[]{:S(2)}, u32[]{:S(2)}) collective-permute-start(f32[4,8,128]{2,1,0:T(8,128)S(1)} %get-tuple-element.34), channel_id=1, source_target_pairs={{1,2},{2,1},{3,4},{4,3},{5,6},{6,5},{7,8},{8,7},{9,10},{10,9},{11,... | collective-permute-start | bytes 49160 | tf_op jit(solution)/shard_map/ppermute | solution.py:377
  35.5 6.2 %collective-permute-start.5 = (f32[16,8,128]{2,1,0:T(8,128)S(1)}, f32[16,8,128]{2,1,0:T(8,128)S(1)}, u32[]{:S(2)}, u32[]{:S(2)}) collective-permute-start(f32[16,8,128]{2,1,0:T(8,128)S(1)} %get-tuple-element.45), channel_id=1, source_target_pairs={{0,16},{16,0},{32,48},{48,32},{64,80},{80,64},{96,112},{112,96},{1... | collective-permute-start | bytes 196616 | tf_op jit(solution)/shard_map/ppermute | solution.py:388
  38.9 6.2 %collective-permute-start.6 = (f32[16,8,128]{2,1,0:T(8,128)S(1)}, f32[16,8,128]{2,1,0:T(8,128)S(1)}, u32[]{:S(2)}, u32[]{:S(2)}) collective-permute-start(f32[16,8,128]{2,1,0:T(8,128)S(1)} %get-tuple-element.46), channel_id=1, source_target_pairs={{16,32},{32,16},{48,64},{64,48},{80,96},{96,80},{17,33},{33,17},{4... | collective-permute-start | bytes 196616 | tf_op jit(solution)/shard_map/ppermute | solution.py:387

commit v9 on v8

--- a/solution.py
+++ b/solution.py
@@ -153,16 +153,22 @@
     return packed
 
 
-def second_kernel(v_ref, w_ref, v1_ref, w1_ref, v2_ref, w2_ref, al_ref, ah_ref, b_ref, z_ref, ya_ref, yb_ref):
+def second_kernel(v_ref, w_ref, v1_ref, w1_ref, v2_ref, w2_ref, al_ref, ah_ref, b_ref, z_ref):
+    level0, level1, level2 = extended(
+        lax.axis_index("gx"), v_ref, w_ref, v1_ref, w1_ref, v2_ref, w2_ref, al_ref, ah_ref, b_ref
+    )
+    ends = edge_lanes(level0[1:13])
+    for i, tile in enumerate((ends[0:8], ends[8:16], edge_lanes(level1[1:9]), edge_lanes(level2[1:7]))):
+        z_ref[i] = tile
+
+
+def faces_kernel(v_ref, w_ref, v1_ref, w1_ref, v2_ref, w2_ref, al_ref, ah_ref, b_ref, ya_ref, yb_ref):
     gx, gy = lax.axis_index("gx"), lax.axis_index("gy")
     level0, level1, level2 = extended(gx, v_ref, w_ref, v1_ref, w1_ref, v2_ref, w2_ref, al_ref, ah_ref, b_ref)
     lane, row = lanes(), rows()
     low = lane < 64
     quad = (lane & 63) < 32
     up = (gy & 1) == 0
-    ends = edge_lanes(level0[1:13])
-    for i, tile in enumerate((ends[0:8], ends[8:16], edge_lanes(level1[1:9]), edge_lanes(level2[1:7]))):
-        z_ref[i] = tile
     for k in range(12):
         v, w = level0[k + 1]
         if k < 8:
@@ -366,13 +372,21 @@
     s_in = lax.all_to_all(s_out, ("gx", "gy"), 0, 0, tiled=True, axis_index_groups=[ring])
     ah_in = lax.ppermute(a_out, "gx", even(nx)[nx // 2 :])
     limit = pltpu.CompilerParams(vmem_limit_bytes=8 << 20)
-    z_out, ya_own, yb_own = call(
+    z_out = call(
         second_kernel,
-        out_shape=[shape((4, 8, 128), F32)] + [shape((12, 8, 128), F32)] * 2,
+        out_shape=shape((4, 8, 128), F32),
         in_specs=[VMEM] * 9,
-        out_specs=[VMEM] * 3,
+        out_specs=VMEM,
         compiler_params=limit,
         name="second",
+    )(*own, al_in, ah_in, b_in)
+    ya_own, yb_own = call(
+        faces_kernel,
+        out_shape=[shape((12, 8, 128), F32)] * 2,
+        in_specs=[VMEM] * 9,
+        out_specs=[VMEM] * 2,
+        compiler_params=limit,
+        name="faces",
     )(*own, al_in, ah_in, b_in)
     zb_in = lax.ppermute(z_out, "gz", odd(nz))
     za_in = lax.ppermute(z_out, "gz", even(nz))

time: 46.9 us -> 46.9 us (level)
  no operation moved by 1% of the time
where the time goes in v9:
time: 46.9 us; the launch traced here: 46.5 us
  starting transfers between devices  35.8 us (76%)
  waiting for transfers between devices  6.89 us (15%)
  Pallas kernels  2.83 us (6%)
  other arithmetic  0.88 us (2%)
    all_to_all x1, starting transfers between devices, per_device(): lax.all_to_all(s_out, ('gx', 'gy'), 0, 0, tiled=True, axis_index_groups=[...  19 us
    ppermute x1, starting transfers between devices, per_device(): zb_in = lax.ppermute(z_out, 'gz', odd(nz))  4.35 us
    ppermute x1, starting transfers between devices, per_device(): za_in = lax.ppermute(z_out, 'gz', even(nz))  3.48 us
    ppermute x1, waiting for transfers between devices, per_device(): yb_in = lax.ppermute(yb_out, 'gy', odd(ny))  3.36 us
    ppermute x1, starting transfers between devices, per_device(): ya_in = lax.ppermute(ya_out, 'gy', even(ny))  3.36 us
    ppermute x1, waiting for transfers between devices, per_device(): zb_in = lax.ppermute(z_out, 'gz', odd(nz))  3.33 us
    ppermute x1, starting transfers between devices, per_device(): yb_in = lax.ppermute(yb_out, 'gy', odd(ny))  2.39 us
    ppermute x1, starting transfers between devices, per_device(): al_in = lax.ppermute(a_out, 'gx', even(nx)[:nx // 2])  1.91 us
  transfers between devices with their start and end apart: 8, of which 3 were waited for; matrix products, arithmetic and copies ran while one was open for 0% of the time, Pallas kernels for 1%

profile of v9, /device:TPU:38, one launch (start us, length us, event | category | flops | bytes accessed | tf_op | source)
XLA Modules:
  0.0 46.5 jit_solution(13763693100281976103)
XLA Ops:
  0.0 0.9 %pad_maximum_fusion.in_ref = f32[2,8,16,128]{3,2,1,0:T(8,128)S(1)} fusion(f32[1,8,16,128]{3,2,1,0:T(8,128)} %bitcast.2, f32[1,8,16,128]{3,2,1,0:T(8,128)} %bitcast.3), kind=kLoop, calls=%fused_computation | loop fusion | flops 32768 | bytes 262144 | tf_op jit(solution)/shard_map/stack | solution.py:366
  0.9 0.9 %first.1 = (f32[14,8,128]{2,1,0:T(8,128)S(1)}, f32[14,8,128]{2,1,0:T(8,128)S(1)}, f32[32,2,128]{2,1,0:T(2,128)}, f32[8,16,128]{2,1,0:T(8,128)S(1)}, f32[8,16,128...) custom-call(f32[2,8,16,128]{3,2,1,0:T(8,128)S(1)} %pad_maximum_fusio, ...), custom_call_target="tpu_custom_call" | custom-call | tf_op jit(solution)/shard_map/first/pallas_call | solution.py:358
  1.8 1.9 %collective-permute-start = (f32[14,8,128]{2,1,0:T(8,128)S(1)}, f32[14,8,128]{2,1,0:T(8,128)S(1)}, u32[]{:S(2)}, u32[]{:S(2)}) collective-permute-start(f32[14,8,128]{2,1,0:T(8,128)S(1)} %get-tuple-element.31), channel_id=1, source_target_pairs={{0,128},{128,0},{1,129},{129,1},{2,130},{130,2},{3,131},{131,3},{4... | collective-permute-start | bytes 172040 | tf_op jit(solution)/shard_map/ppermute | solution.py:369
  3.7 0.7 %collective-permute-start.1 = (f32[14,8,128]{2,1,0:T(8,128)S(1)}, f32[14,8,128]{2,1,0:T(8,128)S(1)}, u32[]{:S(2)}, u32[]{:S(2)}) collective-permute-start(f32[14,8,128]{2,1,0:T(8,128)S(1)} %get-tuple-element.31), channel_id=1, source_target_pairs={{256,384},{384,256},{257,385},{385,257},{258,386},{386,258},{259,3... | collective-permute-start | bytes 172040 | tf_op jit(solution)/shard_map/ppermute | solution.py:373
  4.4 0.7 %collective-permute-start.2 = (f32[14,8,128]{2,1,0:T(8,128)S(1)}, f32[14,8,128]{2,1,0:T(8,128)S(1)}, u32[]{:S(2)}, u32[]{:S(2)}) collective-permute-start(f32[14,8,128]{2,1,0:T(8,128)S(1)} %get-tuple-element.32), channel_id=1, source_target_pairs={{128,256},{256,128},{129,257},{257,129},{130,258},{258,130},{131,2... | collective-permute-start | bytes 172040 | tf_op jit(solution)/shard_map/ppermute | solution.py:370
  5.1 19.0 %all-to-all-start = ((f32[32,2,128]{2,1,0:T(2,128)}), f32[32,2,128]{2,1,0:T(2,128)S(1)}, u32[]{:S(2)}, u32[]{:S(2)}) async-start(f32[32,2,128]{2,1,0:T(2,128)} %get-tuple-element.33), calls=%async_computation | async-start | bytes 65536 | tf_op jit(solution)/shard_map/all_to_all | solution.py:372
  24.1 0.0 collective-permute-done.al_ref
  24.1 0.0 collective-permute-done.1.ah_ref
  24.1 0.0 collective-permute-done.2.b_ref
  24.1 0.2 second.1
  24.3 3.5 %collective-permute-start.3 = (f32[4,8,128]{2,1,0:T(8,128)S(1)}, f32[4,8,128]{2,1,0:T(8,128)S(1)}, u32[]{:S(2)}, u32[]{:S(2)}) collective-permute-start(f32[4,8,128]{2,1,0:T(8,128)S(1)} %second.1), channel_id=1, source_target_pairs={{0,1},{1,0},{2,3},{3,2},{4,5},{5,4},{6,7},{7,6},{8,9},{9,8},{10,11... | collective-permute-start | bytes 49160 | tf_op jit(solution)/shard_map/ppermute | solution.py:392
  27.8 4.4 %collective-permute-start.4 = (f32[4,8,128]{2,1,0:T(8,128)S(1)}, f32[4,8,128]{2,1,0:T(8,128)S(1)}, u32[]{:S(2)}, u32[]{:S(2)}) collective-permute-start(f32[4,8,128]{2,1,0:T(8,128)S(1)} %second.1), channel_id=1, source_target_pairs={{1,2},{2,1},{3,4},{4,3},{5,6},{6,5},{7,8},{8,7},{9,10},{10,9},{11,... | collective-permute-start | bytes 49160 | tf_op jit(solution)/shard_map/ppermute | solution.py:391
  32.2 0.0 collective-permute-done.3.za_ref
  32.2 3.3 %collective-permute-done.4.zb_ref = f32[4,8,128]{2,1,0:T(8,128)S(1)} collective-permute-done((f32[4,8,128]{2,1,0:T(8,128)S(1)}, f32[4,8,128]{2,1,0:T(8,128)S(1)}, u32[]{:S(2)}, u32[]{:S(2)}) %collective-permute-start.4) | collective-permute-done | bytes 16416 | tf_op jit(solution)/shard_map/ppermute | solution.py:391
  35.5 3.4 %collective-permute-start.5 = (f32[16,8,128]{2,1,0:T(8,128)S(1)}, f32[16,8,128]{2,1,0:T(8,128)S(1)}, u32[]{:S(2)}, u32[]{:S(2)}) collective-permute-start(f32[16,8,128]{2,1,0:T(8,128)S(1)} %get-tuple-element.43), channel_id=1, source_target_pairs={{0,16},{16,0},{32,48},{48,32},{64,80},{80,64},{96,112},{112,96},{1... | collective-permute-start | bytes 196616 | tf_op jit(solution)/shard_map/ppermute | solution.py:402
  38.9 2.4 %collective-permute-start.6 = (f32[16,8,128]{2,1,0:T(8,128)S(1)}, f32[16,8,128]{2,1,0:T(8,128)S(1)}, u32[]{:S(2)}, u32[]{:S(2)}) collective-permute-start(f32[16,8,128]{2,1,0:T(8,128)S(1)} %get-tuple-element.44), channel_id=1, source_target_pairs={{16,32},{32,16},{48,64},{64,48},{80,96},{96,80},{17,33},{33,17},{4... | collective-permute-start | bytes 196616 | tf_op jit(solution)/shard_map/ppermute | solution.py:401
  41.3 0.0 all-to-all-done.s_ref
  41.3 0.2 fourth.1
  41.5 0.2 collective-permute-done.5.ya_ref
  41.7 3.4 %collective-permute-done.6.yb_ref = f32[16,8,128]{2,1,0:T(8,128)S(1)} collective-permute-done((f32[16,8,128]{2,1,0:T(8,128)S(1)}, f32[16,8,128]{2,1,0:T(8,128)S(1)}, u32[]{:S(2)}, u32[]{:S(2)}) %collective-permute-start.6) | collective-permute-done | bytes 65568 | tf_op jit(solution)/shard_map/ppermute | solution.py:401
  45.1 1.5 %last.1 = f32[8,16,128]{2,1,0:T(8,128)} custom-call(f32[4,8,128]{2,1,0:T(8,128)S(1)} %collective-permute-done.3.za_ref, f32[4,8,128]{2,1,0:T(8,128)S(1)} %collective-permute-done.4.zb_ref, f32[14,16,256]{2,1,0:T(8,128)S(1)} %get-tuple-element.34.fv_ref, f32[14,16,256]{2,1,0:T(8,128)S(1)} %get-tuple-element.35.fw_ref, ...), custom_call_target="tpu_custom_call" | custom-call | tf_op jit(solution)/shard_map/last/pallas_call | solution.py:415
  (2 shorter events, 0.1 us)
Async XLA Ops:
  1.8 22.3 %collective-permute-start = (f32[14,8,128]{2,1,0:T(8,128)S(1)}, f32[14,8,128]{2,1,0:T(8,128)S(1)}, u32[]{:S(2)}, u32[]{:S(2)}) collective-permute-start(f32[14,8,128]{2,1,0:T(8,128)S(1)} %get-tuple-element.31), channel_id=1, source_target_pairs={{0,128},{128,0},{1,129},{129,1},{2,130},{130,2},{3,131},{131,3},{4... | collective-permute-start | bytes 172040 | tf_op jit(solution)/shard_map/ppermute | solution.py:369
  3.7 20.4 %collective-permute-start.1 = (f32[14,8,128]{2,1,0:T(8,128)S(1)}, f32[14,8,128]{2,1,0:T(8,128)S(1)}, u32[]{:S(2)}, u32[]{:S(2)}) collective-permute-start(f32[14,8,128]{2,1,0:T(8,128)S(1)} %get-tuple-element.31), channel_id=1, source_target_pairs={{256,384},{384,256},{257,385},{385,257},{258,386},{386,258},{259,3... | collective-permute-start | bytes 172040 | tf_op jit(solution)/shard_map/ppermute | solution.py:373
  4.4 19.7 %collective-permute-start.2 = (f32[14,8,128]{2,1,0:T(8,128)S(1)}, f32[14,8,128]{2,1,0:T(8,128)S(1)}, u32[]{:S(2)}, u32[]{:S(2)}) collective-permute-start(f32[14,8,128]{2,1,0:T(8,128)S(1)} %get-tuple-element.32), channel_id=1, source_target_pairs={{128,256},{256,128},{129,257},{257,129},{130,258},{258,130},{131,2... | collective-permute-start | bytes 172040 | tf_op jit(solution)/shard_map/ppermute | solution.py:370
  5.1 36.2 %all-to-all-start = ((f32[32,2,128]{2,1,0:T(2,128)}), f32[32,2,128]{2,1,0:T(2,128)S(1)}, u32[]{:S(2)}, u32[]{:S(2)}) async-start(f32[32,2,128]{2,1,0:T(2,128)} %get-tuple-element.33), calls=%async_computation | async-start | bytes 65536 | tf_op jit(solution)/shard_map/all_to_all | solution.py:372
  24.3 7.9 %collective-permute-start.3 = (f32[4,8,128]{2,1,0:T(8,128)S(1)}, f32[4,8,128]{2,1,0:T(8,128)S(1)}, u32[]{:S(2)}, u32[]{:S(2)}) collective-permute-start(f32[4,8,128]{2,1,0:T(8,128)S(1)} %second.1), channel_id=1, source_target_pairs={{0,1},{1,0},{2,3},{3,2},{4,5},{5,4},{6,7},{7,6},{8,9},{9,8},{10,11... | collective-permute-start | bytes 49160 | tf_op jit(solution)/shard_map/ppermute | solution.py:392
  27.8 7.7 %collective-permute-start.4 = (f32[4,8,128]{2,1,0:T(8,128)S(1)}, f32[4,8,128]{2,1,0:T(8,128)S(1)}, u32[]{:S(2)}, u32[]{:S(2)}) collective-permute-start(f32[4,8,128]{2,1,0:T(8,128)S(1)} %second.1), channel_id=1, source_target_pairs={{1,2},{2,1},{3,4},{4,3},{5,6},{6,5},{7,8},{8,7},{9,10},{10,9},{11,... | collective-permute-start | bytes 49160 | tf_op jit(solution)/shard_map/ppermute | solution.py:391
  35.5 6.2 %collective-permute-start.5 = (f32[16,8,128]{2,1,0:T(8,128)S(1)}, f32[16,8,128]{2,1,0:T(8,128)S(1)}, u32[]{:S(2)}, u32[]{:S(2)}) collective-permute-start(f32[16,8,128]{2,1,0:T(8,128)S(1)} %get-tuple-element.43), channel_id=1, source_target_pairs={{0,16},{16,0},{32,48},{48,32},{64,80},{80,64},{96,112},{112,96},{1... | collective-permute-start | bytes 196616 | tf_op jit(solution)/shard_map/ppermute | solution.py:402
  38.9 6.2 %collective-permute-start.6 = (f32[16,8,128]{2,1,0:T(8,128)S(1)}, f32[16,8,128]{2,1,0:T(8,128)S(1)}, u32[]{:S(2)}, u32[]{:S(2)}) collective-permute-start(f32[16,8,128]{2,1,0:T(8,128)S(1)} %get-tuple-element.44), channel_id=1, source_target_pairs={{16,32},{32,16},{48,64},{64,48},{80,96},{96,80},{17,33},{33,17},{4... | collective-permute-start | bytes 196616 | tf_op jit(solution)/shard_map/ppermute | solution.py:401
